TPU v7x, 256 devices: a whole 4x4x8 slice. The times are simulated.
256 devices in a mesh: dp: 4 (over y), expert: 64 (over z, x, core).
Axes of the slice: x: 4, y: 4, z: 8, core: 2. Of those that a mesh axis runs over, the one named last changes fastest.
Arguments:
- tokens: bfloat16 [8192, 4096], P('expert'), may hold values from -6 to 6
- out_grad: bfloat16 [8192, 4096], P('expert'), may hold values from -6 to 6
- expert_ids: int32 [8192, 8], P('expert'), may hold values from 0 to 127, all different within a row; in each aligned block of 128 rows (0 to 127, 128 to 255, ...) at most 12 rows name the same one
- combine: bfloat16 [8192, 8], P('expert'), may hold values from 0.049804688 to 0.5
- gate_weight: bfloat16 [64, 768, 4096], P('expert', 'dp'), may hold values from -6 to 6
- up_weight: bfloat16 [64, 768, 4096], P('expert', 'dp'), may hold values from -6 to 6
- down_weight: bfloat16 [64, 768, 4096], P('expert', 'dp'), may hold values from -6 to 6
Outputs:
- input_grad: bfloat16 [8192, 4096], P('expert')
- combine_grad: float32 [8192, 8], P('expert')
- gate_grad: bfloat16 [64, 768, 4096], P('expert', 'dp')
- up_grad: bfloat16 [64, 768, 4096], P('expert', 'dp')
- down_grad: bfloat16 [64, 768, 4096], P('expert', 'dp')
Inputs may be any that keep to these rules, and one draw needn't show every extreme that they name: `expert_ids`: each row names 8 different experts. Among the 128 rows of one aligned block no id is named by more than 12 rows, and in some block some id is named by exactly 12.
All inputs are finite; a program needn't handle non-finite values.
Results may differ from a plain program's by a relative error of at most 0.015.
Values may be sent and summed in bfloat16 or wider, within the bound.
No kernel may reach another device: no remote copies, remote signals or barrier semaphores. Data moves between devices by JAX's collectives and lax.ppermute only.
A program may use at most 128 MiB of HBM per device.

v0:
```python
import jax
import jax.numpy as jnp
from jax import lax
from jax.sharding import PartitionSpec as P

D = 4096
FF = 1536
ROUTED = 128
TOP = 8
CAP = 12


def slot_table(routes, weights_in, experts):
    expert_list = jnp.arange(experts, dtype=jnp.int32)
    matches = routes[:, :, None] == expert_list[None, None, :]
    member = jnp.sum(matches.astype(jnp.int32), axis=1)
    weight_of = jnp.sum(
        jnp.where(matches, weights_in.astype(jnp.float32)[:, :, None], jnp.float32(0.0)), axis=1
    )
    rank_of = jnp.cumsum(member, axis=0) - 1
    slot_ids = jnp.arange(CAP, dtype=jnp.int32)
    placed = (member.T[:, None, :] == 1) & (rank_of.T[:, None, :] == slot_ids[None, :, None])
    placed = placed.astype(jnp.float32)
    slot_weight = jnp.sum(placed * weight_of.T[:, None, :], axis=2)
    return (placed, slot_weight)


def expert_rows(token_rows, grad_rows, row_weight, gate_w, up_w, down_w, batch_rows):
    contract = (((1,), (1,)), ((), ()))
    rows_first = (((0,), (0,)), ((), ()))
    gate_pre = lax.dot_general(
        token_rows, gate_w, contract, preferred_element_type=jnp.float32
    ) * D ** (-0.5)
    up_pre = lax.dot_general(
        token_rows, up_w, contract, preferred_element_type=jnp.float32
    ) * D ** (-0.5)
    back_proj = lax.dot_general(grad_rows, down_w, contract, preferred_element_type=jnp.float32)
    sigmoid = jax.nn.sigmoid(gate_pre)
    active = gate_pre * sigmoid
    hidden = active * up_pre
    slope_of = sigmoid * (1.0 + gate_pre * (1.0 - sigmoid))
    scaled = row_weight[:, None] * back_proj * D ** (-0.5)
    grad_gate = (scaled * up_pre * slope_of).astype(jnp.bfloat16)
    grad_up = (scaled * active).astype(jnp.bfloat16)
    weighted = (row_weight[:, None] * hidden).astype(jnp.bfloat16)
    input_part = jnp.dot(grad_gate, gate_w, preferred_element_type=jnp.float32)
    input_part = (input_part + jnp.dot(grad_up, up_w, preferred_element_type=jnp.float32)) * (
        2 * FF
    ) ** (-0.5)
    combine_part = jnp.sum(hidden * back_proj, axis=1) * (D * FF) ** (-0.5)
    factor = float(batch_rows) ** (-0.5)
    wgrad_gate = (
        lax.dot_general(grad_gate, token_rows, rows_first, preferred_element_type=jnp.float32)
        * factor
    ).astype(jnp.bfloat16)
    wgrad_up = (
        lax.dot_general(grad_up, token_rows, rows_first, preferred_element_type=jnp.float32)
        * factor
    ).astype(jnp.bfloat16)
    wgrad_down = (
        lax.dot_general(weighted, grad_rows, rows_first, preferred_element_type=jnp.float32)
        * factor
    ).astype(jnp.bfloat16)
    return (input_part, combine_part, (wgrad_gate, wgrad_up, wgrad_down))


def on_device(tokens, out_grad, expert_ids, combine, gate_weight, up_weight, down_weight):
    axis_width = lax.axis_size("expert")
    experts = axis_width // 2
    token_count = tokens.shape[0]
    model_width = tokens.shape[1]
    batch_rows = token_count * axis_width * TOP // ROUTED
    highest = lax.Precision.HIGHEST
    placed, slot_weight = slot_table(expert_ids, combine, experts)
    place_low = placed.astype(jnp.bfloat16)
    spread = jnp.repeat(place_low, 2, axis=0)
    sent_tokens = jnp.einsum(
        "ict,td->icd", spread, tokens, preferred_element_type=jnp.float32
    ).astype(jnp.bfloat16)
    sent_grads = jnp.einsum(
        "ict,td->icd", spread, out_grad, preferred_element_type=jnp.float32
    ).astype(jnp.bfloat16)
    sent_weight = jnp.repeat(slot_weight, 2, axis=0).astype(jnp.bfloat16)
    got_tokens, got_grads, got_weight = (
        lax.all_to_all(sent_tokens, "expert", split_axis=0, concat_axis=0, tiled=True),
        lax.all_to_all(sent_grads, "expert", split_axis=0, concat_axis=0, tiled=True),
        lax.all_to_all(sent_weight, "expert", split_axis=0, concat_axis=0, tiled=True),
    )
    input_part, combine_part, weight_grads = expert_rows(
        got_tokens.reshape(-1, model_width),
        got_grads.reshape(-1, model_width),
        got_weight.reshape(-1).astype(jnp.float32),
        gate_weight[0],
        up_weight[0],
        down_weight[0],
        batch_rows,
    )
    low_input = lax.optimization_barrier(input_part.astype(jnp.bfloat16)).reshape(
        axis_width, CAP, model_width
    )
    low_combine = lax.optimization_barrier(combine_part.astype(jnp.bfloat16)).reshape(
        axis_width, CAP
    )
    back_input, back_combine = (
        lax.all_to_all(low_input, "expert", split_axis=0, concat_axis=0, tiled=True),
        lax.all_to_all(low_combine, "expert", split_axis=0, concat_axis=0, tiled=True),
    )
    sum_input = lax.psum_scatter(
        back_input.astype(jnp.float32).astype(jnp.bfloat16), "dp", scatter_dimension=2, tiled=True
    ).astype(jnp.float32)
    sum_combine = lax.psum(back_combine.astype(jnp.float32), "dp")
    column_width = sum_input.shape[2]
    pair_input = jnp.sum(sum_input.reshape(experts, 2, CAP, column_width), axis=1)
    pair_combine = jnp.sum(sum_combine.reshape(experts, 2, CAP), axis=1)
    input_columns = jnp.einsum("ect,ecd->td", placed, pair_input, precision=highest).astype(
        jnp.bfloat16
    )
    input_grad = lax.all_gather(input_columns, "dp", axis=1, tiled=True)
    token_weight = jnp.einsum("ect,ec->et", placed, pair_combine, precision=highest)
    matches = (
        expert_ids[:, :, None] == jnp.arange(experts, dtype=jnp.int32)[None, None, :]
    ).astype(jnp.float32)
    combine_grad = jnp.einsum("tke,et->tk", matches, token_weight, precision=highest)
    wgrad_gate, wgrad_up, wgrad_down = weight_grads
    return (input_grad, combine_grad, wgrad_gate[None], wgrad_up[None], wgrad_down[None])


def solution(mesh):
    placed = (
        P("expert", None),
        P("expert", None),
        P("expert", None),
        P("expert", None),
        P("expert", "dp", None),
        P("expert", "dp", None),
        P("expert", "dp", None),
    )
    return jax.shard_map(
        on_device,
        mesh=mesh,
        in_specs=placed,
        out_specs=(
            P("expert", None),
            P("expert", None),
            P("expert", "dp", None),
            P("expert", "dp", None),
            P("expert", "dp", None),
        ),
        check_vma=False,
    )
```

profile of v0, /device:TPU:2, one launch (start us, length us, event | category | flops | bytes accessed | tf_op | source)
XLA Modules:
  0.0 778.7 jit_solution(14647430415118032151)
XLA Ops:
  7.2 0.0 copy-start
  7.2 0.8 convert_reduce_fusion.1
  8.0 0.1 copy.41
  8.1 0.7 convert_element_type.80
  8.8 0.7 select_reduce_fusion.2
  9.5 0.2 reduce_window_sum.11
  9.7 0.1 copy.42
  9.8 0.2 select_reduce_fusion
  9.9 0.1 copy.43
  10.0 0.6 copy.44
  10.7 12.0 %all-to-all-start = ((bf16[64,1,12]{2,1,0:T(2,128)(2,1)}), bf16[64,1,12]{2,1,0:T(2,128)(2,1)S(1)}, u32[]{:S(2)}, u32[]{:S(2)}) async-start(bf16[64,1,12]{2,1,0:T(2,128)(2,1)} %copy.44), calls=%async_computation | async-start | bytes 65536 | tf_op jit(solution)/shard_map/all_to_all | solution.py:87
  22.7 0.1 fusion.36
  22.8 0.1 broadcast_in_dim.41
  22.9 3.0 convolution_convert_fusion
  25.9 6.8 copy.46
  32.7 0.0 copy-start.4
  32.7 0.0 all-to-all-done
  32.7 10.6 %all-to-all-start.2 = ((bf16[64,12,4096]{2,1,0:T(8,128)(2,1)}), bf16[64,12,4096]{2,1,0:T(8,128)(2,1)}, u32[]{:S(2)}, u32[]{:S(2)}) async-start(bf16[64,12,4096]{2,1,0:T(8,128)(2,1)} %copy.46), calls=%async_computation.2 | async-start | bytes 16777216 | tf_op jit(solution)/shard_map/all_to_all | solution.py:85
  43.3 0.0 copy-done.4
  43.3 1.8 convolution_convert_fusion.1
  45.1 6.8 copy.45
  51.9 177.7 %all-to-all-done.2 = bf16[64,12,4096]{2,1,0:T(8,128)(2,1)} async-done(((bf16[64,12,4096]{2,1,0:T(8,128)(2,1)}), bf16[64,12,4096]{2,1,0:T(8,128)(2,1)}, u32[]{:S(2)}, u32[]{:S(2)}) %all-to-all-start.2) | async-done | bytes 6291488 | tf_op jit(solution)/shard_map/all_to_all | solution.py:85
  229.6 6.4 all-to-all-start.1
  236.0 0.3 reduce-scatter.2.cloned.1.call-start
  236.2 0.1 convert_reduce_fusion.2
  236.3 0.1 reshape.73
  236.4 9.9 %reshape.68 = bf16[768,4096]{1,0:T(8,128)(2,1)} reshape(bf16[64,12,4096]{2,1,0:T(8,128)(2,1)} %all-to-all-done.2) | data formatting | bytes 12582912 | tf_op jit(solution)/shard_map/reshape | solution.py:90
  246.3 0.0 copy-done
  246.3 0.0 copy-start.2
  246.3 0.0 copy-start.3
  246.3 6.0 fusion.20
  252.3 0.0 copy-done.2
  252.3 0.0 copy-done.3
  252.3 3.0 fusion.17
  255.3 165.7 %all-to-all-done.1 = bf16[64,12,4096]{2,1,0:T(8,128)(2,1)} async-done(((bf16[64,12,4096]{2,1,0:T(8,128)(2,1)}), bf16[64,12,4096]{2,1,0:T(8,128)(2,1)}, u32[]{:S(2)}, u32[]{:S(2)}) %all-to-all-start.1) | async-done | bytes 6291488 | tf_op jit(solution)/shard_map/all_to_all | solution.py:86
  421.0 9.9 %reshape.67 = bf16[768,4096]{1,0:T(8,128)(2,1)} reshape(bf16[64,12,4096]{2,1,0:T(8,128)(2,1)} %all-to-all-done.1) | data formatting | bytes 12582912 | tf_op jit(solution)/shard_map/reshape | solution.py:91
  430.9 5.9 multiply_reduce_fusion
  436.8 0.0 copy-start.5
  436.8 1.8 fusion.6
  438.7 0.0 copy-done.5
  438.7 4.6 multiply_convert_fusion
  443.3 9.8 %reshape.69 = bf16[64,12,4096]{2,1,0:T(8,128)(2,1)} reshape(bf16[768,4096]{1,0:T(8,128)(2,1)} %multiply_convert_fusion) | data formatting | bytes 12582912 | tf_op jit(solution)/shard_map/reshape | solution.py:98
  453.1 193.6 %all_to_all.31 = bf16[64,12,4096]{2,1,0:T(8,128)(2,1)} all-to-all(bf16[64,12,4096]{2,1,0:T(8,128)(2,1)} %reshape.69), channel_id=1, replica_groups=mesh['dp'=4,'expert'=64] {'expert'}, dimensions={0} | all-to-all | bytes 12582912 | tf_op jit(solution)/shard_map/all_to_all | solution.py:105
  646.7 0.0 reduce-scatter.2.cloned.1.call-update
  646.8 0.3 all-gather.2.cloned.1.call-start
  647.1 0.6 copy-done.6
  647.7 5.3 fusion.5
  653.0 73.3 %reduce-scatter.2.cloned.1.call-done = bf16[64,12,1024]{2,1,0:T(8,128)(2,1)} async-done(((bf16[64,12,4096]{2,1,0:T(8,128)(2,1)}), bf16[64,12,1024]{2,1,0:T(8,128)(2,1)}) %reduce-scatter.2.cloned.1.call-update) | async-done | bytes 1572880 | tf_op jit(solution)/shard_map/reduce_scatter | solution.py:108
  726.3 2.4 convert_reduce_fusion
  728.7 2.4 fusion.26
  731.1 0.0 all-gather.2.cloned.1.call-update
  731.1 0.7 all_to_all.25
  731.8 10.6 %all-to-all-start.4 = ((bf16[64,1,12]{2,1,0:T(2,128)(2,1)}), bf16[64,1,12]{2,1,0:T(2,128)(2,1)S(1)}, u32[]{:S(2)}, u32[]{:S(2)}) async-start(bf16[64,1,12]{2,1,0:T(2,128)(2,1)} %all_to_all.25), calls=%async_computation.5 | async-start | bytes 65536 | tf_op jit(solution)/shard_map/all_to_all | solution.py:106
  742.4 0.0 copy-done.8
  742.4 0.0 copy-done.9
  742.4 5.5 fusion.3
  748.0 5.5 fusion.4
  753.5 0.0 all-to-all-done.4
  753.5 15.1 %psum.7 = f32[32,2,12]{2,1,0:T(2,128)S(1)} all-reduce(f32[32,2,12]{2,1,0:T(2,128)S(1)} %bitcast.72), channel_id=1, replica_groups=mesh['dp'=4,'expert'=64] {'dp'}, use_global_device_ids=true, to_apply=%region_7.8 | all-reduce | flops 768 | bytes 6144 | tf_op jit(solution)/shard_map/psum | solution.py:111
  768.7 0.3 fusion.33
  769.0 0.0 copy-done.7
  769.0 0.6 select_reduce_fusion.1
  769.6 2.3 copy.69
  771.9 0.0 copy-done.1
  (12 shorter events, 0.1 us)
Async XLA Ops:
  7.2 239.1 %copy-start = (bf16[1,192,4096]{2,1,0:T(8,128)(2,1)S(1)}, bf16[1,192,4096]{2,1,0:T(8,128)(2,1)}, u32[]{:S(2)}) copy-start(bf16[1,192,4096]{2,1,0:T(8,128)(2,1)} %param.11) | copy-start | bytes 4718596
  10.7 22.0 %all-to-all-start = ((bf16[64,1,12]{2,1,0:T(2,128)(2,1)}), bf16[64,1,12]{2,1,0:T(2,128)(2,1)S(1)}, u32[]{:S(2)}, u32[]{:S(2)}) async-start(bf16[64,1,12]{2,1,0:T(2,128)(2,1)} %copy.44), calls=%async_computation | async-start | bytes 65536 | tf_op jit(solution)/shard_map/all_to_all | solution.py:87
  32.7 10.6 %copy-start.4 = (bf16[128,4096]{1,0:T(8,128)(2,1)S(1)}, bf16[128,4096]{1,0:T(8,128)(2,1)}, u32[]{:S(2)}) copy-start(bf16[128,4096]{1,0:T(8,128)(2,1)} %param.8) | copy-start | bytes 3145732
  32.7 196.9 %all-to-all-start.2 = ((bf16[64,12,4096]{2,1,0:T(8,128)(2,1)}), bf16[64,12,4096]{2,1,0:T(8,128)(2,1)}, u32[]{:S(2)}, u32[]{:S(2)}) async-start(bf16[64,12,4096]{2,1,0:T(8,128)(2,1)} %copy.46), calls=%async_computation.2 | async-start | bytes 16777216 | tf_op jit(solution)/shard_map/all_to_all | solution.py:85
  229.6 191.4 %all-to-all-start.1 = ((bf16[64,12,4096]{2,1,0:T(8,128)(2,1)}), bf16[64,12,4096]{2,1,0:T(8,128)(2,1)}, u32[]{:S(2)}, u32[]{:S(2)}) async-start(bf16[64,12,4096]{2,1,0:T(8,128)(2,1)} %copy.45), calls=%async_computation.1 | async-start | bytes 16777216 | tf_op jit(solution)/shard_map/all_to_all | solution.py:86
  236.0 490.4 %reduce-scatter.2.cloned.1.call-start = ((), (), s32[]{:S(2)}) async-start(), calls=%async_computation.6 | async-start | bytes 10485760 | tf_op jit(solution)/shard_map/reduce_scatter | solution.py:108
  246.3 6.0 copy-start.2
  246.3 6.0 copy-start.3
  436.8 1.9 copy-start.5
  646.7 1.0 copy-start.6
  646.8 122.8 %all-gather.2.cloned.1.call-start = ((), (), s32[]{:S(2)}) async-start(), calls=%async_computation.7 | async-start | bytes 1310720 | tf_op jit(solution)/shard_map/all_gather | solution.py:118
  653.0 89.4 %copy-start.8 = (f32[768,192]{0,1:T(8,128)S(1)}, f32[768,192]{0,1:T(8,128)}, u32[]{:S(2)}) copy-start(f32[768,192]{0,1:T(8,128)} %fusion.20) | copy-start | bytes 1769476
  653.0 89.4 %copy-start.9 = (f32[768,192]{0,1:T(8,128)S(1)}, f32[768,192]{0,1:T(8,128)}, u32[]{:S(2)}) copy-start(f32[768,192]{0,1:T(8,128)} %fusion.17) | copy-start | bytes 1769476
  731.8 21.7 %all-to-all-start.4 = ((bf16[64,1,12]{2,1,0:T(2,128)(2,1)}), bf16[64,1,12]{2,1,0:T(2,128)(2,1)S(1)}, u32[]{:S(2)}, u32[]{:S(2)}) async-start(bf16[64,1,12]{2,1,0:T(2,128)(2,1)} %all_to_all.25), calls=%async_computation.5 | async-start | bytes 65536 | tf_op jit(solution)/shard_map/all_to_all | solution.py:106
  748.0 21.0 %copy-start.7 = (s32[128,8]{0,1:T(8,128)S(1)}, s32[128,8]{0,1:T(8,128)}, u32[]{:S(2)}) copy-start(s32[128,8]{0,1:T(8,128)} %param.9) | copy-start | bytes 12292
  748.0 23.9 %copy-start.1 = (bf16[1,192,4096]{2,1,0:T(8,128)(2,1)S(1)}, bf16[1,192,4096]{2,1,0:T(8,128)(2,1)}, u32[]{:S(2)}) copy-start(bf16[1,192,4096]{2,1,0:T(8,128)(2,1)} %param.11) | copy-start | bytes 4718596
Sparse Core Ops, SparseCore 0:
  646.9 79.4 reduce-scatter.1
  731.2 26.2 all-gather.1
where the time goes:
time: 780 us; the launch traced here: 779 us
  waiting for transfers between devices  417 us (53%)
  blocking collectives  209 us (27%)
  local copies, waits for them, and re-layouts  48 us (6%)
  matrix products  45.3 us (6%)
  starting transfers between devices  40.2 us (5%)
  between operations  14.3 us (2%)
    all_to_all x1, blocking collectives, on_device(): lax.all_to_all(low_input, 'expert', split_axis=0, concat_axis=0, tiled=True)  194 us
    all_to_all x1, waiting for transfers between devices, on_device(): lax.all_to_all(sent_tokens, 'expert', split_axis=0, concat_axis=0, tiled=...  178 us
    all_to_all x1, waiting for transfers between devices, on_device(): lax.all_to_all(sent_grads, 'expert', split_axis=0, concat_axis=0, tiled=T...  166 us
    reduce_scatter x1, waiting for transfers between devices, on_device(): lax.psum_scatter(back_input.astype(jnp.float32).astype(jnp.bfloat16), 'dp...  73.3 us
  transfers between devices with their start and end apart: 6, of which 3 were waited for; matrix products, arithmetic and copies ran while one was open for 7% of the time, Pallas kernels for 0%

commit v1 on v0

v1 whole, which is shorter than its diff:
```python
import functools

import jax
import jax.numpy as jnp
from jax import lax
from jax.experimental import pallas as pl
from jax.experimental.pallas import tpu as pltpu
from jax.sharding import PartitionSpec as P

D = 4096
FF = 1536
TOP = 8
EXPERTS = 32
BF = jnp.bfloat16
F32 = jnp.float32
I32 = jnp.int32
HALF = D // 2
CH = 512
CAP = 12
GROUP = 2 * CAP
ROWS = EXPERTS * GROUP
UNITS = 384
NT = (((1,), (1,)), ((), ()))
NN = (((1,), (0,)), ((), ()))
OFFS = (0, -1, 1, 2)

SMEM = pl.BlockSpec(memory_space=pltpu.SMEM)
VMEM = pl.BlockSpec(memory_space=pltpu.VMEM)


def mm(a, b, dims=NN):
    return lax.dot_general(a, b, dims, preferred_element_type=F32)


def iota(shape, axis):
    return lax.broadcasted_iota(I32, shape, axis)


def onehot(mask):
    return jnp.where(mask, F32(1.0), F32(0.0))


COST = {
    "pack": 2, "send": 3, "weight_send": 4, "weight_join": 6, "gate_up": 7, "back": 5, "mid": 10,
    "wgrad_other": 8, "wgrad_own": 8, "finish": 2, "collect": 3, "merge": 2, "assemble": 2,
}


def call(body, outs, args, scratch=(), name=None):
    return pl.pallas_call(
        body,
        out_shape=[jax.ShapeDtypeStruct(s, t) for s, t in outs],
        in_specs=[SMEM] + [VMEM] * (len(args) - 1),
        out_specs=[VMEM] * len(outs),
        scratch_shapes=list(scratch),
        compiler_params=pltpu.CompilerParams(vmem_limit_bytes=60 * 1024 * 1024),
        cost_estimate=pl.CostEstimate(
            flops=COST[name] * 100_000_000_000, transcendentals=0, bytes_accessed=0
        ),
        name=name,
    )(*args)


def at(start, size):
    return pl.ds(pl.multiple_of(start, size), size)


def chunk_cols(y, off):
    return at(lax.rem(y + (off + 4), 4) * CH, CH)


def row_parts(r):
    e = (r * 2731) >> 16
    q = r - e * GROUP
    core = q >= CAP
    return e, core, jnp.where(core, q - CAP, q)


def slot_key(ids):
    e = iota((EXPERTS, 128), 0)
    member = jnp.zeros((EXPERTS, 128), F32)
    for k in range(TOP):
        member = member + onehot(ids[k : k + 1, :] == e)
    upto = onehot(iota((128, 128), 0) <= iota((128, 128), 1)).astype(BF)
    rank = mm(member.astype(BF), upto) - 1.0
    return jnp.where(member > 0.5, rank, F32(-1.0))


def slot_weight(ids, comb):
    e = iota((EXPERTS, 128), 0)
    out = jnp.zeros((EXPERTS, 128), F32)
    for k in range(TOP):
        out = out + jnp.where(ids[k : k + 1, :] == e, comb[k : k + 1, :], F32(0.0))
    return out.astype(BF)


def expert_rows():
    e, _, _ = row_parts(iota((ROWS, EXPERTS), 0))
    return onehot(e == iota((ROWS, EXPERTS), 1)).astype(BF)


def got_ids(pk):
    return pk[256:272, :128].astype(F32)[:8].astype(I32)


def pack_body(pos, ids, comb, tokens, grads, out):
    cols = at((1 - pos[1]) * HALF + pos[0] * CH, CH)
    out[:128, :] = tokens[:, cols]
    out[128:256, :] = grads[:, cols]
    row = jnp.concatenate(
        [ids[...].astype(F32), comb[...].astype(F32), jnp.zeros((8, 256), F32)], axis=1
    )
    out[256:, :] = jnp.concatenate([row, jnp.zeros((8, CH), F32)], axis=0).astype(BF)


def send_body(weighted, pos, ids, comb, pk, rows_ref, out):
    y, h = pos[0], pos[1]
    rows = expert_rows()
    _, core, slot = row_parts(iota((ROWS, 128), 0))
    slot = slot.astype(F32)
    parts = []
    for mine, idv, cv in (
        (True, ids[...], comb[...].astype(F32)),
        (False, got_ids(pk), pk[256:272, 128:256].astype(F32)[:8]),
    ):
        key = mm(rows, slot_key(idv).astype(BF))
        member = (key == slot) & (core == ((h == 1) if mine else (h == 0)))
        if weighted:
            parts.append(jnp.where(member, mm(rows, slot_weight(idv, cv)), F32(0.0)))
        else:
            parts.append(onehot(member))
    lhs = jnp.concatenate(parts, axis=1).astype(BF)
    got = pk[128:256, :] if weighted else pk[:128, :]
    rhs = jnp.concatenate([rows_ref[:, at(h * HALF + y * CH, CH)], got], axis=0)
    out[...] = mm(lhs, rhs).astype(BF)


def weight_send_body(pos, gw, uw, dw, out):
    other = at((1 - pos[1]) * HALF, HALF)
    for m, w in enumerate((gw, uw, dw)):
        out[m] = w[:, other]


def weight_join_body(pos, gw, uw, dw, got, out):
    h = pos[1]
    for m, w in enumerate((gw, uw, dw)):
        out[m, at(h * 192, 192), :] = w[:, at(h * HALF, HALF)]
        out[m, at((1 - h) * 192, 192), :] = got[m]


def partial_body(first, count, pos, x0, x1, x2, x3, w, out):
    y = pos[0]

    def block(i, carry):
        rs = at(i * 256, 256)
        acc = None
        for x, off in zip((x0, x1, x2, x3), OFFS):
            wc = w[first : first + count, :, chunk_cols(y, off)].reshape(count * UNITS, CH)
            part = mm(x[rs, :], wc, NT)
            acc = part if acc is None else acc + part
        out[rs, :] = acc
        return carry

    lax.fori_loop(0, 3, block, 0)


def input_part(both, w, y, off):
    wc = w[0:2, :, chunk_cols(y, off)].reshape(2 * UNITS, CH)
    return (mm(both[...], wc) * (2 * FF) ** (-0.5)).astype(BF)


def mid_body(pos, gu_a, gu_b, bk_a, bk_b, w, both, hd, cb, d2, dp, dm, d0):
    y, h = pos[0], pos[1]
    scale = D**-0.5
    own = (iota((128, UNITS), 1) >= 192) == (h == 1)

    def block(i, carry):
        rs = at(i * 128, 128)
        gate = (gu_a[rs, :UNITS] + gu_b[rs, :UNITS]) * scale
        up = (gu_a[rs, UNITS:] + gu_b[rs, UNITS:]) * scale
        back = bk_a[rs, :] + bk_b[rs, :]
        sig = jax.nn.sigmoid(gate)
        active = gate * sig
        hidden = active * up
        slope = sig * (1.0 + gate * (1.0 - sig))
        scaled = back * scale
        both[rs, :UNITS] = (scaled * up * slope).astype(BF)
        both[rs, UNITS:] = (scaled * active).astype(BF)
        hd[rs, :] = hidden.astype(BF)
        c = jnp.sum(jnp.where(own, hidden * back, F32(0.0)), axis=1, keepdims=True)
        cb[rs, :] = jnp.broadcast_to(c * (D * FF) ** (-0.5), (128, 128)).astype(BF)
        return carry

    lax.fori_loop(0, 6, block, 0)
    d2[...] = input_part(both, w, y, 2)
    dp[...] = input_part(both, w, y, 1)
    dm[...] = input_part(both, w, y, -1)
    d0[...] = input_part(both, w, y, 0)


def finish_body(pos, d0, a, b, c, out):
    total = d0[...].astype(F32) + a[...].astype(F32) + b[...].astype(F32) + c[...].astype(F32)
    out[...] = total.astype(BF)


def wgrad(pos, half, gu_t, hd_t, xs, gs, store):
    y = pos[0]
    rows = at(half * 192, 192)
    lhs = gu_t[:, rows, :].reshape(2 * 192, ROWS)
    low = hd_t[rows, :]
    factor = 512.0 ** (-0.5)
    for x, g, off in zip(xs, gs, OFFS):
        part = (mm(lhs, x[...]) * factor).astype(BF)
        c = lax.rem(y + (off + 4), 4) * CH
        store(0, c, part[:192])
        store(1, c, part[192:])
        store(2, c, (mm(low, g[...]) * factor).astype(BF))


def wgrad_other_body(pos, both, hd, *refs):
    xs, gs, (gu_t, hd_t, out) = refs[:4], refs[4:8], refs[8:]
    for m in range(2):
        gu_t[m] = both[:, m * UNITS : (m + 1) * UNITS].T
    hd_t[...] = hd[...].T

    def store(m, c, part):
        out[m, :, at(c, CH)] = part

    wgrad(pos, 1 - pos[1], gu_t, hd_t, xs, gs, store)


def wgrad_own_body(pos, gu_t, hd_t, got, *refs):
    xs, gs, outs = refs[:4], refs[4:8], refs[8:]
    h = pos[1]
    for m in range(3):
        outs[m][:, at((1 - h) * HALF, HALF)] = got[m]

    def store(m, c, part):
        outs[m][:, at(h * HALF + c, CH)] = part

    wgrad(pos, h, gu_t, hd_t, xs, gs, store)


def hi_lo(x):
    hi = x.astype(BF).astype(F32)
    wide = jnp.concatenate([hi, x - hi], axis=0)
    return jnp.concatenate([wide, jnp.zeros((16, CH - 128), F32)], axis=1).astype(BF)


def collect_body(pos, ids, pk, r, cb, q, cg, sib):
    h = pos[1]
    pair = (ids[...], got_ids(pk))
    key = jnp.concatenate([slot_key(i).T for i in pair], axis=0).astype(BF)
    rows = expert_rows()
    key = mm(key, rows, NT)
    _, core, slot = row_parts(iota((256, ROWS), 1))
    core = core == ((iota((256, ROWS), 0) >= 128) != (h == 1))
    lhs = onehot((key == slot.astype(F32)) & core).astype(BF)
    acc = mm(lhs, r[...])
    q[...] = acc[:128].astype(BF)
    sib[:128, :] = acc[128:].astype(BF)
    tokw = mm(lhs, (cb[:, :EXPERTS].astype(F32) * rows.astype(F32)).astype(BF))
    e = iota((EXPERTS, 128), 0)
    sums = []
    for b, idv in enumerate(pair):
        tw = tokw[b * 128 : (b + 1) * 128].T
        picked = [
            jnp.sum(jnp.where(idv[k : k + 1, :] == e, tw, F32(0.0)), axis=0, keepdims=True)
            for k in range(TOP)
        ]
        sums.append(jnp.concatenate(picked, axis=0))
    cg[...] = sums[0]
    sib[128:, :] = hi_lo(sums[1])


def merge_body(pos, q, cg, got, out):
    out[:128, :] = q[...]
    out[128:256, :] = got[:128, :]
    tail = got[128:144, :128].astype(F32)
    out[256:, :] = hi_lo(cg[...] + tail[:8] + tail[8:])


def assemble_body(pos, comb, q, left, right, across, out, cg):
    y, h = pos[0], pos[1]
    total = jnp.zeros((16, 128), F32)
    for off, ref in zip(OFFS, (q, left, right, across)):
        c = lax.rem(y + (off + 4), 4) * CH
        out[:, at(h * HALF + c, CH)] = ref[:128, :]
        out[:, at((1 - h) * HALF + c, CH)] = ref[128:256, :]
        total = total + ref[256:272, :128].astype(F32)
    cg[...] = (total[:8] + total[8:]) / comb[...].astype(F32)


def on_device(tokens, out_grad, expert_ids, combine, gate_weight, up_weight, down_weight):
    n_dp = lax.axis_size("dp")
    width = lax.axis_size("expert")
    up_ring = [(i, (i + 1) % n_dp) for i in range(n_dp)]
    down_ring = [(i, (i - 1) % n_dp) for i in range(n_dp)]
    far = [(i, (i + 2) % n_dp) for i in range(n_dp)]
    cores = [(i, i ^ 1) for i in range(width)]
    same_core = [list(range(c, width, 2)) for c in range(2)]

    def up(x):
        return lax.ppermute(x, "dp", up_ring)

    def down(x):
        return lax.ppermute(x, "dp", down_ring)

    def swap(x):
        return lax.ppermute(x, "expert", cores)

    def exchange(x):
        n = x.shape[1]
        x = x.reshape(EXPERTS, GROUP, n)
        x = lax.all_to_all(
            x, "expert", split_axis=0, concat_axis=0, axis_index_groups=same_core, tiled=True
        )
        return x.reshape(ROWS, n)

    def across(x):
        return lax.ppermute(x, "dp", far)

    def spread(x):
        return x, up(x), down(x), across(x)

    tie = lax.optimization_barrier
    pos = jnp.stack([lax.axis_index("dp"), lax.axis_index("expert") & 1]).astype(I32)
    ids = expert_ids.T
    comb = combine.T
    gw, uw, dw = gate_weight[0], up_weight[0], down_weight[0]

    (pk,) = call(
        pack_body, [((272, CH), BF)], (pos, ids, comb, tokens, out_grad), name="pack"
    )
    pk = swap(pk)

    def send(weighted, rows):
        return call(
            functools.partial(send_body, weighted), [((ROWS, CH), BF)],
            (pos, ids, comb, pk, rows), name="send",
        )[0]

    xs = exchange(send(False, tokens))
    gs, xs = tie((send(True, out_grad), xs))
    gs = exchange(gs)
    (wsend,) = call(
        weight_send_body, [((3, 192, HALF), BF)], (pos, gw, uw, dw), name="weight_send"
    )
    wgot = swap(wsend)
    (wall,) = call(
        weight_join_body, [((3, UNITS, HALF), BF)], (pos, gw, uw, dw, wgot), name="weight_join"
    )
    xs, gs = spread(xs), spread(gs)
    (gu_a,) = call(
        functools.partial(partial_body, 0, 2), [((ROWS, 2 * UNITS), F32)], (pos, *xs, wall),
        name="gate_up",
    )
    gu_b = swap(gu_a)
    (bk_a,) = call(
        functools.partial(partial_body, 2, 1), [((ROWS, UNITS), F32)], (pos, *gs, wall),
        name="back",
    )
    bk_b = swap(bk_a)
    both, hd, cb, d2, dp, dm, d0 = call(
        mid_body,
        [((ROWS, 2 * UNITS), BF), ((ROWS, UNITS), BF), ((ROWS, 128), BF)]
        + [((ROWS, CH), BF)] * 4,
        (pos, gu_a, gu_b, bk_a, bk_b, wall), name="mid",
    )
    d2, dp, dm = across(d2), up(dp), down(dm)
    dp, cb = tie((dp, cb))
    cb = exchange(cb)
    gu_t, hd_t, dsend = call(
        wgrad_other_body,
        [((2, UNITS, ROWS), BF), ((UNITS, ROWS), BF), ((3, 192, HALF), BF)],
        (pos, both, hd, *xs, *gs), name="wgrad_other",
    )
    dgot = swap(dsend)
    d0, gu_t, cb = tie((d0, gu_t, cb))
    (r,) = call(finish_body, [((ROWS, CH), BF)], (pos, d0, dp, dm, d2), name="finish")
    gu_t, r = tie((gu_t, r))
    r = exchange(r)
    dwg, dwu, dwd = call(
        wgrad_own_body, [((192, D), BF)] * 3, (pos, gu_t, hd_t, dgot, *xs, *gs),
        name="wgrad_own",
    )
    r, dwg = tie((r, dwg))
    q, cg, sib = call(
        collect_body, [((128, CH), BF), ((TOP, 128), F32), ((144, CH), BF)],
        (pos, ids, pk, r, cb), name="collect",
    )
    got = swap(sib)
    (q,) = call(merge_body, [((272, CH), BF)], (pos, q, cg, got), name="merge")
    input_grad, cg = call(
        assemble_body, [((128, D), BF), ((TOP, 128), F32)], (pos, comb, *spread(q)),
        name="assemble",
    )
    return (input_grad, cg.T, dwg[None], dwu[None], dwd[None])


def solution(mesh):
    rows = P("expert", None)
    units = P("expert", "dp", None)
    return jax.shard_map(
        on_device,
        mesh=mesh,
        in_specs=(rows, rows, rows, rows, units, units, units),
        out_specs=(rows, rows, units, units, units),
        check_vma=False,
    )
```

time: 780 us -> 234 us (0.30)
  waiting for transfers between devices: 417 us -> 114 us
  blocking collectives: 209 us -> 0 us
  Pallas kernels: 0 us -> 66.7 us
  local copies, waits for them, and re-layouts: 48 us -> 2.63 us
  matrix products: 45.3 us -> 0 us
  between operations: 14.3 us -> 0.72 us
    all_to_all x4, waiting for transfers between devices: 343 us -> 51.3 us  [exchange(): lax.all_to_all(x, 'expert', split_axis=0, concat_axis=0, axis_index_group...]
    all_to_all x1 -> x0, blocking collectives: 194 us -> none  [on_device(): lax.all_to_all(low_input, 'expert', split_axis=0, concat_axis=0, tiled=True)]
    reduce_scatter x1 -> x0, waiting for transfers between devices: 73.3 us -> none  [on_device(): lax.psum_scatter(back_input.astype(jnp.float32).astype(jnp.bfloat16), 'dp...]
    pallas_call x0 -> x14, Pallas kernels: none -> 66.7 us  [call(): pl.pallas_call(body, out_shape=[jax.ShapeDtypeStruct(s, t) for s, t in ou...]
    ppermute x0 -> x18, waiting for transfers between devices: none -> 63 us  [the longest x4 24.3 us: down(): return lax.ppermute(x, 'dp', down_ring)]
    dot_general x12 -> x0, matrix products: 45.3 us -> none  [the longest x1 5.97 us: expert_rows(): lax.dot_general(token_rows, gate_w, contract, preferred_element_type=jnp....]
    reshape x3 -> x0, local copies, waits for them, and re-layouts: 29.6 us -> none  [the longest x1 9.94 us: on_device(): got_grads.reshape(-1, model_width)]
    ppermute x0 -> x18, starting transfers between devices: none -> 18.2 us  [the longest x4 8 us: across(): return lax.ppermute(x, 'dp', far)]
  transfers between devices with their start and end apart: 6 -> 22, of which waited for: 3 -> 15; matrix products, arithmetic and copies ran while one was open for 7% -> 0% of each run, Pallas kernels for 0% -> 18%
where the time goes in v1:
time: 234 us; the launch traced here: 233 us
  waiting for transfers between devices  114 us (49%)
  Pallas kernels  66.7 us (29%)
  starting transfers between devices  47.8 us (20%)
  local copies, waits for them, and re-layouts  2.63 us (1%)
    pallas_call x14, Pallas kernels, call(): pl.pallas_call(body, out_shape=[jax.ShapeDtypeStruct(s, t) for s, t in ou...  66.7 us
    all_to_all x4, waiting for transfers between devices, exchange(): lax.all_to_all(x, 'expert', split_axis=0, concat_axis=0, axis_index_group...  51.3 us
    all_to_all x4, starting transfers between devices, exchange(): lax.all_to_all(x, 'expert', split_axis=0, concat_axis=0, axis_index_group...  29.7 us
    ppermute x4, waiting for transfers between devices, down(): return lax.ppermute(x, 'dp', down_ring)  24.3 us
    ppermute x4, waiting for transfers between devices, across(): return lax.ppermute(x, 'dp', far)  17.3 us
    ppermute x4, waiting for transfers between devices, up(): return lax.ppermute(x, 'dp', up_ring)  16.8 us
    ppermute x4, starting transfers between devices, across(): return lax.ppermute(x, 'dp', far)  8 us
    ppermute x4, starting transfers between devices, down(): return lax.ppermute(x, 'dp', down_ring)  6.64 us
  transfers between devices with their start and end apart: 22, of which 15 were waited for; matrix products, arithmetic and copies ran while one was open for 0% of the time, Pallas kernels for 18%

profile of v1, /device:TPU:2, one launch (start us, length us, event | category | flops | bytes accessed | tf_op | source)
XLA Modules:
  0.0 232.7 jit_solution(7139744002876711573)
XLA Ops:
  0.6 0.6 pad_add_fusion.pos
  1.2 2.3 pack.1
  3.5 0.0 collective-permute-start
  3.5 3.9 %weight_send.1 = bf16[3,192,2048]{2,1,0:T(8,128)(2,1)} custom-call(s32[2]{0:T(128)} %pad_add_fusion.pos, bf16[192,4096]{1,0:T(8,128)(2,1)} %bitcast.23, bf16[192,4096]{1,0:T(8,128)(2,1)} %bitcast.25, bf16[192,4096]{1,0:T(8,128)(2,1)} %bitcast.27), custom_call_target="tpu_custom_call" | custom-call | flops 399999991808 | tf_op jit(solution)/shard_map/weight_send/pallas_call | solution.py:50
  7.5 0.5 collective-permute-start.4
  8.0 0.0 collective-permute-done.pk
  8.0 3.0 %send.3 = bf16[768,512]{1,0:T(8,128)(2,1)} custom-call(s32[2]{0:T(128)} %pad_add_fusion.pos, s32[8,128]{1,0:T(8,128)} %bitcast.30, bf16[8,128]{1,0:T(8,128)(2,1)} %bitcast.34, bf16[272,512]{1,0:T(8,128)(2,1)} %collective-permute-done.pk, bf16[128,4096]{1,0:T(8,128)(2,1)} %rows_ref.3), custom_call_target="tpu_custom_call" | custom-call | flops 299999985664 | tf_op jit(solution)/shard_map/send/pallas_call | solution.py:50
  11.0 11.7 %all-to-all-start = ((bf16[32,24,512]{2,1,0:T(8,128)(2,1)}), bf16[32,24,512]{2,1,0:T(8,128)(2,1)}, u32[]{:S(2)}, u32[]{:S(2)}) async-start(bf16[32,24,512]{2,1,0:T(8,128)(2,1)} %bitcast.21), calls=%async_computation | async-start | bytes 1572864 | tf_op jit(solution)/shard_map/all_to_all | solution.py:315
  22.6 3.2 %send.2 = bf16[768,512]{1,0:T(8,128)(2,1)} custom-call(s32[2]{0:T(128)} %pad_add_fusion.pos, s32[8,128]{1,0:T(8,128)} %bitcast.31, bf16[8,128]{1,0:T(8,128)(2,1)} %bitcast.35, bf16[272,512]{1,0:T(8,128)(2,1)} %collective-permute-done.pk, bf16[128,4096]{1,0:T(8,128)(2,1)} %rows_ref.2), custom_call_target="tpu_custom_call" | custom-call | flops 299999985664 | tf_op jit(solution)/shard_map/send/pallas_call | solution.py:50
  25.8 19.5 %all-to-all-done = bf16[32,24,512]{2,1,0:T(8,128)(2,1)} async-done(((bf16[32,24,512]{2,1,0:T(8,128)(2,1)}), bf16[32,24,512]{2,1,0:T(8,128)(2,1)}, u32[]{:S(2)}, u32[]{:S(2)}) %all-to-all-start) | async-done | bytes 786464 | tf_op jit(solution)/shard_map/all_to_all | solution.py:315
  45.3 3.2 %collective-permute-start.3 = (bf16[768,512]{1,0:T(8,128)(2,1)}, bf16[768,512]{1,0:T(8,128)(2,1)}, u32[]{:S(2)}, u32[]{:S(2)}) collective-permute-start(bf16[768,512]{1,0:T(8,128)(2,1)} %bitcast.5.x0.refs_0_), channel_id=1, source_target_pairs={{0,128},{64,192},{128,0},{192,64},{1,129},{65,193},{129,1},{193,65... | collective-permute-start | bytes 2359304 | tf_op jit(solution)/shard_map/ppermute | solution.py:321
  48.5 1.1 collective-permute-start.2
  49.6 1.0 collective-permute-start.1
  50.5 5.6 %all-to-all-start.1 = ((bf16[32,24,512]{2,1,0:T(8,128)(2,1)}), bf16[32,24,512]{2,1,0:T(8,128)(2,1)}, u32[]{:S(2)}, u32[]{:S(2)}) async-start(bf16[32,24,512]{2,1,0:T(8,128)(2,1)} %bitcast.20), calls=%async_computation.1 | async-start | bytes 1572864 | tf_op jit(solution)/shard_map/all_to_all | solution.py:315
  56.2 0.0 collective-permute-done.4.got
  56.2 5.6 %weight_join.1.w = bf16[3,384,2048]{2,1,0:T(8,128)(2,1)} custom-call(s32[2]{0:T(128)} %pad_add_fusion.pos, bf16[192,4096]{1,0:T(8,128)(2,1)} %bitcast.24, bf16[192,4096]{1,0:T(8,128)(2,1)} %bitcast.26, bf16[192,4096]{1,0:T(8,128)(2,1)} %bitcast.28, bf16[3,192,2048]{2,1,0:T(8,128)(2,1)} %collective-permute-done.4.got), custom_call_target="tpu_custom_call" | custom-call | flops 599999971328 | tf_op jit(solution)/shard_map/weight_join/pallas_call | solution.py:50
  61.7 15.0 %all-to-all-done.1 = bf16[32,24,512]{2,1,0:T(8,128)(2,1)} async-done(((bf16[32,24,512]{2,1,0:T(8,128)(2,1)}), bf16[32,24,512]{2,1,0:T(8,128)(2,1)}, u32[]{:S(2)}, u32[]{:S(2)}) %all-to-all-start.1) | async-done | bytes 786464 | tf_op jit(solution)/shard_map/all_to_all | solution.py:315
  76.8 1.0 collective-permute-start.8
  77.8 2.3 %collective-permute-start.7 = (bf16[768,512]{1,0:T(8,128)(2,1)}, bf16[768,512]{1,0:T(8,128)(2,1)}, u32[]{:S(2)}, u32[]{:S(2)}) collective-permute-start(bf16[768,512]{1,0:T(8,128)(2,1)} %bitcast.10.x0.refs_4_), channel_id=1, source_target_pairs={{0,192},{64,0},{128,64},{192,128},{1,193},{65,1},{129,65},{193,129... | collective-permute-start | bytes 2359304 | tf_op jit(solution)/shard_map/ppermute | solution.py:307
  80.1 0.0 collective-permute-done.3.x3.refs_3_
  80.1 0.0 collective-permute-start.6
  80.1 4.7 %collective-permute-done.2.x2.refs_2_ = bf16[768,512]{1,0:T(8,128)(2,1)} collective-permute-done((bf16[768,512]{1,0:T(8,128)(2,1)}, bf16[768,512]{1,0:T(8,128)(2,1)}, u32[]{:S(2)}, u32[]{:S(2)}) %collective-permute-start.2) | collective-permute-done | bytes 786464 | tf_op jit(solution)/shard_map/ppermute | solution.py:307
  84.8 0.0 collective-permute-done.1.x1.refs_1_
  84.8 7.8 %gate_up.1.gu_a = f32[768,768]{1,0:T(8,128)} custom-call(s32[2]{0:T(128)} %pad_add_fusion.pos, bf16[768,512]{1,0:T(8,128)(2,1)} %bitcast.5.x0.refs_0_, bf16[768,512]{1,0:T(8,128)(2,1)} %collective-permute-done.1.x1.refs_1_, bf16[768,512]{1,0:T(8,128)(2,1)} %collective-permute-done.2.x2.refs_2_, bf16[768,512]{1,0:T(8,128)(2,1)} %collective-permute-done.3.x3.refs_3_, ...), custom_call_target="tpu_custom_call" | custom-call | flops 699999977472 | tf_op jit(solution)/shard_map/gate_up/pallas_call | solution.py:50
  92.7 0.0 collective-permute-start.5
  92.7 8.8 %collective-permute-done.8.x3.refs_7_ = bf16[768,512]{1,0:T(8,128)(2,1)} collective-permute-done((bf16[768,512]{1,0:T(8,128)(2,1)}, bf16[768,512]{1,0:T(8,128)(2,1)}, u32[]{:S(2)}, u32[]{:S(2)}) %collective-permute-start.8) | collective-permute-done | bytes 786464 | tf_op jit(solution)/shard_map/ppermute | solution.py:321
  101.4 14.4 %collective-permute-done.7.x2.refs_6_ = bf16[768,512]{1,0:T(8,128)(2,1)} collective-permute-done((bf16[768,512]{1,0:T(8,128)(2,1)}, bf16[768,512]{1,0:T(8,128)(2,1)}, u32[]{:S(2)}, u32[]{:S(2)}) %collective-permute-start.7) | collective-permute-done | bytes 786464 | tf_op jit(solution)/shard_map/ppermute | solution.py:307
  115.8 0.0 collective-permute-done.6.x1.refs_5_
  115.8 6.5 %back.1.bk_a = f32[768,384]{1,0:T(8,128)} custom-call(s32[2]{0:T(128)} %pad_add_fusion.pos, bf16[768,512]{1,0:T(8,128)(2,1)} %bitcast.10.x0.refs_4_, bf16[768,512]{1,0:T(8,128)(2,1)} %collective-permute-done.6.x1.refs_5_, bf16[768,512]{1,0:T(8,128)(2,1)} %collective-permute-done.7.x2.refs_6_, bf16[768,512]{1,0:T(8,128)(2,1)} %collective-permute-done.8.x3.refs_7_, ...), custom_call_target="tpu_custom_call" | custom-call | flops 499999997952 | tf_op jit(solution)/shard_map/back/pallas_call | solution.py:50
  122.3 0.0 collective-permute-start.9
  122.3 0.0 collective-permute-done.5.gu_b
  122.3 3.0 %collective-permute-done.9.bk_b = f32[768,384]{1,0:T(8,128)S(1)} collective-permute-done((f32[768,384]{1,0:T(8,128)}, f32[768,384]{1,0:T(8,128)S(1)}, u32[]{:S(2)}, u32[]{:S(2)}) %collective-permute-start.9) | collective-permute-done | bytes 1179680 | tf_op jit(solution)/shard_map/ppermute | solution.py:310
  125.4 1.0 copy-done
  126.4 9.4 %mid.1 = (bf16[768,768]{1,0:T(8,128)(2,1)}, bf16[768,384]{1,0:T(8,128)(2,1)}, bf16[768,128]{1,0:T(8,128)(2,1)}, bf16[768,512]{1,0:T(8,128)(2,1)}, bf16[768,512]{...) custom-call(s32[2]{0:T(128)} %pad_add_fusion.pos, f32[768,768]{1,0:T(8,128)} %gate_up.1.gu_a, ...), custom_call_target="tpu_custom_call" | custom-call | flops 999999995904 | tf_op jit(solution)/shard_map/mid/pallas_call | solution.py:50
  135.7 1.3 collective-permute-start.10
  137.1 1.9 collective-permute-start.11
  139.0 1.5 collective-permute-start.12
  140.5 16.3 %collective-permute-done.10.a = bf16[768,512]{1,0:T(8,128)(2,1)} collective-permute-done((bf16[768,512]{1,0:T(8,128)(2,1)}, bf16[768,512]{1,0:T(8,128)(2,1)}, u32[]{:S(2)}, u32[]{:S(2)}) %collective-permute-start.10) | collective-permute-done | bytes 786464 | tf_op jit(solution)/shard_map/ppermute | solution.py:304
  156.8 6.2 %all-to-all-start.2 = ((bf16[32,24,128]{2,1,0:T(8,128)(2,1)}), bf16[32,24,128]{2,1,0:T(8,128)(2,1)}, u32[]{:S(2)}, u32[]{:S(2)}) async-start(bf16[32,24,128]{2,1,0:T(8,128)(2,1)} %bitcast.22), calls=%async_computation.2 | async-start | bytes 393216 | tf_op jit(solution)/shard_map/all_to_all | solution.py:315
  163.0 7.1 %wgrad_other.1 = (bf16[2,384,768]{2,1,0:T(8,128)(2,1)}, bf16[384,768]{1,0:T(8,128)(2,1)}, bf16[3,192,2048]{2,1,0:T(8,128)(2,1)}) custom-call(s32[2]{0:T(128)} %pad_add_fusion.pos, bf16[768,768]{1,0:T(8,128)(2,1)} %get-tuple-element.37.both, bf16[768,384]{1,0:T(8,128)(2,1)} %get-tuple-element.38.hd, bf16[768,512]{1,0:T(8,128)(2,1)} %bitcast.5.x0.refs_0_, ...), custom_call_target="tpu_custom_call" | custom-call | flops 799999983616 | tf_op jit(solution)/shard_map/wgrad_other/pallas_call | solution.py:50
  170.1 0.0 collective-permute-start.13
  170.1 2.3 all-to-all-done.2
  172.4 0.6 collective-permute-done.11.b
  173.0 1.5 collective-permute-done.12.c
  174.5 3.1 %finish.1 = bf16[768,512]{1,0:T(8,128)(2,1)} custom-call(s32[2]{0:T(128)} %pad_add_fusion.pos, bf16[768,512]{1,0:T(8,128)(2,1)} %get-tuple-element.44.d0, bf16[768,512]{1,0:T(8,128)(2,1)} %collective-permute-done.10.a, bf16[768,512]{1,0:T(8,128)(2,1)} %collective-permute-done.11.b, bf16[768,512]{1,0:T(8,128)(2,1)} %collective-permute-done.12.c), custom_call_target="tpu_custom_call" | custom-call | flops 199999995904 | tf_op jit(solution)/shard_map/finish/pallas_call | solution.py:50
  177.6 6.2 %all-to-all-start.3 = ((bf16[32,24,512]{2,1,0:T(8,128)(2,1)}), bf16[32,24,512]{2,1,0:T(8,128)(2,1)}, u32[]{:S(2)}, u32[]{:S(2)}) async-start(bf16[32,24,512]{2,1,0:T(8,128)(2,1)} %bitcast.19), calls=%async_computation.3 | async-start | bytes 1572864 | tf_op jit(solution)/shard_map/all_to_all | solution.py:315
  183.8 0.0 collective-permute-done.13.got
  183.8 8.0 %wgrad_own.1 = (bf16[192,4096]{1,0:T(8,128)(2,1)}, bf16[192,4096]{1,0:T(8,128)(2,1)}, bf16[192,4096]{1,0:T(8,128)(2,1)}) custom-call(s32[2]{0:T(128)} %pad_add_fusion.pos, bf16[2,384,768]{2,1,0:T(8,128)(2,1)} %get-tuple-element.49.gu_t, bf16[384,768]{1,0:T(8,128)(2,1)} %get-tuple-element.50.hd_t, bf16[3,192,2048]{2,1,0:T(8,128)(2,1)} %collective-permute-done.13.got, ...), custom_call_target="tpu_custom_call" | custom-call | flops 799999983616 | tf_op jit(solution)/shard_map/wgrad_own/pallas_call | solution.py:50
  191.8 14.5 %all-to-all-done.3 = bf16[32,24,512]{2,1,0:T(8,128)(2,1)} async-done(((bf16[32,24,512]{2,1,0:T(8,128)(2,1)}), bf16[32,24,512]{2,1,0:T(8,128)(2,1)}, u32[]{:S(2)}, u32[]{:S(2)}) %all-to-all-start.3) | async-done | bytes 786464 | tf_op jit(solution)/shard_map/all_to_all | solution.py:315
  206.3 2.8 %collect.1 = (bf16[128,512]{1,0:T(8,128)(2,1)}, f32[8,128]{1,0:T(8,128)}, bf16[144,512]{1,0:T(8,128)(2,1)}) custom-call(s32[2]{0:T(128)} %pad_add_fusion.pos, s32[8,128]{1,0:T(8,128)} %bitcast.32, bf16[272,512]{1,0:T(8,128)(2,1)} %collective-permute-done.pk, bf16[768,512]{1,0:T(8,128)(2,1)} %bitcast.14.r, bf16[768,128]{1,0:T(8,128)(2,1)} %bitcast.12.cb), custom_call_target="tpu_custom_call" | custom-call | flops 299999985664 | tf_op jit(solution)/shard_map/collect/pallas_call | solution.py:50
  209.1 0.0 collective-permute-start.14
  209.1 1.6 collective-permute-done.14.got
  210.7 0.7 copy-done.4
  211.3 1.7 merge.1.q
  213.0 2.3 collective-permute-start.17
  215.3 1.4 collective-permute-start.16
  216.6 0.7 collective-permute-start.15
  217.3 7.0 %collective-permute-done.17.across = bf16[272,512]{1,0:T(8,128)(2,1)S(1)} collective-permute-done((bf16[272,512]{1,0:T(8,128)(2,1)}, bf16[272,512]{1,0:T(8,128)(2,1)S(1)}, u32[]{:S(2)}, u32[]{:S(2)}) %collective-permute-start.17) | collective-permute-done | bytes 278560 | tf_op jit(solution)/shard_map/ppermute | solution.py:321
  224.3 4.7 %collective-permute-done.16.right = bf16[272,512]{1,0:T(8,128)(2,1)S(1)} collective-permute-done((bf16[272,512]{1,0:T(8,128)(2,1)}, bf16[272,512]{1,0:T(8,128)(2,1)S(1)}, u32[]{:S(2)}, u32[]{:S(2)}) %collective-permute-start.16) | collective-permute-done | bytes 278560 | tf_op jit(solution)/shard_map/ppermute | solution.py:307
  229.0 0.5 collective-permute-done.15.left
  229.4 0.0 copy-done.1
  229.4 0.2 copy-done.2
  229.7 0.7 copy-done.3
  230.4 2.3 assemble.1
  (5 shorter events, 0.0 us)
Async XLA Ops:
  3.5 4.5 %collective-permute-start = (bf16[272,512]{1,0:T(8,128)(2,1)}, bf16[272,512]{1,0:T(8,128)(2,1)}, u32[]{:S(2)}, u32[]{:S(2)}) collective-permute-start(bf16[272,512]{1,0:T(8,128)(2,1)} %pack.1), channel_id=1, source_target_pairs={{0,1},{1,0},{2,3},{3,2},{4,5},{5,4},{6,7},{7,6},{8,9},{9,8},{10,11... | collective-permute-start | bytes 835592 | tf_op jit(solution)/shard_map/ppermute | solution.py:310
  7.5 48.7 %collective-permute-start.4 = (bf16[3,192,2048]{2,1,0:T(8,128)(2,1)}, bf16[3,192,2048]{2,1,0:T(8,128)(2,1)}, u32[]{:S(2)}, u32[]{:S(2)}) collective-permute-start(bf16[3,192,2048]{2,1,0:T(8,128)(2,1)} %weight_send.1), channel_id=1, source_target_pairs={{0,1},{1,0},{2,3},{3,2},{4,5},{5,4},{6,7},{7,6},{8,9},{9,8},{10,11... | collective-permute-start | bytes 7077896 | tf_op jit(solution)/shard_map/ppermute | solution.py:310
  11.0 34.3 %all-to-all-start = ((bf16[32,24,512]{2,1,0:T(8,128)(2,1)}), bf16[32,24,512]{2,1,0:T(8,128)(2,1)}, u32[]{:S(2)}, u32[]{:S(2)}) async-start(bf16[32,24,512]{2,1,0:T(8,128)(2,1)} %bitcast.21), calls=%async_computation | async-start | bytes 1572864 | tf_op jit(solution)/shard_map/all_to_all | solution.py:315
  45.3 34.8 %collective-permute-start.3 = (bf16[768,512]{1,0:T(8,128)(2,1)}, bf16[768,512]{1,0:T(8,128)(2,1)}, u32[]{:S(2)}, u32[]{:S(2)}) collective-permute-start(bf16[768,512]{1,0:T(8,128)(2,1)} %bitcast.5.x0.refs_0_), channel_id=1, source_target_pairs={{0,128},{64,192},{128,0},{192,64},{1,129},{65,193},{129,1},{193,65... | collective-permute-start | bytes 2359304 | tf_op jit(solution)/shard_map/ppermute | solution.py:321
  48.5 36.3 %collective-permute-start.2 = (bf16[768,512]{1,0:T(8,128)(2,1)}, bf16[768,512]{1,0:T(8,128)(2,1)}, u32[]{:S(2)}, u32[]{:S(2)}) collective-permute-start(bf16[768,512]{1,0:T(8,128)(2,1)} %bitcast.5.x0.refs_0_), channel_id=1, source_target_pairs={{0,192},{64,0},{128,64},{192,128},{1,193},{65,1},{129,65},{193,129... | collective-permute-start | bytes 2359304 | tf_op jit(solution)/shard_map/ppermute | solution.py:307
  49.6 35.2 %collective-permute-start.1 = (bf16[768,512]{1,0:T(8,128)(2,1)}, bf16[768,512]{1,0:T(8,128)(2,1)}, u32[]{:S(2)}, u32[]{:S(2)}) collective-permute-start(bf16[768,512]{1,0:T(8,128)(2,1)} %bitcast.5.x0.refs_0_), channel_id=1, source_target_pairs={{0,64},{64,128},{128,192},{192,0},{1,65},{65,129},{129,193},{193,1... | collective-permute-start | bytes 2359304 | tf_op jit(solution)/shard_map/ppermute | solution.py:304
  50.5 26.2 %all-to-all-start.1 = ((bf16[32,24,512]{2,1,0:T(8,128)(2,1)}), bf16[32,24,512]{2,1,0:T(8,128)(2,1)}, u32[]{:S(2)}, u32[]{:S(2)}) async-start(bf16[32,24,512]{2,1,0:T(8,128)(2,1)} %bitcast.20), calls=%async_computation.1 | async-start | bytes 1572864 | tf_op jit(solution)/shard_map/all_to_all | solution.py:315
  76.8 24.6 %collective-permute-start.8 = (bf16[768,512]{1,0:T(8,128)(2,1)}, bf16[768,512]{1,0:T(8,128)(2,1)}, u32[]{:S(2)}, u32[]{:S(2)}) collective-permute-start(bf16[768,512]{1,0:T(8,128)(2,1)} %bitcast.10.x0.refs_4_), channel_id=1, source_target_pairs={{0,128},{64,192},{128,0},{192,64},{1,129},{65,193},{129,1},{193,65... | collective-permute-start | bytes 2359304 | tf_op jit(solution)/shard_map/ppermute | solution.py:321
  77.8 38.0 %collective-permute-start.7 = (bf16[768,512]{1,0:T(8,128)(2,1)}, bf16[768,512]{1,0:T(8,128)(2,1)}, u32[]{:S(2)}, u32[]{:S(2)}) collective-permute-start(bf16[768,512]{1,0:T(8,128)(2,1)} %bitcast.10.x0.refs_4_), channel_id=1, source_target_pairs={{0,192},{64,0},{128,64},{192,128},{1,193},{65,1},{129,65},{193,129... | collective-permute-start | bytes 2359304 | tf_op jit(solution)/shard_map/ppermute | solution.py:307
  80.1 35.7 %collective-permute-start.6 = (bf16[768,512]{1,0:T(8,128)(2,1)}, bf16[768,512]{1,0:T(8,128)(2,1)}, u32[]{:S(2)}, u32[]{:S(2)}) collective-permute-start(bf16[768,512]{1,0:T(8,128)(2,1)} %bitcast.10.x0.refs_4_), channel_id=1, source_target_pairs={{0,64},{64,128},{128,192},{192,0},{1,65},{65,129},{129,193},{193,1... | collective-permute-start | bytes 2359304 | tf_op jit(solution)/shard_map/ppermute | solution.py:304
  92.7 29.7 %collective-permute-start.5 = (f32[768,768]{1,0:T(8,128)}, f32[768,768]{1,0:T(8,128)}, u32[]{:S(2)}, u32[]{:S(2)}) collective-permute-start(f32[768,768]{1,0:T(8,128)} %gate_up.1.gu_a), channel_id=1, source_target_pairs={{0,1},{1,0},{2,3},{3,2},{4,5},{5,4},{6,7},{7,6},{8,9},{9,8},{10,11... | collective-permute-start | bytes 7077896 | tf_op jit(solution)/shard_map/ppermute | solution.py:310
  122.3 3.1 %collective-permute-start.9 = (f32[768,384]{1,0:T(8,128)}, f32[768,384]{1,0:T(8,128)S(1)}, u32[]{:S(2)}, u32[]{:S(2)}) collective-permute-start(f32[768,384]{1,0:T(8,128)} %back.1.bk_a), channel_id=1, source_target_pairs={{0,1},{1,0},{2,3},{3,2},{4,5},{5,4},{6,7},{7,6},{8,9},{9,8},{10,11... | collective-permute-start | bytes 3538952 | tf_op jit(solution)/shard_map/ppermute | solution.py:310
  125.4 1.0 copy-start
  135.7 21.1 %collective-permute-start.10 = (bf16[768,512]{1,0:T(8,128)(2,1)}, bf16[768,512]{1,0:T(8,128)(2,1)}, u32[]{:S(2)}, u32[]{:S(2)}) collective-permute-start(bf16[768,512]{1,0:T(8,128)(2,1)} %get-tuple-element.40), channel_id=1, source_target_pairs={{0,64},{64,128},{128,192},{192,0},{1,65},{65,129},{129,193},{193,1... | collective-permute-start | bytes 2359304 | tf_op jit(solution)/shard_map/ppermute | solution.py:304
  137.1 35.9 %collective-permute-start.11 = (bf16[768,512]{1,0:T(8,128)(2,1)}, bf16[768,512]{1,0:T(8,128)(2,1)}, u32[]{:S(2)}, u32[]{:S(2)}) collective-permute-start(bf16[768,512]{1,0:T(8,128)(2,1)} %get-tuple-element.46), channel_id=1, source_target_pairs={{0,192},{64,0},{128,64},{192,128},{1,193},{65,1},{129,65},{193,129... | collective-permute-start | bytes 2359304 | tf_op jit(solution)/shard_map/ppermute | solution.py:307
  139.0 35.5 %collective-permute-start.12 = (bf16[768,512]{1,0:T(8,128)(2,1)}, bf16[768,512]{1,0:T(8,128)(2,1)}, u32[]{:S(2)}, u32[]{:S(2)}) collective-permute-start(bf16[768,512]{1,0:T(8,128)(2,1)} %get-tuple-element.47), channel_id=1, source_target_pairs={{0,128},{64,192},{128,0},{192,64},{1,129},{65,193},{129,1},{193,65... | collective-permute-start | bytes 2359304 | tf_op jit(solution)/shard_map/ppermute | solution.py:321
  156.8 15.6 %all-to-all-start.2 = ((bf16[32,24,128]{2,1,0:T(8,128)(2,1)}), bf16[32,24,128]{2,1,0:T(8,128)(2,1)}, u32[]{:S(2)}, u32[]{:S(2)}) async-start(bf16[32,24,128]{2,1,0:T(8,128)(2,1)} %bitcast.22), calls=%async_computation.2 | async-start | bytes 393216 | tf_op jit(solution)/shard_map/all_to_all | solution.py:315
  170.1 13.7 %collective-permute-start.13 = (bf16[3,192,2048]{2,1,0:T(8,128)(2,1)}, bf16[3,192,2048]{2,1,0:T(8,128)(2,1)}, u32[]{:S(2)}, u32[]{:S(2)}) collective-permute-start(bf16[3,192,2048]{2,1,0:T(8,128)(2,1)} %get-tuple-element.51), channel_id=1, source_target_pairs={{0,1},{1,0},{2,3},{3,2},{4,5},{5,4},{6,7},{7,6},{8,9},{9,8},{10,11... | collective-permute-start | bytes 7077896 | tf_op jit(solution)/shard_map/ppermute | solution.py:310
  177.6 28.6 %all-to-all-start.3 = ((bf16[32,24,512]{2,1,0:T(8,128)(2,1)}), bf16[32,24,512]{2,1,0:T(8,128)(2,1)}, u32[]{:S(2)}, u32[]{:S(2)}) async-start(bf16[32,24,512]{2,1,0:T(8,128)(2,1)} %bitcast.19), calls=%async_computation.3 | async-start | bytes 1572864 | tf_op jit(solution)/shard_map/all_to_all | solution.py:315
  209.1 1.6 collective-permute-start.14
  210.7 0.7 copy-start.4
  213.0 11.3 %collective-permute-start.17 = (bf16[272,512]{1,0:T(8,128)(2,1)}, bf16[272,512]{1,0:T(8,128)(2,1)S(1)}, u32[]{:S(2)}, u32[]{:S(2)}) collective-permute-start(bf16[272,512]{1,0:T(8,128)(2,1)} %merge.1.q), channel_id=1, source_target_pairs={{0,128},{64,192},{128,0},{192,64},{1,129},{65,193},{129,1},{193,65... | collective-permute-start | bytes 835592 | tf_op jit(solution)/shard_map/ppermute | solution.py:321
  215.3 13.7 %collective-permute-start.16 = (bf16[272,512]{1,0:T(8,128)(2,1)}, bf16[272,512]{1,0:T(8,128)(2,1)S(1)}, u32[]{:S(2)}, u32[]{:S(2)}) collective-permute-start(bf16[272,512]{1,0:T(8,128)(2,1)} %merge.1.q), channel_id=1, source_target_pairs={{0,192},{64,0},{128,64},{192,128},{1,193},{65,1},{129,65},{193,129... | collective-permute-start | bytes 835592 | tf_op jit(solution)/shard_map/ppermute | solution.py:307
  216.6 12.8 %collective-permute-start.15 = (bf16[272,512]{1,0:T(8,128)(2,1)}, bf16[272,512]{1,0:T(8,128)(2,1)S(1)}, u32[]{:S(2)}, u32[]{:S(2)}) collective-permute-start(bf16[272,512]{1,0:T(8,128)(2,1)} %merge.1.q), channel_id=1, source_target_pairs={{0,64},{64,128},{128,192},{192,0},{1,65},{65,129},{129,193},{193,1... | collective-permute-start | bytes 835592 | tf_op jit(solution)/shard_map/ppermute | solution.py:304
  224.3 5.1 %copy-start.1 = (bf16[272,512]{1,0:T(8,128)(2,1)}, bf16[272,512]{1,0:T(8,128)(2,1)S(1)}, u32[]{:S(2)}) copy-start(bf16[272,512]{1,0:T(8,128)(2,1)S(1)} %collective-permute-done.17.across) | copy-start | bytes 835588
  229.0 0.7 copy-start.2
  229.7 0.7 copy-start.3

commit v2 on v1

--- a/solution.py
+++ b/solution.py
@@ -22,6 +22,7 @@
 UNITS = 384
 NT = (((1,), (1,)), ((), ()))
 NN = (((1,), (0,)), ((), ()))
+HR = ROWS // 2
 OFFS = (0, -1, 1, 2)
 
 SMEM = pl.BlockSpec(memory_space=pltpu.SMEM)
@@ -41,8 +42,9 @@
 
 
 COST = {
-    "pack": 2, "send": 3, "weight_send": 4, "weight_join": 6, "gate_up": 7, "back": 5, "mid": 10,
-    "wgrad_other": 8, "wgrad_own": 8, "finish": 2, "collect": 3, "merge": 2, "assemble": 2,
+    "pack": 2, "send": 3, "weight_send": 4, "weight_join": 6, "gate_up": 8, "back_near": 5, "back": 3,
+    "mid": 8, "rest": 4, "pass_on": 2,
+    "wgrad": 13, "wgrad_join": 5, "finish": 2, "collect": 3, "merge": 2, "assemble": 2,
 }
 
 
@@ -148,15 +150,16 @@
         out[m, at((1 - h) * 192, 192), :] = got[m]
 
 
-def partial_body(first, count, pos, x0, x1, x2, x3, w, out):
-    y = pos[0]
-
+def unit_weights(w, first, count, y, off):
+    return w[first : first + count, :, chunk_cols(y, off)].reshape(count * UNITS, CH)
+
+
+def near(first, count, y, xs, w, out):
     def block(i, carry):
         rs = at(i * 256, 256)
         acc = None
-        for x, off in zip((x0, x1, x2, x3), OFFS):
-            wc = w[first : first + count, :, chunk_cols(y, off)].reshape(count * UNITS, CH)
-            part = mm(x[rs, :], wc, NT)
+        for x, off in zip(xs, OFFS[:3]):
+            part = mm(x[rs, :], unit_weights(w, first, count, y, off), NT)
             acc = part if acc is None else acc + part
         out[rs, :] = acc
         return carry
@@ -164,12 +167,30 @@
     lax.fori_loop(0, 3, block, 0)
 
 
+def gate_up_body(pos, x0, x1, x2, xa, xb, w, out):
+    y = pos[0]
+    near(0, 2, y, (x0, x1, x2), w, out)
+    wc = unit_weights(w, 0, 2, y, 2)
+    out[:HR, :] += mm(xa[...], wc, NT)
+    out[HR:, :] += mm(xb[...], wc, NT)
+
+
+def back_near_body(pos, x0, x1, x2, w, out):
+    near(2, 1, pos[0], (x0, x1, x2), w, out)
+
+
+def back_body(pos, acc, xa, xb, w, out):
+    wc = unit_weights(w, 2, 1, pos[0], 2)
+    out[:HR, :] = acc[:HR, :] + mm(xa[...], wc, NT)
+    out[HR:, :] = acc[HR:, :] + mm(xb[...], wc, NT)
+
+
 def input_part(both, w, y, off):
-    wc = w[0:2, :, chunk_cols(y, off)].reshape(2 * UNITS, CH)
+    wc = unit_weights(w, 0, 2, y, off)
     return (mm(both[...], wc) * (2 * FF) ** (-0.5)).astype(BF)
 
 
-def mid_body(pos, gu_a, gu_b, bk_a, bk_b, w, both, hd, cb, d2, dp, dm, d0):
+def mid_body(pos, gu_a, gu_b, bk_a, bk_b, w, both, hd, cb, d2a, d2b):
     y, h = pos[0], pos[1]
     scale = D**-0.5
     own = (iota((128, UNITS), 1) >= 192) == (h == 1)
@@ -192,15 +213,29 @@
         return carry
 
     lax.fori_loop(0, 6, block, 0)
-    d2[...] = input_part(both, w, y, 2)
-    dp[...] = input_part(both, w, y, 1)
-    dm[...] = input_part(both, w, y, -1)
+    part = input_part(both, w, y, 2)
+    d2a[...] = part[:HR]
+    d2b[...] = part[HR:]
+
+
+def rest_body(pos, both, w, dpa, dpb, dma, dmb, d0):
+    y = pos[0]
+    for off, (top, bottom) in ((1, (dpa, dpb)), (-1, (dma, dmb))):
+        part = input_part(both, w, y, off)
+        top[...] = part[:HR]
+        bottom[...] = part[HR:]
     d0[...] = input_part(both, w, y, 0)
 
 
-def finish_body(pos, d0, a, b, c, out):
-    total = d0[...].astype(F32) + a[...].astype(F32) + b[...].astype(F32) + c[...].astype(F32)
-    out[...] = total.astype(BF)
+def pass_on_body(pos, dpa, r2, dmb, q2, pa, mb):
+    pa[...] = (dpa[...].astype(F32) + r2[...].astype(F32)).astype(BF)
+    mb[...] = (dmb[...].astype(F32) + q2[...].astype(F32)).astype(BF)
+
+
+def finish_body(pos, d0, ma, pa, mb, pb, out):
+    for rs, a, b in ((slice(0, HR), ma, pa), (slice(HR, ROWS), mb, pb)):
+        total = d0[rs, :].astype(F32) + a[...].astype(F32) + b[...].astype(F32)
+        out[rs, :] = total.astype(BF)
 
 
 def wgrad(pos, half, gu_t, hd_t, xs, gs, store):
@@ -209,36 +244,38 @@
     lhs = gu_t[:, rows, :].reshape(2 * 192, ROWS)
     low = hd_t[rows, :]
     factor = 512.0 ** (-0.5)
-    for x, g, off in zip(xs, gs, OFFS):
-        part = (mm(lhs, x[...]) * factor).astype(BF)
+    for i, off in enumerate(OFFS):
+        if i < 3:
+            part, last = mm(lhs, xs[i][...]), mm(low, gs[i][...])
+        else:
+            part = mm(lhs[:, :HR], xs[3][...]) + mm(lhs[:, HR:], xs[4][...])
+            last = mm(low[:, :HR], gs[3][...]) + mm(low[:, HR:], gs[4][...])
+        part = (part * factor).astype(BF)
         c = lax.rem(y + (off + 4), 4) * CH
         store(0, c, part[:192])
         store(1, c, part[192:])
-        store(2, c, (mm(low, g[...]) * factor).astype(BF))
-
-
-def wgrad_other_body(pos, both, hd, *refs):
-    xs, gs, (gu_t, hd_t, out) = refs[:4], refs[4:8], refs[8:]
+        store(2, c, (last * factor).astype(BF))
+
+
+def wgrad_body(pos, both, hd, *refs):
+    xs, gs, (own, other, gu_t, hd_t) = refs[:5], refs[5:10], refs[10:]
+    h = pos[1]
     for m in range(2):
         gu_t[m] = both[:, m * UNITS : (m + 1) * UNITS].T
     hd_t[...] = hd[...].T
-
-    def store(m, c, part):
-        out[m, :, at(c, CH)] = part
-
-    wgrad(pos, 1 - pos[1], gu_t, hd_t, xs, gs, store)
-
-
-def wgrad_own_body(pos, gu_t, hd_t, got, *refs):
-    xs, gs, outs = refs[:4], refs[4:8], refs[8:]
+    for half, out in ((1 - h, other), (h, own)):
+
+        def store(m, c, part, out=out):
+            out[m, :, at(c, CH)] = part
+
+        wgrad(pos, half, gu_t, hd_t, xs, gs, store)
+
+
+def wgrad_join_body(pos, own, got, *outs):
     h = pos[1]
     for m in range(3):
+        outs[m][:, at(h * HALF, HALF)] = own[m]
         outs[m][:, at((1 - h) * HALF, HALF)] = got[m]
-
-    def store(m, c, part):
-        outs[m][:, at(h * HALF + c, CH)] = part
-
-    wgrad(pos, h, gu_t, hd_t, xs, gs, store)
 
 
 def hi_lo(x):
@@ -321,7 +358,8 @@
         return lax.ppermute(x, "dp", far)
 
     def spread(x):
-        return x, up(x), down(x), across(x)
+        left, right = up(x), down(x)
+        return x, left, right, up(left[:HR]), down(right[HR:])
 
     tie = lax.optimization_barrier
     pos = jnp.stack([lax.axis_index("dp"), lax.axis_index("expert") & 1]).astype(I32)
@@ -340,59 +378,66 @@
             (pos, ids, comb, pk, rows), name="send",
         )[0]
 
-    xs = exchange(send(False, tokens))
+    xs, later = tie((send(False, tokens), pos))
+    xs = exchange(xs)
     gs, xs = tie((send(True, out_grad), xs))
     gs = exchange(gs)
     (wsend,) = call(
-        weight_send_body, [((3, 192, HALF), BF)], (pos, gw, uw, dw), name="weight_send"
+        weight_send_body, [((3, 192, HALF), BF)], (later, gw, uw, dw), name="weight_send"
     )
     wgot = swap(wsend)
     (wall,) = call(
         weight_join_body, [((3, UNITS, HALF), BF)], (pos, gw, uw, dw, wgot), name="weight_join"
     )
     xs, gs = spread(xs), spread(gs)
-    (gu_a,) = call(
-        functools.partial(partial_body, 0, 2), [((ROWS, 2 * UNITS), F32)], (pos, *xs, wall),
-        name="gate_up",
-    )
+    (gu_a,) = call(gate_up_body, [((ROWS, 2 * UNITS), F32)], (pos, *xs, wall), name="gate_up")
     gu_b = swap(gu_a)
     (bk_a,) = call(
-        functools.partial(partial_body, 2, 1), [((ROWS, UNITS), F32)], (pos, *gs, wall),
-        name="back",
+        back_near_body, [((ROWS, UNITS), F32)], (pos, *gs[:3], wall), name="back_near"
+    )
+    (bk_a,) = call(
+        back_body, [((ROWS, UNITS), F32)], (pos, bk_a, *gs[3:], wall), name="back"
     )
     bk_b = swap(bk_a)
-    both, hd, cb, d2, dp, dm, d0 = call(
+    both, hd, cb, d2a, d2b = call(
         mid_body,
         [((ROWS, 2 * UNITS), BF), ((ROWS, UNITS), BF), ((ROWS, 128), BF)]
-        + [((ROWS, CH), BF)] * 4,
+        + [((HR, CH), BF)] * 2,
         (pos, gu_a, gu_b, bk_a, bk_b, wall), name="mid",
     )
-    d2, dp, dm = across(d2), up(dp), down(dm)
-    dp, cb = tie((dp, cb))
+    r2, q2 = up(d2a), down(d2b)
+    dpa, dpb, dma, dmb, d0 = call(
+        rest_body, [((HR, CH), BF)] * 4 + [((ROWS, CH), BF)], (pos, both, wall), name="rest"
+    )
+    pb, ma = up(dpb), down(dma)
+    pa, mb = call(pass_on_body, [((HR, CH), BF)] * 2, (pos, dpa, r2, dmb, q2), name="pass_on")
+    pa, mb = up(pa), down(mb)
+    pb, cb = tie((pb, cb))
     cb = exchange(cb)
-    gu_t, hd_t, dsend = call(
-        wgrad_other_body,
-        [((2, UNITS, ROWS), BF), ((UNITS, ROWS), BF), ((3, 192, HALF), BF)],
-        (pos, both, hd, *xs, *gs), name="wgrad_other",
-    )
-    dgot = swap(dsend)
-    d0, gu_t, cb = tie((d0, gu_t, cb))
-    (r,) = call(finish_body, [((ROWS, CH), BF)], (pos, d0, dp, dm, d2), name="finish")
-    gu_t, r = tie((gu_t, r))
+    d0, cb = tie((d0, cb))
+    (r,) = call(finish_body, [((ROWS, CH), BF)], (pos, d0, ma, pa, mb, pb), name="finish")
+    both, r = tie((both, r))
     r = exchange(r)
-    dwg, dwu, dwd = call(
-        wgrad_own_body, [((192, D), BF)] * 3, (pos, gu_t, hd_t, dgot, *xs, *gs),
-        name="wgrad_own",
-    )
-    r, dwg = tie((r, dwg))
+    w_own, w_other = call(
+        wgrad_body, [((3, 192, HALF), BF)] * 2, (pos, both, hd, *xs, *gs),
+        scratch=[pltpu.VMEM((2, UNITS, ROWS), BF), pltpu.VMEM((UNITS, ROWS), BF)],
+        name="wgrad",
+    )
+    r, w_other = tie((r, w_other))
+    dgot = swap(w_other)
     q, cg, sib = call(
         collect_body, [((128, CH), BF), ((TOP, 128), F32), ((144, CH), BF)],
         (pos, ids, pk, r, cb), name="collect",
     )
     got = swap(sib)
     (q,) = call(merge_body, [((272, CH), BF)], (pos, q, cg, got), name="merge")
+    q, w_own = tie((q, w_own))
+    dwg, dwu, dwd = call(
+        wgrad_join_body, [((192, D), BF)] * 3, (pos, w_own, dgot), name="wgrad_join"
+    )
+    comb, dwg = tie((comb, dwg))
     input_grad, cg = call(
-        assemble_body, [((128, D), BF), ((TOP, 128), F32)], (pos, comb, *spread(q)),
+        assemble_body, [((128, D), BF), ((TOP, 128), F32)], (pos, comb, q, up(q), down(q), across(q)),
         name="assemble",
     )
     return (input_grad, cg.T, dwg[None], dwu[None], dwd[None])

time: 234 us -> 219 us (0.936)
  waiting for transfers between devices: 114 us -> 65.8 us
  blocking collectives: 0 us -> 16.4 us
  Pallas kernels: 66.7 us -> 75.4 us
  local copies, waits for them, and re-layouts: 2.63 us -> 9.08 us
    all_to_all x4 -> x3, waiting for transfers between devices: 51.3 us -> 25.9 us  [exchange(): lax.all_to_all(x, 'expert', split_axis=0, concat_axis=0, axis_index_group...]
    ppermute x4 -> x8, starting transfers between devices: 6.64 us -> 25 us  [down(): return lax.ppermute(x, 'dp', down_ring)]
    all_to_all x0 -> x1, blocking collectives: none -> 16.4 us  [exchange(): lax.all_to_all(x, 'expert', split_axis=0, concat_axis=0, axis_index_group...]
    ppermute x4 -> x1, waiting for transfers between devices: 17.3 us -> 4.52 us  [across(): return lax.ppermute(x, 'dp', far)]
    pallas_call x14 -> x17, Pallas kernels: 66.7 us -> 75.4 us  [call(): pl.pallas_call(body, out_shape=[jax.ShapeDtypeStruct(s, t) for s, t in ou...]
    ppermute x4 -> x1, starting transfers between devices: 8 us -> 0.01 us  [across(): return lax.ppermute(x, 'dp', far)]
    ppermute x4 -> x8, waiting for transfers between devices: 24.3 us -> 17.4 us  [down(): return lax.ppermute(x, 'dp', down_ring)]
    all_to_all x4 -> x3, starting transfers between devices: 29.7 us -> 23.7 us  [exchange(): lax.all_to_all(x, 'expert', split_axis=0, concat_axis=0, axis_index_group...]
  transfers between devices with their start and end apart: 22 -> 26, of which waited for: 15 -> 15; matrix products, arithmetic and copies ran while one was open for 0% -> 2% of each run, Pallas kernels for 18% -> 24%
where the time goes in v2:
time: 219 us; the launch traced here: 217 us
  Pallas kernels  75.4 us (34%)
  waiting for transfers between devices  65.8 us (30%)
  starting transfers between devices  49.3 us (23%)
  blocking collectives  16.4 us (7%)
  local copies, waits for them, and re-layouts  9.08 us (4%)
    pallas_call x17, Pallas kernels, call(): pl.pallas_call(body, out_shape=[jax.ShapeDtypeStruct(s, t) for s, t in ou...  75.4 us
    all_to_all x3, waiting for transfers between devices, exchange(): lax.all_to_all(x, 'expert', split_axis=0, concat_axis=0, axis_index_group...  25.9 us
    ppermute x8, starting transfers between devices, down(): return lax.ppermute(x, 'dp', down_ring)  25 us
    all_to_all x3, starting transfers between devices, exchange(): lax.all_to_all(x, 'expert', split_axis=0, concat_axis=0, axis_index_group...  23.7 us
    ppermute x8, waiting for transfers between devices, down(): return lax.ppermute(x, 'dp', down_ring)  17.4 us
    all_to_all x1, blocking collectives, exchange(): lax.all_to_all(x, 'expert', split_axis=0, concat_axis=0, axis_index_group...  16.4 us
    ppermute x8, waiting for transfers between devices, up(): return lax.ppermute(x, 'dp', up_ring)  12 us
    ppermute x6, waiting for transfers between devices, swap(): return lax.ppermute(x, 'expert', cores)  6.07 us
  transfers between devices with their start and end apart: 26, of which 15 were waited for; matrix products, arithmetic and copies ran while one was open for 2% of the time, Pallas kernels for 24%

profile of v2, /device:TPU:2, one launch (start us, length us, event | category | flops | bytes accessed | tf_op | source)
XLA Modules:
  0.0 217.4 jit_solution(10377957748939625515)
XLA Ops:
  0.6 0.6 pad_add_fusion.pos
  1.3 2.3 %pack.1 = bf16[272,512]{1,0:T(8,128)(2,1)} custom-call(s32[2]{0:T(128)} %pad_add_fusion.pos, s32[8,128]{1,0:T(8,128)} %bitcast.30, bf16[8,128]{1,0:T(8,128)(2,1)} %bitcast.34, bf16[128,4096]{1,0:T(8,128)(2,1)} %rows_ref.3, bf16[128,4096]{1,0:T(8,128)(2,1)} %rows_ref.2), custom_call_target="tpu_custom_call" | custom-call | flops 199999995904 | tf_op jit(solution)/shard_map/pack/pallas_call | solution.py:52
  3.6 0.0 collective-permute-start
  3.6 1.8 collective-permute-done.pk
  5.3 0.7 copy-done.6
  6.0 3.0 %send.3 = bf16[768,512]{1,0:T(8,128)(2,1)} custom-call(s32[2]{0:T(128)} %pad_add_fusion.pos, s32[8,128]{1,0:T(8,128)} %bitcast.31, bf16[8,128]{1,0:T(8,128)(2,1)} %bitcast.35, bf16[272,512]{1,0:T(8,128)(2,1)} %copy-done.6, bf16[128,4096]{1,0:T(8,128)(2,1)} %rows_ref.3), custom_call_target="tpu_custom_call" | custom-call | flops 299999985664 | tf_op jit(solution)/shard_map/send/pallas_call | solution.py:52
  9.0 11.7 %all-to-all-start = ((bf16[32,24,512]{2,1,0:T(8,128)(2,1)}), bf16[32,24,512]{2,1,0:T(8,128)(2,1)}, u32[]{:S(2)}, u32[]{:S(2)}) async-start(bf16[32,24,512]{2,1,0:T(8,128)(2,1)} %bitcast.21), calls=%async_computation | async-start | bytes 1572864 | tf_op jit(solution)/shard_map/all_to_all | solution.py:352
  20.7 4.0 %weight_send.1 = bf16[3,192,2048]{2,1,0:T(8,128)(2,1)} custom-call(s32[2]{0:T(128)} %pad_add_fusion.pos, bf16[192,4096]{1,0:T(8,128)(2,1)} %bitcast.24, bf16[192,4096]{1,0:T(8,128)(2,1)} %bitcast.26, bf16[192,4096]{1,0:T(8,128)(2,1)} %bitcast.28), custom_call_target="tpu_custom_call" | custom-call | flops 399999991808 | tf_op jit(solution)/shard_map/weight_send/pallas_call | solution.py:52
  24.7 3.2 %send.2 = bf16[768,512]{1,0:T(8,128)(2,1)} custom-call(s32[2]{0:T(128)} %pad_add_fusion.pos, s32[8,128]{1,0:T(8,128)} %bitcast.32, bf16[8,128]{1,0:T(8,128)(2,1)} %bitcast.36, bf16[272,512]{1,0:T(8,128)(2,1)} %copy-done.6, bf16[128,4096]{1,0:T(8,128)(2,1)} %rows_ref.2), custom_call_target="tpu_custom_call" | custom-call | flops 299999985664 | tf_op jit(solution)/shard_map/send/pallas_call | solution.py:52
  27.8 15.7 %all-to-all-done = bf16[32,24,512]{2,1,0:T(8,128)(2,1)} async-done(((bf16[32,24,512]{2,1,0:T(8,128)(2,1)}), bf16[32,24,512]{2,1,0:T(8,128)(2,1)}, u32[]{:S(2)}, u32[]{:S(2)}) %all-to-all-start) | async-done | bytes 786464 | tf_op jit(solution)/shard_map/all_to_all | solution.py:352
  43.5 3.0 %collective-permute-start.2 = (bf16[768,512]{1,0:T(8,128)(2,1)}, bf16[768,512]{1,0:T(8,128)(2,1)S(1)}, u32[]{:S(2)}, u32[]{:S(2)}) collective-permute-start(bf16[768,512]{1,0:T(8,128)(2,1)} %bitcast.5.x0.refs_0_), channel_id=1, source_target_pairs={{0,192},{64,0},{128,64},{192,128},{1,193},{65,1},{129,65},{193,129... | collective-permute-start | bytes 2359304 | tf_op jit(solution)/shard_map/ppermute | solution.py:344
  46.5 5.6 %all-to-all-start.1 = ((bf16[32,24,512]{2,1,0:T(8,128)(2,1)}), bf16[32,24,512]{2,1,0:T(8,128)(2,1)}, u32[]{:S(2)}, u32[]{:S(2)}) async-start(bf16[32,24,512]{2,1,0:T(8,128)(2,1)} %bitcast.19), calls=%async_computation.1 | async-start | bytes 1572864 | tf_op jit(solution)/shard_map/all_to_all | solution.py:352
  52.1 10.0 %collective-permute-done.2.x2.refs_2_ = bf16[768,512]{1,0:T(8,128)(2,1)S(1)} collective-permute-done((bf16[768,512]{1,0:T(8,128)(2,1)}, bf16[768,512]{1,0:T(8,128)(2,1)S(1)}, u32[]{:S(2)}, u32[]{:S(2)}) %collective-permute-start.2) | collective-permute-done | bytes 786464 | tf_op jit(solution)/shard_map/ppermute | solution.py:344
  62.2 0.8 slice.17
  63.0 3.6 %collective-permute-start.4 = (bf16[384,512]{1,0:T(8,128)(2,1)}, bf16[384,512]{1,0:T(8,128)(2,1)}, u32[]{:S(2)}, u32[]{:S(2)}) collective-permute-start(bf16[384,512]{1,0:T(8,128)(2,1)} %slice.17), channel_id=1, source_target_pairs={{0,192},{64,0},{128,64},{192,128},{1,193},{65,1},{129,65},{193,129... | collective-permute-start | bytes 1179656 | tf_op jit(solution)/shard_map/ppermute | solution.py:344
  66.6 0.8 slice.16
  67.4 0.0 collective-permute-start.3
  67.4 0.0 collective-permute-done.5.got
  67.4 5.6 %weight_join.1.w = bf16[3,384,2048]{2,1,0:T(8,128)(2,1)} custom-call(s32[2]{0:T(128)} %pad_add_fusion.pos, bf16[192,4096]{1,0:T(8,128)(2,1)} %bitcast.25, bf16[192,4096]{1,0:T(8,128)(2,1)} %bitcast.27, bf16[192,4096]{1,0:T(8,128)(2,1)} %bitcast.29, bf16[3,192,2048]{2,1,0:T(8,128)(2,1)} %collective-permute-done.5.got), custom_call_target="tpu_custom_call" | custom-call | flops 599999971328 | tf_op jit(solution)/shard_map/weight_join/pallas_call | solution.py:52
  73.0 0.5 all-to-all-done.1
  73.5 3.0 %collective-permute-start.8 = (bf16[768,512]{1,0:T(8,128)(2,1)}, bf16[768,512]{1,0:T(8,128)(2,1)}, u32[]{:S(2)}, u32[]{:S(2)}) collective-permute-start(bf16[768,512]{1,0:T(8,128)(2,1)} %bitcast.10.x0.refs_5_), channel_id=1, source_target_pairs={{0,192},{64,0},{128,64},{192,128},{1,193},{65,1},{129,65},{193,129... | collective-permute-start | bytes 2359304 | tf_op jit(solution)/shard_map/ppermute | solution.py:344
  76.4 0.8 collective-permute-done.3.xa.refs_3_
  77.2 8.0 %gate_up.1.gu_a = f32[768,768]{1,0:T(8,128)} custom-call(s32[2]{0:T(128)} %pad_add_fusion.pos, bf16[768,512]{1,0:T(8,128)(2,1)} %bitcast.5.x0.refs_0_, bf16[768,512]{1,0:T(8,128)(2,1)} %copy-done.1, bf16[768,512]{1,0:T(8,128)(2,1)} %copy-done, bf16[384,512]{1,0:T(8,128)(2,1)} %collective-permute-done.3.xa.refs_3_, ...), custom_call_target="tpu_custom_call" | custom-call | flops 799999983616 | tf_op jit(solution)/shard_map/gate_up/pallas_call | solution.py:52
  85.2 5.3 %collective-permute-done.8.x2.refs_7_ = bf16[768,512]{1,0:T(8,128)(2,1)} collective-permute-done((bf16[768,512]{1,0:T(8,128)(2,1)}, bf16[768,512]{1,0:T(8,128)(2,1)}, u32[]{:S(2)}, u32[]{:S(2)}) %collective-permute-start.8) | collective-permute-done | bytes 786464 | tf_op jit(solution)/shard_map/ppermute | solution.py:344
  90.5 1.8 slice.19
  92.3 3.7 %collective-permute-start.10 = (bf16[384,512]{1,0:T(8,128)(2,1)}, bf16[384,512]{1,0:T(8,128)(2,1)}, u32[]{:S(2)}, u32[]{:S(2)}) collective-permute-start(bf16[384,512]{1,0:T(8,128)(2,1)} %slice.19), channel_id=1, source_target_pairs={{0,192},{64,0},{128,64},{192,128},{1,193},{65,1},{129,65},{193,129... | collective-permute-start | bytes 1179656 | tf_op jit(solution)/shard_map/ppermute | solution.py:344
  96.0 0.0 collective-permute-done.7.x1.refs_6_
  96.0 1.8 slice.18
  97.8 0.0 collective-permute-start.9
  97.8 5.9 %back_near.1.acc = f32[768,384]{1,0:T(8,128)} custom-call(s32[2]{0:T(128)} %pad_add_fusion.pos, bf16[768,512]{1,0:T(8,128)(2,1)} %bitcast.10.x0.refs_5_, bf16[768,512]{1,0:T(8,128)(2,1)} %collective-permute-done.7.x1.refs_6_, bf16[768,512]{1,0:T(8,128)(2,1)} %collective-permute-done.8.x2.refs_7_, bf16[3,384,2048]{2,1,0:T(8,128)(2,1)} %weight_join.1.w), custom_call_target="tpu_custom_call" | custom-call | flops 499999997952 | tf_op jit(solution)/shard_map/back_near/pallas_call | solution.py:52
  103.6 0.0 collective-permute-done.10.xb.refs_9_
  103.6 3.4 %collective-permute-done.9.xa.refs_8_ = bf16[384,512]{1,0:T(8,128)(2,1)} collective-permute-done((bf16[384,512]{1,0:T(8,128)(2,1)}, bf16[384,512]{1,0:T(8,128)(2,1)}, u32[]{:S(2)}, u32[]{:S(2)}) %collective-permute-start.9) | collective-permute-done | bytes 393248 | tf_op jit(solution)/shard_map/ppermute | solution.py:341
  107.1 4.6 %back.1.bk_a = f32[768,384]{1,0:T(8,128)} custom-call(s32[2]{0:T(128)} %pad_add_fusion.pos, f32[768,384]{1,0:T(8,128)} %back_near.1.acc, bf16[384,512]{1,0:T(8,128)(2,1)} %collective-permute-done.9.xa.refs_8_, bf16[384,512]{1,0:T(8,128)(2,1)} %collective-permute-done.10.xb.refs_9_, bf16[3,384,2048]{2,1,0:T(8,128)(2,1)} %weight_join.1.w), custom_call_target="tpu_custom_call" | custom-call | flops 299999985664 | tf_op jit(solution)/shard_map/back/pallas_call | solution.py:52
  111.6 3.0 %collective-permute-done.11.bk_b = f32[768,384]{1,0:T(8,128)S(1)} collective-permute-done((f32[768,384]{1,0:T(8,128)}, f32[768,384]{1,0:T(8,128)S(1)}, u32[]{:S(2)}, u32[]{:S(2)}) %collective-permute-start.11) | collective-permute-done | bytes 1179680 | tf_op jit(solution)/shard_map/ppermute | solution.py:347
  114.7 1.0 copy-done.3
  115.7 7.5 %mid.1 = (bf16[768,768]{1,0:T(8,128)(2,1)}, bf16[768,384]{1,0:T(8,128)(2,1)}, bf16[768,128]{1,0:T(8,128)(2,1)}, bf16[384,512]{1,0:T(8,128)(2,1)}, bf16[384,512]{1,0:T(8,128)(2,1)}) custom-call(s32[2]{0:T(128)} %pad_add_fusion.pos, f32[768,768]{1,0:T(8,128)} %gate_up.1.gu_a, f32[768,768]{1,0:T(8,128)} %collective-permute-done.6.gu_b, f32[768,384]{1,0:T(8,128)} %back.1.bk_a, ...), custom_call_target="tpu_custom_call" | custom-call | flops 799999983616 | tf_op jit(solution)/shard_map/mid/pallas_call | solution.py:52
  123.2 3.2 %collective-permute-start.15 = (bf16[384,512]{1,0:T(8,128)(2,1)}, bf16[384,512]{1,0:T(8,128)(2,1)}, u32[]{:S(2)}, u32[]{:S(2)}) collective-permute-start(bf16[384,512]{1,0:T(8,128)(2,1)} %get-tuple-element.57), channel_id=1, source_target_pairs={{0,192},{64,0},{128,64},{192,128},{1,193},{65,1},{129,65},{193,129... | collective-permute-start | bytes 1179656 | tf_op jit(solution)/shard_map/ppermute | solution.py:344
  126.4 5.6 %rest.1 = (bf16[384,512]{1,0:T(8,128)(2,1)}, bf16[384,512]{1,0:T(8,128)(2,1)}, bf16[384,512]{1,0:T(8,128)(2,1)}, bf16[384,512]{1,0:T(8,128)(2,1)}, bf16[768,512]{1,0:T(8,128)(2,1)}) custom-call(s32[2]{0:T(128)} %pad_add_fusion.pos, bf16[768,768]{1,0:T(8,128)(2,1)} %get-tuple-element.62.both, bf16[3,384,2048]{2,1,0:T(8,128)(2,1)} %weight_join.1.w), custom_call_target="tpu_custom_call" | custom-call | flops 399999991808 | tf_op jit(solution)/shard_map/rest/pallas_call | solution.py:52
  132.0 0.0 collective-permute-start.12
  132.0 3.2 %collective-permute-start.13 = (bf16[384,512]{1,0:T(8,128)(2,1)}, bf16[384,512]{1,0:T(8,128)(2,1)}, u32[]{:S(2)}, u32[]{:S(2)}) collective-permute-start(bf16[384,512]{1,0:T(8,128)(2,1)} %get-tuple-element.53), channel_id=1, source_target_pairs={{0,192},{64,0},{128,64},{192,128},{1,193},{65,1},{129,65},{193,129... | collective-permute-start | bytes 1179656 | tf_op jit(solution)/shard_map/ppermute | solution.py:344
  135.3 0.7 collective-permute-done.14.r2
  135.9 0.0 collective-permute-done.15.q2
  135.9 2.4 %pass_on.1 = (bf16[384,512]{1,0:T(8,128)(2,1)}, bf16[384,512]{1,0:T(8,128)(2,1)}) custom-call(s32[2]{0:T(128)} %pad_add_fusion.pos, bf16[384,512]{1,0:T(8,128)(2,1)} %get-tuple-element.54.dpa, bf16[384,512]{1,0:T(8,128)(2,1)} %collective-permute-done.14.r2, bf16[384,512]{1,0:T(8,128)(2,1)} %get-tuple-element.56.dmb, bf16[384,512]{1,0:T(8,128)(2,1)} %collective-permute-done.15.q2), custom_call_target="tpu_custom_call" | custom-call | flops 199999995904 | tf_op jit(solution)/shard_map/pass_on/pallas_call | solution.py:52
  138.3 0.0 collective-permute-start.16
  138.3 3.2 %collective-permute-start.17 = (bf16[384,512]{1,0:T(8,128)(2,1)}, bf16[384,512]{1,0:T(8,128)(2,1)S(1)}, u32[]{:S(2)}, u32[]{:S(2)}) collective-permute-start(bf16[384,512]{1,0:T(8,128)(2,1)} %get-tuple-element.59), channel_id=1, source_target_pairs={{0,192},{64,0},{128,64},{192,128},{1,193},{65,1},{129,65},{193,129... | collective-permute-start | bytes 1179656 | tf_op jit(solution)/shard_map/ppermute | solution.py:344
  141.5 4.1 %collective-permute-done.12.pb = bf16[384,512]{1,0:T(8,128)(2,1)} collective-permute-done((bf16[384,512]{1,0:T(8,128)(2,1)}, bf16[384,512]{1,0:T(8,128)(2,1)}, u32[]{:S(2)}, u32[]{:S(2)}) %collective-permute-start.12) | collective-permute-done | bytes 393248 | tf_op jit(solution)/shard_map/ppermute | solution.py:341
  145.6 16.4 %all_to_all.20 = bf16[32,24,128]{2,1,0:T(8,128)(2,1)} all-to-all(bf16[32,24,128]{2,1,0:T(8,128)(2,1)S(1)} %bitcast.22), channel_id=1, replica_groups={{0,2,4,6,8,10,12,14,16,18,20,22,24,26,28,30,32,34,36,38,40,42,44,46,48,..., dimensions={0} | all-to-all | bytes 393216 | tf_op jit(solution)/shard_map/all_to_all | solution.py:352
  162.1 0.7 copy-done.4
  162.8 0.8 copy-done.5
  163.6 2.8 %finish.1 = bf16[768,512]{1,0:T(8,128)(2,1)} custom-call(s32[2]{0:T(128)} %pad_add_fusion.pos, bf16[768,512]{1,0:T(8,128)(2,1)} %get-tuple-element.52.d0, bf16[384,512]{1,0:T(8,128)(2,1)} %collective-permute-done.13.ma, bf16[384,512]{1,0:T(8,128)(2,1)} %copy-done.4, bf16[384,512]{1,0:T(8,128)(2,1)} %copy-done.5, bf16[384,512]{1,0:T(8,128)(2,1)} %collective-permute-done.12.pb), custom_call_target="tpu_custom_call" | custom-call | flops 199999995904 | tf_op jit(solution)/shard_map/finish/pallas_call | solution.py:52
  166.3 6.5 %all-to-all-start.3 = ((bf16[32,24,512]{2,1,0:T(8,128)(2,1)}), bf16[32,24,512]{2,1,0:T(8,128)(2,1)}, u32[]{:S(2)}, u32[]{:S(2)}) async-start(bf16[32,24,512]{2,1,0:T(8,128)(2,1)} %bitcast.20), calls=%async_computation.3 | async-start | bytes 1572864 | tf_op jit(solution)/shard_map/all_to_all | solution.py:352
  172.8 9.2 %wgrad.1 = (bf16[3,192,2048]{2,1,0:T(8,128)(2,1)}, bf16[3,192,2048]{2,1,0:T(8,128)(2,1)}) custom-call(s32[2]{0:T(128)} %pad_add_fusion.pos, bf16[768,768]{1,0:T(8,128)(2,1)} %get-tuple-element.62.both, bf16[768,384]{1,0:T(8,128)(2,1)} %get-tuple-element.63.hd, bf16[768,512]{1,0:T(8,128)(2,1)} %bitcast.5.x0.refs_0_, bf16[768,512]{1,0:T(8,128)(2,1)} %copy-done.1, ...), custom_call_target="tpu_custom_call" | custom-call | flops 1300000014336 | tf_op jit(solution)/shard_map/wgrad/pallas_call | solution.py:52
  182.0 9.7 %all-to-all-done.3 = bf16[32,24,512]{2,1,0:T(8,128)(2,1)} async-done(((bf16[32,24,512]{2,1,0:T(8,128)(2,1)}), bf16[32,24,512]{2,1,0:T(8,128)(2,1)}, u32[]{:S(2)}, u32[]{:S(2)}) %all-to-all-start.3) | async-done | bytes 786464 | tf_op jit(solution)/shard_map/all_to_all | solution.py:352
  191.7 2.8 %collect.1 = (bf16[128,512]{1,0:T(8,128)(2,1)}, f32[8,128]{1,0:T(8,128)}, bf16[144,512]{1,0:T(8,128)(2,1)}) custom-call(s32[2]{0:T(128)} %pad_add_fusion.pos, s32[8,128]{1,0:T(8,128)} %bitcast.33, bf16[272,512]{1,0:T(8,128)(2,1)} %copy-done.6, bf16[768,512]{1,0:T(8,128)(2,1)} %bitcast.14.r, bf16[768,128]{1,0:T(8,128)(2,1)} %bitcast.23), custom_call_target="tpu_custom_call" | custom-call | flops 299999985664 | tf_op jit(solution)/shard_map/collect/pallas_call | solution.py:52
  194.5 0.5 collective-permute-start.19
  195.0 1.2 collective-permute-done.18.got
  196.2 0.7 copy-done.7
  196.9 1.7 merge.1.q
  198.6 2.1 collective-permute-start.21
  200.7 4.8 %wgrad_join.1 = (bf16[192,4096]{1,0:T(8,128)(2,1)}, bf16[192,4096]{1,0:T(8,128)(2,1)}, bf16[192,4096]{1,0:T(8,128)(2,1)}) custom-call(s32[2]{0:T(128)} %pad_add_fusion.pos, bf16[3,192,2048]{2,1,0:T(8,128)(2,1)} %get-tuple-element.71.own, bf16[3,192,2048]{2,1,0:T(8,128)(2,1)} %collective-permute-done.19.got), custom_call_target="tpu_custom_call" | custom-call | flops 499999997952 | tf_op jit(solution)/shard_map/wgrad_join/pallas_call | solution.py:52
  205.5 4.5 %collective-permute-done.22.across = bf16[272,512]{1,0:T(8,128)(2,1)} collective-permute-done((bf16[272,512]{1,0:T(8,128)(2,1)}, bf16[272,512]{1,0:T(8,128)(2,1)}, u32[]{:S(2)}, u32[]{:S(2)}) %collective-permute-start.22) | collective-permute-done | bytes 278560 | tf_op jit(solution)/shard_map/ppermute | solution.py:358
  210.0 2.0 collective-permute-done.21.right
  212.0 3.1 %collective-permute-done.20.left = bf16[272,512]{1,0:T(8,128)(2,1)} collective-permute-done((bf16[272,512]{1,0:T(8,128)(2,1)}, bf16[272,512]{1,0:T(8,128)(2,1)}, u32[]{:S(2)}, u32[]{:S(2)}) %collective-permute-start.20) | collective-permute-done | bytes 278560 | tf_op jit(solution)/shard_map/ppermute | solution.py:341
  215.1 2.3 %assemble.1 = (bf16[128,4096]{1,0:T(8,128)(2,1)}, f32[8,128]{1,0:T(8,128)}) custom-call(s32[2]{0:T(128)} %pad_add_fusion.pos, bf16[8,128]{1,0:T(8,128)(2,1)} %bitcast.37, bf16[272,512]{1,0:T(8,128)(2,1)} %merge.1.q, bf16[272,512]{1,0:T(8,128)(2,1)} %collective-permute-done.20.left, bf16[272,512]{1,0:T(8,128)(2,1)} %collective-permute-done.21.right, ...), custom_call_target="tpu_custom_call" | custom-call | flops 199999995904 | tf_op jit(solution)/shard_map/assemble/pallas_call | solution.py:52
  (27 shorter events, 0.1 us)
Async XLA Ops:
  3.6 1.8 collective-permute-start
  5.3 0.7 copy-start.6
  9.0 34.5 %all-to-all-start = ((bf16[32,24,512]{2,1,0:T(8,128)(2,1)}), bf16[32,24,512]{2,1,0:T(8,128)(2,1)}, u32[]{:S(2)}, u32[]{:S(2)}) async-start(bf16[32,24,512]{2,1,0:T(8,128)(2,1)} %bitcast.21), calls=%async_computation | async-start | bytes 1572864 | tf_op jit(solution)/shard_map/all_to_all | solution.py:352
  24.7 42.7 %collective-permute-start.5 = (bf16[3,192,2048]{2,1,0:T(8,128)(2,1)}, bf16[3,192,2048]{2,1,0:T(8,128)(2,1)}, u32[]{:S(2)}, u32[]{:S(2)}) collective-permute-start(bf16[3,192,2048]{2,1,0:T(8,128)(2,1)} %weight_send.1), channel_id=1, source_target_pairs={{0,1},{1,0},{2,3},{3,2},{4,5},{5,4},{6,7},{7,6},{8,9},{9,8},{10,11... | collective-permute-start | bytes 7077896 | tf_op jit(solution)/shard_map/ppermute | solution.py:347
  43.5 18.7 %collective-permute-start.2 = (bf16[768,512]{1,0:T(8,128)(2,1)}, bf16[768,512]{1,0:T(8,128)(2,1)S(1)}, u32[]{:S(2)}, u32[]{:S(2)}) collective-permute-start(bf16[768,512]{1,0:T(8,128)(2,1)} %bitcast.5.x0.refs_0_), channel_id=1, source_target_pairs={{0,192},{64,0},{128,64},{192,128},{1,193},{65,1},{129,65},{193,129... | collective-permute-start | bytes 2359304 | tf_op jit(solution)/shard_map/ppermute | solution.py:344
  46.5 20.1 %collective-permute-start.1 = (bf16[768,512]{1,0:T(8,128)(2,1)}, bf16[768,512]{1,0:T(8,128)(2,1)S(1)}, u32[]{:S(2)}, u32[]{:S(2)}) collective-permute-start(bf16[768,512]{1,0:T(8,128)(2,1)} %bitcast.5.x0.refs_0_), channel_id=1, source_target_pairs={{0,64},{64,128},{128,192},{192,0},{1,65},{65,129},{129,193},{193,1... | collective-permute-start | bytes 2359304 | tf_op jit(solution)/shard_map/ppermute | solution.py:341
  46.5 27.0 %all-to-all-start.1 = ((bf16[32,24,512]{2,1,0:T(8,128)(2,1)}), bf16[32,24,512]{2,1,0:T(8,128)(2,1)}, u32[]{:S(2)}, u32[]{:S(2)}) async-start(bf16[32,24,512]{2,1,0:T(8,128)(2,1)} %bitcast.19), calls=%async_computation.1 | async-start | bytes 1572864 | tf_op jit(solution)/shard_map/all_to_all | solution.py:352
  62.2 10.8 %copy-start = (bf16[768,512]{1,0:T(8,128)(2,1)}, bf16[768,512]{1,0:T(8,128)(2,1)S(1)}, u32[]{:S(2)}) copy-start(bf16[768,512]{1,0:T(8,128)(2,1)S(1)} %collective-permute-done.2.x2.refs_2_) | copy-start | bytes 2359300
  63.0 13.5 %collective-permute-start.4 = (bf16[384,512]{1,0:T(8,128)(2,1)}, bf16[384,512]{1,0:T(8,128)(2,1)}, u32[]{:S(2)}, u32[]{:S(2)}) collective-permute-start(bf16[384,512]{1,0:T(8,128)(2,1)} %slice.17), channel_id=1, source_target_pairs={{0,192},{64,0},{128,64},{192,128},{1,193},{65,1},{129,65},{193,129... | collective-permute-start | bytes 1179656 | tf_op jit(solution)/shard_map/ppermute | solution.py:344
  66.6 6.4 %copy-start.1 = (bf16[768,512]{1,0:T(8,128)(2,1)}, bf16[768,512]{1,0:T(8,128)(2,1)S(1)}, u32[]{:S(2)}) copy-start(bf16[768,512]{1,0:T(8,128)(2,1)S(1)} %collective-permute-done.1.x1.refs_1_) | copy-start | bytes 2359300
  67.4 9.8 %collective-permute-start.3 = (bf16[384,512]{1,0:T(8,128)(2,1)}, bf16[384,512]{1,0:T(8,128)(2,1)}, u32[]{:S(2)}, u32[]{:S(2)}) collective-permute-start(bf16[384,512]{1,0:T(8,128)(2,1)} %slice.16), channel_id=1, source_target_pairs={{0,64},{64,128},{128,192},{192,0},{1,65},{65,129},{129,193},{193,1... | collective-permute-start | bytes 1179656 | tf_op jit(solution)/shard_map/ppermute | solution.py:341
  73.5 17.0 %collective-permute-start.8 = (bf16[768,512]{1,0:T(8,128)(2,1)}, bf16[768,512]{1,0:T(8,128)(2,1)}, u32[]{:S(2)}, u32[]{:S(2)}) collective-permute-start(bf16[768,512]{1,0:T(8,128)(2,1)} %bitcast.10.x0.refs_5_), channel_id=1, source_target_pairs={{0,192},{64,0},{128,64},{192,128},{1,193},{65,1},{129,65},{193,129... | collective-permute-start | bytes 2359304 | tf_op jit(solution)/shard_map/ppermute | solution.py:344
  76.4 19.5 %collective-permute-start.7 = (bf16[768,512]{1,0:T(8,128)(2,1)}, bf16[768,512]{1,0:T(8,128)(2,1)}, u32[]{:S(2)}, u32[]{:S(2)}) collective-permute-start(bf16[768,512]{1,0:T(8,128)(2,1)} %bitcast.10.x0.refs_5_), channel_id=1, source_target_pairs={{0,64},{64,128},{128,192},{192,0},{1,65},{65,129},{129,193},{193,1... | collective-permute-start | bytes 2359304 | tf_op jit(solution)/shard_map/ppermute | solution.py:341
  85.2 26.4 %collective-permute-start.6 = (f32[768,768]{1,0:T(8,128)}, f32[768,768]{1,0:T(8,128)}, u32[]{:S(2)}, u32[]{:S(2)}) collective-permute-start(f32[768,768]{1,0:T(8,128)} %gate_up.1.gu_a), channel_id=1, source_target_pairs={{0,1},{1,0},{2,3},{3,2},{4,5},{5,4},{6,7},{7,6},{8,9},{9,8},{10,11... | collective-permute-start | bytes 7077896 | tf_op jit(solution)/shard_map/ppermute | solution.py:347
  92.3 11.4 %collective-permute-start.10 = (bf16[384,512]{1,0:T(8,128)(2,1)}, bf16[384,512]{1,0:T(8,128)(2,1)}, u32[]{:S(2)}, u32[]{:S(2)}) collective-permute-start(bf16[384,512]{1,0:T(8,128)(2,1)} %slice.19), channel_id=1, source_target_pairs={{0,192},{64,0},{128,64},{192,128},{1,193},{65,1},{129,65},{193,129... | collective-permute-start | bytes 1179656 | tf_op jit(solution)/shard_map/ppermute | solution.py:344
  97.8 9.3 %collective-permute-start.9 = (bf16[384,512]{1,0:T(8,128)(2,1)}, bf16[384,512]{1,0:T(8,128)(2,1)}, u32[]{:S(2)}, u32[]{:S(2)}) collective-permute-start(bf16[384,512]{1,0:T(8,128)(2,1)} %slice.18), channel_id=1, source_target_pairs={{0,64},{64,128},{128,192},{192,0},{1,65},{65,129},{129,193},{193,1... | collective-permute-start | bytes 1179656 | tf_op jit(solution)/shard_map/ppermute | solution.py:341
  111.6 3.1 %collective-permute-start.11 = (f32[768,384]{1,0:T(8,128)}, f32[768,384]{1,0:T(8,128)S(1)}, u32[]{:S(2)}, u32[]{:S(2)}) collective-permute-start(f32[768,384]{1,0:T(8,128)} %back.1.bk_a), channel_id=1, source_target_pairs={{0,1},{1,0},{2,3},{3,2},{4,5},{5,4},{6,7},{7,6},{8,9},{9,8},{10,11... | collective-permute-start | bytes 3538952 | tf_op jit(solution)/shard_map/ppermute | solution.py:347
  114.7 1.0 copy-start.3
  123.2 12.8 %collective-permute-start.14 = (bf16[384,512]{1,0:T(8,128)(2,1)}, bf16[384,512]{1,0:T(8,128)(2,1)}, u32[]{:S(2)}, u32[]{:S(2)}) collective-permute-start(bf16[384,512]{1,0:T(8,128)(2,1)} %get-tuple-element.55), channel_id=1, source_target_pairs={{0,64},{64,128},{128,192},{192,0},{1,65},{65,129},{129,193},{193,1... | collective-permute-start | bytes 1179656 | tf_op jit(solution)/shard_map/ppermute | solution.py:341
  123.2 12.8 %collective-permute-start.15 = (bf16[384,512]{1,0:T(8,128)(2,1)}, bf16[384,512]{1,0:T(8,128)(2,1)}, u32[]{:S(2)}, u32[]{:S(2)}) collective-permute-start(bf16[384,512]{1,0:T(8,128)(2,1)} %get-tuple-element.57), channel_id=1, source_target_pairs={{0,192},{64,0},{128,64},{192,128},{1,193},{65,1},{129,65},{193,129... | collective-permute-start | bytes 1179656 | tf_op jit(solution)/shard_map/ppermute | solution.py:344
  132.0 13.6 %collective-permute-start.12 = (bf16[384,512]{1,0:T(8,128)(2,1)}, bf16[384,512]{1,0:T(8,128)(2,1)}, u32[]{:S(2)}, u32[]{:S(2)}) collective-permute-start(bf16[384,512]{1,0:T(8,128)(2,1)} %get-tuple-element.49), channel_id=1, source_target_pairs={{0,64},{64,128},{128,192},{192,0},{1,65},{65,129},{129,193},{193,1... | collective-permute-start | bytes 1179656 | tf_op jit(solution)/shard_map/ppermute | solution.py:341
  132.0 30.0 %collective-permute-start.13 = (bf16[384,512]{1,0:T(8,128)(2,1)}, bf16[384,512]{1,0:T(8,128)(2,1)}, u32[]{:S(2)}, u32[]{:S(2)}) collective-permute-start(bf16[384,512]{1,0:T(8,128)(2,1)} %get-tuple-element.53), channel_id=1, source_target_pairs={{0,192},{64,0},{128,64},{192,128},{1,193},{65,1},{129,65},{193,129... | collective-permute-start | bytes 1179656 | tf_op jit(solution)/shard_map/ppermute | solution.py:344
  135.9 9.7 %copy-start.2 = (bf16[768,128]{1,0:T(8,128)(2,1)S(1)}, bf16[768,128]{1,0:T(8,128)(2,1)}, u32[]{:S(2)}) copy-start(bf16[768,128]{1,0:T(8,128)(2,1)} %get-tuple-element.51) | copy-start | bytes 589828
  138.3 23.7 %collective-permute-start.16 = (bf16[384,512]{1,0:T(8,128)(2,1)}, bf16[384,512]{1,0:T(8,128)(2,1)S(1)}, u32[]{:S(2)}, u32[]{:S(2)}) collective-permute-start(bf16[384,512]{1,0:T(8,128)(2,1)} %get-tuple-element.58), channel_id=1, source_target_pairs={{0,64},{64,128},{128,192},{192,0},{1,65},{65,129},{129,193},{193,1... | collective-permute-start | bytes 1179656 | tf_op jit(solution)/shard_map/ppermute | solution.py:341
  138.3 23.7 %collective-permute-start.17 = (bf16[384,512]{1,0:T(8,128)(2,1)}, bf16[384,512]{1,0:T(8,128)(2,1)S(1)}, u32[]{:S(2)}, u32[]{:S(2)}) collective-permute-start(bf16[384,512]{1,0:T(8,128)(2,1)} %get-tuple-element.59), channel_id=1, source_target_pairs={{0,192},{64,0},{128,64},{192,128},{1,193},{65,1},{129,65},{193,129... | collective-permute-start | bytes 1179656 | tf_op jit(solution)/shard_map/ppermute | solution.py:344
  162.0 0.7 copy-start.4
  162.8 0.8 copy-start.5
  166.3 25.3 %all-to-all-start.3 = ((bf16[32,24,512]{2,1,0:T(8,128)(2,1)}), bf16[32,24,512]{2,1,0:T(8,128)(2,1)}, u32[]{:S(2)}, u32[]{:S(2)}) async-start(bf16[32,24,512]{2,1,0:T(8,128)(2,1)} %bitcast.20), calls=%async_computation.3 | async-start | bytes 1572864 | tf_op jit(solution)/shard_map/all_to_all | solution.py:352
  194.5 1.8 collective-permute-start.18
  194.5 6.2 %collective-permute-start.19 = (bf16[3,192,2048]{2,1,0:T(8,128)(2,1)}, bf16[3,192,2048]{2,1,0:T(8,128)(2,1)}, u32[]{:S(2)}, u32[]{:S(2)}) collective-permute-start(bf16[3,192,2048]{2,1,0:T(8,128)(2,1)} %get-tuple-element.72), channel_id=1, source_target_pairs={{0,1},{1,0},{2,3},{3,2},{4,5},{5,4},{6,7},{7,6},{8,9},{9,8},{10,11... | collective-permute-start | bytes 7077896 | tf_op jit(solution)/shard_map/ppermute | solution.py:347
  196.2 0.7 copy-start.7
  198.6 11.4 %collective-permute-start.22 = (bf16[272,512]{1,0:T(8,128)(2,1)}, bf16[272,512]{1,0:T(8,128)(2,1)}, u32[]{:S(2)}, u32[]{:S(2)}) collective-permute-start(bf16[272,512]{1,0:T(8,128)(2,1)} %merge.1.q), channel_id=1, source_target_pairs={{0,128},{64,192},{128,0},{192,64},{1,129},{65,193},{129,1},{193,65... | collective-permute-start | bytes 835592 | tf_op jit(solution)/shard_map/ppermute | solution.py:358
  198.6 13.4 %collective-permute-start.21 = (bf16[272,512]{1,0:T(8,128)(2,1)}, bf16[272,512]{1,0:T(8,128)(2,1)}, u32[]{:S(2)}, u32[]{:S(2)}) collective-permute-start(bf16[272,512]{1,0:T(8,128)(2,1)} %merge.1.q), channel_id=1, source_target_pairs={{0,192},{64,0},{128,64},{192,128},{1,193},{65,1},{129,65},{193,129... | collective-permute-start | bytes 835592 | tf_op jit(solution)/shard_map/ppermute | solution.py:344
  200.7 14.4 %collective-permute-start.20 = (bf16[272,512]{1,0:T(8,128)(2,1)}, bf16[272,512]{1,0:T(8,128)(2,1)}, u32[]{:S(2)}, u32[]{:S(2)}) collective-permute-start(bf16[272,512]{1,0:T(8,128)(2,1)} %merge.1.q), channel_id=1, source_target_pairs={{0,64},{64,128},{128,192},{192,0},{1,65},{65,129},{129,193},{193,1... | collective-permute-start | bytes 835592 | tf_op jit(solution)/shard_map/ppermute | solution.py:341

commit v3 on v2

--- a/solution.py
+++ b/solution.py
@@ -44,7 +44,7 @@
 COST = {
     "pack": 2, "send": 3, "weight_send": 4, "weight_join": 6, "gate_up": 8, "back_near": 5, "back": 3,
     "mid": 8, "rest": 4, "pass_on": 2,
-    "wgrad": 13, "wgrad_join": 5, "finish": 2, "collect": 3, "merge": 2, "assemble": 2,
+    "wgrad": 13, "wgrad_join": 5, "finish": 2, "collect": 3, "assemble": 2,
 }
 
 
@@ -143,50 +143,55 @@
         out[m] = w[:, other]
 
 
-def weight_join_body(pos, gw, uw, dw, got, out):
+def weight_join_body(pos, gw, uw, dw, got, gu, down):
     h = pos[1]
-    for m, w in enumerate((gw, uw, dw)):
-        out[m, at(h * 192, 192), :] = w[:, at(h * HALF, HALF)]
-        out[m, at((1 - h) * 192, 192), :] = got[m]
-
-
-def unit_weights(w, first, count, y, off):
-    return w[first : first + count, :, chunk_cols(y, off)].reshape(count * UNITS, CH)
-
-
-def near(first, count, y, xs, w, out):
+    for m, w in enumerate((gw, uw)):
+        gu[m, at(h * 192, 192), :] = w[:, at(h * HALF, HALF)]
+        gu[m, at((1 - h) * 192, 192), :] = got[m]
+    down[at(h * 192, 192), :] = dw[:, at(h * HALF, HALF)]
+    down[at((1 - h) * 192, 192), :] = got[2]
+
+
+def unit_weights(w, y, off):
+    return w[:, :, chunk_cols(y, off)].reshape(2 * UNITS, CH)
+
+
+def gate_up_body(pos, x0, x1, x2, xa, xb, w, out):
+    y = pos[0]
+
     def block(i, carry):
         rs = at(i * 256, 256)
         acc = None
-        for x, off in zip(xs, OFFS[:3]):
-            part = mm(x[rs, :], unit_weights(w, first, count, y, off), NT)
+        for x, off in zip((x0, x1, x2), OFFS[:3]):
+            part = mm(x[rs, :], unit_weights(w, y, off), NT)
             acc = part if acc is None else acc + part
         out[rs, :] = acc
         return carry
 
     lax.fori_loop(0, 3, block, 0)
-
-
-def gate_up_body(pos, x0, x1, x2, xa, xb, w, out):
-    y = pos[0]
-    near(0, 2, y, (x0, x1, x2), w, out)
-    wc = unit_weights(w, 0, 2, y, 2)
+    wc = unit_weights(w, y, 2)
     out[:HR, :] += mm(xa[...], wc, NT)
     out[HR:, :] += mm(xb[...], wc, NT)
 
 
-def back_near_body(pos, x0, x1, x2, w, out):
-    near(2, 1, pos[0], (x0, x1, x2), w, out)
+def back_near_body(pos, *refs):
+    xs, w, out = refs[:6], refs[6], refs[7]
+    for half in range(2):
+        acc = None
+        for x, off in zip(xs[half::2], OFFS[:3]):
+            part = mm(x[...], w[:, chunk_cols(pos[0], off)], NT)
+            acc = part if acc is None else acc + part
+        out[half * HR : (half + 1) * HR, :] = acc
 
 
 def back_body(pos, acc, xa, xb, w, out):
-    wc = unit_weights(w, 2, 1, pos[0], 2)
+    wc = w[:, chunk_cols(pos[0], 2)]
     out[:HR, :] = acc[:HR, :] + mm(xa[...], wc, NT)
     out[HR:, :] = acc[HR:, :] + mm(xb[...], wc, NT)
 
 
 def input_part(both, w, y, off):
-    wc = unit_weights(w, 0, 2, y, off)
+    wc = unit_weights(w, y, off)
     return (mm(both[...], wc) * (2 * FF) ** (-0.5)).astype(BF)
 
 
@@ -246,10 +251,10 @@
     factor = 512.0 ** (-0.5)
     for i, off in enumerate(OFFS):
         if i < 3:
-            part, last = mm(lhs, xs[i][...]), mm(low, gs[i][...])
+            part = mm(lhs, xs[i][...])
         else:
             part = mm(lhs[:, :HR], xs[3][...]) + mm(lhs[:, HR:], xs[4][...])
-            last = mm(low[:, :HR], gs[3][...]) + mm(low[:, HR:], gs[4][...])
+        last = mm(low[:, :HR], gs[2 * i][...]) + mm(low[:, HR:], gs[2 * i + 1][...])
         part = (part * factor).astype(BF)
         c = lax.rem(y + (off + 4), 4) * CH
         store(0, c, part[:192])
@@ -258,7 +263,7 @@
 
 
 def wgrad_body(pos, both, hd, *refs):
-    xs, gs, (own, other, gu_t, hd_t) = refs[:5], refs[5:10], refs[10:]
+    xs, gs, (own, other, gu_t, hd_t) = refs[:5], refs[5:13], refs[13:]
     h = pos[1]
     for m in range(2):
         gu_t[m] = both[:, m * UNITS : (m + 1) * UNITS].T
@@ -284,7 +289,7 @@
     return jnp.concatenate([wide, jnp.zeros((16, CH - 128), F32)], axis=1).astype(BF)
 
 
-def collect_body(pos, ids, pk, r, cb, q, cg, sib):
+def collect_body(pos, ids, pk, r, cb, q, sib):
     h = pos[1]
     pair = (ids[...], got_ids(pk))
     key = jnp.concatenate([slot_key(i).T for i in pair], axis=0).astype(BF)
@@ -294,7 +299,7 @@
     core = core == ((iota((256, ROWS), 0) >= 128) != (h == 1))
     lhs = onehot((key == slot.astype(F32)) & core).astype(BF)
     acc = mm(lhs, r[...])
-    q[...] = acc[:128].astype(BF)
+    q[:128, :] = acc[:128].astype(BF)
     sib[:128, :] = acc[128:].astype(BF)
     tokw = mm(lhs, (cb[:, :EXPERTS].astype(F32) * rows.astype(F32)).astype(BF))
     e = iota((EXPERTS, 128), 0)
@@ -306,25 +311,20 @@
             for k in range(TOP)
         ]
         sums.append(jnp.concatenate(picked, axis=0))
-    cg[...] = sums[0]
+    q[128:, :] = hi_lo(sums[0])
     sib[128:, :] = hi_lo(sums[1])
 
 
-def merge_body(pos, q, cg, got, out):
-    out[:128, :] = q[...]
-    out[128:256, :] = got[:128, :]
-    tail = got[128:144, :128].astype(F32)
-    out[256:, :] = hi_lo(cg[...] + tail[:8] + tail[8:])
-
-
-def assemble_body(pos, comb, q, left, right, across, out, cg):
+def assemble_body(pos, comb, *refs):
+    parts, (out, cg) = refs[:8], refs[8:]
     y, h = pos[0], pos[1]
     total = jnp.zeros((16, 128), F32)
-    for off, ref in zip(OFFS, (q, left, right, across)):
+    for i, off in enumerate(OFFS):
         c = lax.rem(y + (off + 4), 4) * CH
-        out[:, at(h * HALF + c, CH)] = ref[:128, :]
-        out[:, at((1 - h) * HALF + c, CH)] = ref[128:256, :]
-        total = total + ref[256:272, :128].astype(F32)
+        a, b = parts[2 * i], parts[2 * i + 1]
+        out[:, at(h * HALF + c, CH)] = a[:128, :]
+        out[:, at((1 - h) * HALF + c, CH)] = b[:128, :]
+        total = total + a[128:144, :128].astype(F32) + b[128:144, :128].astype(F32)
     cg[...] = (total[:8] + total[8:]) / comb[...].astype(F32)
 
 
@@ -333,7 +333,6 @@
     width = lax.axis_size("expert")
     up_ring = [(i, (i + 1) % n_dp) for i in range(n_dp)]
     down_ring = [(i, (i - 1) % n_dp) for i in range(n_dp)]
-    far = [(i, (i + 2) % n_dp) for i in range(n_dp)]
     cores = [(i, i ^ 1) for i in range(width)]
     same_core = [list(range(c, width, 2)) for c in range(2)]
 
@@ -354,12 +353,13 @@
         )
         return x.reshape(ROWS, n)
 
-    def across(x):
-        return lax.ppermute(x, "dp", far)
-
     def spread(x):
         left, right = up(x), down(x)
         return x, left, right, up(left[:HR]), down(right[HR:])
+
+    def spread_halves(a, b):
+        la, rb, lb, ra = up(a), down(b), up(b), down(a)
+        return a, b, la, lb, ra, rb, up(la), down(rb)
 
     tie = lax.optimization_barrier
     pos = jnp.stack([lax.axis_index("dp"), lax.axis_index("expert") & 1]).astype(I32)
@@ -386,37 +386,37 @@
         weight_send_body, [((3, 192, HALF), BF)], (later, gw, uw, dw), name="weight_send"
     )
     wgot = swap(wsend)
-    (wall,) = call(
-        weight_join_body, [((3, UNITS, HALF), BF)], (pos, gw, uw, dw, wgot), name="weight_join"
-    )
-    xs, gs = spread(xs), spread(gs)
-    (gu_a,) = call(gate_up_body, [((ROWS, 2 * UNITS), F32)], (pos, *xs, wall), name="gate_up")
+    wgu, wd = call(
+        weight_join_body, [((2, UNITS, HALF), BF), ((UNITS, HALF), BF)],
+        (pos, gw, uw, dw, wgot), name="weight_join",
+    )
+    xs, gs = spread(xs), spread_halves(gs[:HR], gs[HR:])
+    (gu_a,) = call(gate_up_body, [((ROWS, 2 * UNITS), F32)], (pos, *xs, wgu), name="gate_up")
     gu_b = swap(gu_a)
     (bk_a,) = call(
-        back_near_body, [((ROWS, UNITS), F32)], (pos, *gs[:3], wall), name="back_near"
+        back_near_body, [((ROWS, UNITS), F32)], (pos, *gs[:6], wd), name="back_near"
     )
     (bk_a,) = call(
-        back_body, [((ROWS, UNITS), F32)], (pos, bk_a, *gs[3:], wall), name="back"
+        back_body, [((ROWS, UNITS), F32)], (pos, bk_a, *gs[6:], wd), name="back"
     )
     bk_b = swap(bk_a)
     both, hd, cb, d2a, d2b = call(
         mid_body,
         [((ROWS, 2 * UNITS), BF), ((ROWS, UNITS), BF), ((ROWS, 128), BF)]
         + [((HR, CH), BF)] * 2,
-        (pos, gu_a, gu_b, bk_a, bk_b, wall), name="mid",
+        (pos, gu_a, gu_b, bk_a, bk_b, wgu), name="mid",
     )
     r2, q2 = up(d2a), down(d2b)
     dpa, dpb, dma, dmb, d0 = call(
-        rest_body, [((HR, CH), BF)] * 4 + [((ROWS, CH), BF)], (pos, both, wall), name="rest"
+        rest_body, [((HR, CH), BF)] * 4 + [((ROWS, CH), BF)], (pos, both, wgu), name="rest"
     )
     pb, ma = up(dpb), down(dma)
     pa, mb = call(pass_on_body, [((HR, CH), BF)] * 2, (pos, dpa, r2, dmb, q2), name="pass_on")
     pa, mb = up(pa), down(mb)
     pb, cb = tie((pb, cb))
     cb = exchange(cb)
-    d0, cb = tie((d0, cb))
     (r,) = call(finish_body, [((ROWS, CH), BF)], (pos, d0, ma, pa, mb, pb), name="finish")
-    both, r = tie((both, r))
+    both, r, cb = tie((both, r, cb))
     r = exchange(r)
     w_own, w_other = call(
         wgrad_body, [((3, 192, HALF), BF)] * 2, (pos, both, hd, *xs, *gs),
@@ -425,20 +425,18 @@
     )
     r, w_other = tie((r, w_other))
     dgot = swap(w_other)
-    q, cg, sib = call(
-        collect_body, [((128, CH), BF), ((TOP, 128), F32), ((144, CH), BF)],
-        (pos, ids, pk, r, cb), name="collect",
-    )
-    got = swap(sib)
-    (q,) = call(merge_body, [((272, CH), BF)], (pos, q, cg, got), name="merge")
-    q, w_own = tie((q, w_own))
+    qa, sib = call(
+        collect_body, [((144, CH), BF)] * 2, (pos, ids, pk, r, cb), name="collect"
+    )
+    qb = swap(sib)
+    parts = spread_halves(qa, qb)
+    qb, w_own = tie((qb, w_own))
     dwg, dwu, dwd = call(
         wgrad_join_body, [((192, D), BF)] * 3, (pos, w_own, dgot), name="wgrad_join"
     )
     comb, dwg = tie((comb, dwg))
     input_grad, cg = call(
-        assemble_body, [((128, D), BF), ((TOP, 128), F32)], (pos, comb, q, up(q), down(q), across(q)),
-        name="assemble",
+        assemble_body, [((128, D), BF), ((TOP, 128), F32)], (pos, comb, *parts), name="assemble"
     )
     return (input_grad, cg.T, dwg[None], dwu[None], dwd[None])
 

time: 219 us -> 206 us (0.941)
  blocking collectives: 16.4 us -> 0 us
  starting transfers between devices: 49.3 us -> 63.1 us
  Pallas kernels: 75.4 us -> 70.5 us
  local copies, waits for them, and re-layouts: 9.08 us -> 6.28 us
    all_to_all x1 -> x0, blocking collectives: 16.4 us -> none  [exchange(): lax.all_to_all(x, 'expert', split_axis=0, concat_axis=0, axis_index_group...]
    all_to_all x3 -> x4, starting transfers between devices: 23.7 us -> 31 us  [exchange(): lax.all_to_all(x, 'expert', split_axis=0, concat_axis=0, axis_index_group...]
    all_to_all x3 -> x4, waiting for transfers between devices: 25.9 us -> 31.6 us  [exchange(): lax.all_to_all(x, 'expert', split_axis=0, concat_axis=0, axis_index_group...]
    ppermute x8 -> x11, waiting for transfers between devices: 17.4 us -> 11.9 us  [down(): return lax.ppermute(x, 'dp', down_ring)]
    pallas_call x17 -> x16, Pallas kernels: 75.4 us -> 70.5 us  [call(): pl.pallas_call(body, out_shape=[jax.ShapeDtypeStruct(s, t) for s, t in ou...]
    ppermute x1 -> x0, waiting for transfers between devices: 4.52 us -> none  [across(): return lax.ppermute(x, 'dp', far)]
    ppermute x8 -> x11, starting transfers between devices: 0.02 us -> 4.23 us  [up(): return lax.ppermute(x, 'dp', up_ring)]
    slice x4 -> x2, local copies, waits for them, and re-layouts: 5.16 us -> 1.62 us  [spread(): return (x, left, right, up(left[:HR]), down(right[HR:]))]
  transfers between devices with their start and end apart: 26 -> 32, of which waited for: 15 -> 16; matrix products, arithmetic and copies ran while one was open for 2% -> 2% of each run, Pallas kernels for 24% -> 26%
where the time goes in v3:
time: 206 us
  Pallas kernels  70.5 us (34%)
  waiting for transfers between devices  64.2 us (31%)
  starting transfers between devices  63.1 us (31%)
  local copies, waits for them, and re-layouts  6.28 us (3%)
    pallas_call x16, Pallas kernels, call(): pl.pallas_call(body, out_shape=[jax.ShapeDtypeStruct(s, t) for s, t in ou...  70.5 us
    all_to_all x4, waiting for transfers between devices, exchange(): lax.all_to_all(x, 'expert', split_axis=0, concat_axis=0, axis_index_group...  31.6 us
    all_to_all x4, starting transfers between devices, exchange(): lax.all_to_all(x, 'expert', split_axis=0, concat_axis=0, axis_index_group...  31 us
    ppermute x11, starting transfers between devices, down(): return lax.ppermute(x, 'dp', down_ring)  27.4 us
    ppermute x11, waiting for transfers between devices, up(): return lax.ppermute(x, 'dp', up_ring)  14.1 us
    ppermute x11, waiting for transfers between devices, down(): return lax.ppermute(x, 'dp', down_ring)  11.9 us
    ppermute x6, waiting for transfers between devices, swap(): return lax.ppermute(x, 'expert', cores)  6.58 us
    ppermute x11, starting transfers between devices, up(): return lax.ppermute(x, 'dp', up_ring)  4.23 us
  transfers between devices with their start and end apart: 32, of which 16 were waited for; matrix products, arithmetic and copies ran while one was open for 2% of the time, Pallas kernels for 26%

profile of v3, /device:TPU:2, one launch (start us, length us, event | category | flops | bytes accessed | tf_op | source)
XLA Modules:
  0.0 205.5 jit_solution(3735050314364055415)
XLA Ops:
  0.6 0.7 pad_add_fusion.pos
  1.3 2.3 %pack.1 = bf16[272,512]{1,0:T(8,128)(2,1)} custom-call(s32[2]{0:T(128)} %pad_add_fusion.pos, s32[8,128]{1,0:T(8,128)} %bitcast.29, bf16[8,128]{1,0:T(8,128)(2,1)} %bitcast.33, bf16[128,4096]{1,0:T(8,128)(2,1)} %rows_ref.3, bf16[128,4096]{1,0:T(8,128)(2,1)} %rows_ref.2), custom_call_target="tpu_custom_call" | custom-call | flops 199999995904 | tf_op jit(solution)/shard_map/pack/pallas_call | solution.py:52
  3.6 0.0 collective-permute-start
  3.6 1.8 collective-permute-done.pk
  5.4 0.7 copy-done.5
  6.1 3.0 %send.3 = bf16[768,512]{1,0:T(8,128)(2,1)} custom-call(s32[2]{0:T(128)} %pad_add_fusion.pos, s32[8,128]{1,0:T(8,128)} %bitcast.30, bf16[8,128]{1,0:T(8,128)(2,1)} %bitcast.34, bf16[272,512]{1,0:T(8,128)(2,1)} %copy-done.5, bf16[128,4096]{1,0:T(8,128)(2,1)} %rows_ref.3), custom_call_target="tpu_custom_call" | custom-call | flops 299999985664 | tf_op jit(solution)/shard_map/send/pallas_call | solution.py:52
  9.1 11.7 %all-to-all-start = ((bf16[32,24,512]{2,1,0:T(8,128)(2,1)}), bf16[32,24,512]{2,1,0:T(8,128)(2,1)}, u32[]{:S(2)}, u32[]{:S(2)}) async-start(bf16[32,24,512]{2,1,0:T(8,128)(2,1)} %bitcast.22), calls=%async_computation | async-start | bytes 1572864 | tf_op jit(solution)/shard_map/all_to_all | solution.py:351
  20.8 3.9 %weight_send.1 = bf16[3,192,2048]{2,1,0:T(8,128)(2,1)} custom-call(s32[2]{0:T(128)} %pad_add_fusion.pos, bf16[192,4096]{1,0:T(8,128)(2,1)} %bitcast.23, bf16[192,4096]{1,0:T(8,128)(2,1)} %bitcast.25, bf16[192,4096]{1,0:T(8,128)(2,1)} %bitcast.27), custom_call_target="tpu_custom_call" | custom-call | flops 399999991808 | tf_op jit(solution)/shard_map/weight_send/pallas_call | solution.py:52
  24.7 0.0 collective-permute-start.5
  24.7 3.2 %send.2 = bf16[768,512]{1,0:T(8,128)(2,1)} custom-call(s32[2]{0:T(128)} %pad_add_fusion.pos, s32[8,128]{1,0:T(8,128)} %bitcast.31, bf16[8,128]{1,0:T(8,128)(2,1)} %bitcast.35, bf16[272,512]{1,0:T(8,128)(2,1)} %copy-done.5, bf16[128,4096]{1,0:T(8,128)(2,1)} %rows_ref.2), custom_call_target="tpu_custom_call" | custom-call | flops 299999985664 | tf_op jit(solution)/shard_map/send/pallas_call | solution.py:52
  27.9 15.7 %all-to-all-done = bf16[32,24,512]{2,1,0:T(8,128)(2,1)} async-done(((bf16[32,24,512]{2,1,0:T(8,128)(2,1)}), bf16[32,24,512]{2,1,0:T(8,128)(2,1)}, u32[]{:S(2)}, u32[]{:S(2)}) %all-to-all-start) | async-done | bytes 786464 | tf_op jit(solution)/shard_map/all_to_all | solution.py:351
  43.6 3.0 %collective-permute-start.2 = (bf16[768,512]{1,0:T(8,128)(2,1)}, bf16[768,512]{1,0:T(8,128)(2,1)S(1)}, u32[]{:S(2)}, u32[]{:S(2)}) collective-permute-start(bf16[768,512]{1,0:T(8,128)(2,1)} %bitcast.5.x0.refs_0_), channel_id=1, source_target_pairs={{0,192},{64,0},{128,64},{192,128},{1,193},{65,1},{129,65},{193,129... | collective-permute-start | bytes 2359304 | tf_op jit(solution)/shard_map/ppermute | solution.py:343
  46.6 0.0 collective-permute-start.1
  46.6 5.6 %all-to-all-start.1 = ((bf16[32,24,512]{2,1,0:T(8,128)(2,1)}), bf16[32,24,512]{2,1,0:T(8,128)(2,1)}, u32[]{:S(2)}, u32[]{:S(2)}) async-start(bf16[32,24,512]{2,1,0:T(8,128)(2,1)} %bitcast.20), calls=%async_computation.1 | async-start | bytes 1572864 | tf_op jit(solution)/shard_map/all_to_all | solution.py:351
  52.2 10.0 %collective-permute-done.2.x2.refs_2_ = bf16[768,512]{1,0:T(8,128)(2,1)S(1)} collective-permute-done((bf16[768,512]{1,0:T(8,128)(2,1)}, bf16[768,512]{1,0:T(8,128)(2,1)S(1)}, u32[]{:S(2)}, u32[]{:S(2)}) %collective-permute-start.2) | collective-permute-done | bytes 786464 | tf_op jit(solution)/shard_map/ppermute | solution.py:343
  62.2 0.8 slice.25
  63.0 3.6 %collective-permute-start.4 = (bf16[384,512]{1,0:T(8,128)(2,1)}, bf16[384,512]{1,0:T(8,128)(2,1)}, u32[]{:S(2)}, u32[]{:S(2)}) collective-permute-start(bf16[384,512]{1,0:T(8,128)(2,1)} %slice.25), channel_id=1, source_target_pairs={{0,192},{64,0},{128,64},{192,128},{1,193},{65,1},{129,65},{193,129... | collective-permute-start | bytes 1179656 | tf_op jit(solution)/shard_map/ppermute | solution.py:343
  66.6 0.8 slice.24
  67.4 0.0 collective-permute-start.3
  67.4 5.6 %weight_join.1 = (bf16[2,384,2048]{2,1,0:T(8,128)(2,1)}, bf16[384,2048]{1,0:T(8,128)(2,1)}) custom-call(s32[2]{0:T(128)} %pad_add_fusion.pos, bf16[192,4096]{1,0:T(8,128)(2,1)} %bitcast.24, bf16[192,4096]{1,0:T(8,128)(2,1)} %bitcast.26, bf16[192,4096]{1,0:T(8,128)(2,1)} %bitcast.28, bf16[3,192,2048]{2,1,0:T(8,128)(2,1)} %collective-permute-done.5.got), custom_call_target="tpu_custom_call" | custom-call | flops 599999971328 | tf_op jit(solution)/shard_map/weight_join/pallas_call | solution.py:52
  72.9 0.6 all-to-all-done.1
  73.6 2.1 fusion
  75.6 3.0 %collective-permute-start.9 = (bf16[384,512]{1,0:T(8,128)(2,1)}, bf16[384,512]{1,0:T(8,128)(2,1)}, u32[]{:S(2)}, u32[]{:S(2)}) collective-permute-start(bf16[384,512]{1,0:T(8,128)(2,1)} %bitcast.10.refs_0_.refs_5_), channel_id=1, source_target_pairs={{0,192},{64,0},{128,64},{192,128},{1,193},{65,1},{129,65},{193,129... | collective-permute-start | bytes 1179656 | tf_op jit(solution)/shard_map/ppermute | solution.py:343
  78.6 3.2 %collective-permute-start.10 = (bf16[384,512]{1,0:T(8,128)(2,1)}, bf16[384,512]{1,0:T(8,128)(2,1)}, u32[]{:S(2)}, u32[]{:S(2)}) collective-permute-start(bf16[384,512]{1,0:T(8,128)(2,1)} %bitcast.11.refs_1_.refs_6_), channel_id=1, source_target_pairs={{0,192},{64,0},{128,64},{192,128},{1,193},{65,1},{129,65},{193,129... | collective-permute-start | bytes 1179656 | tf_op jit(solution)/shard_map/ppermute | solution.py:343
  81.8 7.5 %gate_up.1.gu_a = f32[768,768]{1,0:T(8,128)} custom-call(s32[2]{0:T(128)} %pad_add_fusion.pos, bf16[768,512]{1,0:T(8,128)(2,1)} %bitcast.5.x0.refs_0_, bf16[768,512]{1,0:T(8,128)(2,1)} %copy-done.1, bf16[768,512]{1,0:T(8,128)(2,1)} %copy-done, bf16[384,512]{1,0:T(8,128)(2,1)} %collective-permute-done.3.xa.refs_3_, ...), custom_call_target="tpu_custom_call" | custom-call | flops 799999983616 | tf_op jit(solution)/shard_map/gate_up/pallas_call | solution.py:52
  89.3 0.0 collective-permute-start.6
  89.3 2.5 %collective-permute-done.7.refs_2_.refs_7_ = bf16[384,512]{1,0:T(8,128)(2,1)} collective-permute-done((bf16[384,512]{1,0:T(8,128)(2,1)}, bf16[384,512]{1,0:T(8,128)(2,1)}, u32[]{:S(2)}, u32[]{:S(2)}) %collective-permute-start.7) | collective-permute-done | bytes 393248 | tf_op jit(solution)/shard_map/ppermute | solution.py:340
  91.8 0.8 collective-permute-done.10.refs_5_.refs_10_
  92.6 3.7 %collective-permute-start.12 = (bf16[384,512]{1,0:T(8,128)(2,1)}, bf16[384,512]{1,0:T(8,128)(2,1)}, u32[]{:S(2)}, u32[]{:S(2)}) collective-permute-start(bf16[384,512]{1,0:T(8,128)(2,1)} %collective-permute-done.10.refs_5_.refs_10_), channel_id=1, source_target_pairs={{0,192},{64,0},{128,64},{192,128},{1,193},{65,1},{129,65},{193,129... | collective-permute-start | bytes 1179656 | tf_op jit(solution)/shard_map/ppermute | solution.py:343
  96.3 1.4 collective-permute-done.8.refs_3_.refs_8_
  97.7 4.6 %back_near.1.acc = f32[768,384]{1,0:T(8,128)} custom-call(s32[2]{0:T(128)} %pad_add_fusion.pos, bf16[384,512]{1,0:T(8,128)(2,1)} %bitcast.10.refs_0_.refs_5_, bf16[384,512]{1,0:T(8,128)(2,1)} %bitcast.11.refs_1_.refs_6_, bf16[384,512]{1,0:T(8,128)(2,1)} %collective-permute-done.7.refs_2_.refs_7_, bf16[384,512]{1,0:T(8,128)(2,1)} %collective-permute-done.8.refs_3_.refs_8_, ...), custom_call_target="tpu_custom_call" | custom-call | flops 499999997952 | tf_op jit(solution)/shard_map/back_near/pallas_call | solution.py:52
  102.3 2.2 %collective-permute-done.11.xa.refs_11_ = bf16[384,512]{1,0:T(8,128)(2,1)} collective-permute-done((bf16[384,512]{1,0:T(8,128)(2,1)}, bf16[384,512]{1,0:T(8,128)(2,1)}, u32[]{:S(2)}, u32[]{:S(2)}) %collective-permute-start.11) | collective-permute-done | bytes 393248 | tf_op jit(solution)/shard_map/ppermute | solution.py:340
  104.4 3.6 %back.1.bk_a = f32[768,384]{1,0:T(8,128)} custom-call(s32[2]{0:T(128)} %pad_add_fusion.pos, f32[768,384]{1,0:T(8,128)} %back_near.1.acc, bf16[384,512]{1,0:T(8,128)(2,1)} %collective-permute-done.11.xa.refs_11_, bf16[384,512]{1,0:T(8,128)(2,1)} %collective-permute-done.12.xb.refs_12_, bf16[384,2048]{1,0:T(8,128)(2,1)} %get-tuple-element.47.refs_6_.w), custom_call_target="tpu_custom_call" | custom-call | flops 299999985664 | tf_op jit(solution)/shard_map/back/pallas_call | solution.py:52
  108.1 3.1 %collective-permute-done.13.bk_b = f32[768,384]{1,0:T(8,128)S(1)} collective-permute-done((f32[768,384]{1,0:T(8,128)}, f32[768,384]{1,0:T(8,128)S(1)}, u32[]{:S(2)}, u32[]{:S(2)}) %collective-permute-start.13) | collective-permute-done | bytes 1179680 | tf_op jit(solution)/shard_map/ppermute | solution.py:346
  111.1 1.0 copy-done.2
  112.1 7.0 %mid.1 = (bf16[768,768]{1,0:T(8,128)(2,1)}, bf16[768,384]{1,0:T(8,128)(2,1)}, bf16[768,128]{1,0:T(8,128)(2,1)}, bf16[384,512]{1,0:T(8,128)(2,1)}, bf16[384,512]{1,0:T(8,128)(2,1)}) custom-call(s32[2]{0:T(128)} %pad_add_fusion.pos, f32[768,768]{1,0:T(8,128)} %gate_up.1.gu_a, f32[768,768]{1,0:T(8,128)} %collective-permute-done.6.gu_b, f32[768,384]{1,0:T(8,128)} %back.1.bk_a, ...), custom_call_target="tpu_custom_call" | custom-call | flops 799999983616 | tf_op jit(solution)/shard_map/mid/pallas_call | solution.py:52
  119.2 3.2 %collective-permute-start.16 = (bf16[384,512]{1,0:T(8,128)(2,1)}, bf16[384,512]{1,0:T(8,128)(2,1)}, u32[]{:S(2)}, u32[]{:S(2)}) collective-permute-start(bf16[384,512]{1,0:T(8,128)(2,1)} %get-tuple-element.54), channel_id=1, source_target_pairs={{0,192},{64,0},{128,64},{192,128},{1,193},{65,1},{129,65},{193,129... | collective-permute-start | bytes 1179656 | tf_op jit(solution)/shard_map/ppermute | solution.py:343
  122.4 5.2 %rest.1 = (bf16[384,512]{1,0:T(8,128)(2,1)}, bf16[384,512]{1,0:T(8,128)(2,1)}, bf16[384,512]{1,0:T(8,128)(2,1)}, bf16[384,512]{1,0:T(8,128)(2,1)}, bf16[768,512]{1,0:T(8,128)(2,1)}) custom-call(s32[2]{0:T(128)} %pad_add_fusion.pos, bf16[768,768]{1,0:T(8,128)(2,1)} %get-tuple-element.62.both, bf16[2,384,2048]{2,1,0:T(8,128)(2,1)} %get-tuple-element.45.w), custom_call_target="tpu_custom_call" | custom-call | flops 399999991808 | tf_op jit(solution)/shard_map/rest/pallas_call | solution.py:52
  127.6 0.1 collective-permute-start.14
  127.6 2.0 collective-permute-start.19
  129.6 2.8 %collective-permute-done.15.r2 = bf16[384,512]{1,0:T(8,128)(2,1)} collective-permute-done((bf16[384,512]{1,0:T(8,128)(2,1)}, bf16[384,512]{1,0:T(8,128)(2,1)}, u32[]{:S(2)}, u32[]{:S(2)}) %collective-permute-start.15) | collective-permute-done | bytes 393248 | tf_op jit(solution)/shard_map/ppermute | solution.py:340
  132.4 2.4 %pass_on.1 = (bf16[384,512]{1,0:T(8,128)(2,1)}, bf16[384,512]{1,0:T(8,128)(2,1)}) custom-call(s32[2]{0:T(128)} %pad_add_fusion.pos, bf16[384,512]{1,0:T(8,128)(2,1)} %get-tuple-element.51.dpa, bf16[384,512]{1,0:T(8,128)(2,1)} %collective-permute-done.15.r2, bf16[384,512]{1,0:T(8,128)(2,1)} %get-tuple-element.53.dmb, bf16[384,512]{1,0:T(8,128)(2,1)} %collective-permute-done.16.q2), custom_call_target="tpu_custom_call" | custom-call | flops 199999995904 | tf_op jit(solution)/shard_map/pass_on/pallas_call | solution.py:52
  134.7 0.3 collective-permute-start.17
  135.0 3.3 %collective-permute-start.18 = (bf16[384,512]{1,0:T(8,128)(2,1)}, bf16[384,512]{1,0:T(8,128)(2,1)S(1)}, u32[]{:S(2)}, u32[]{:S(2)}) collective-permute-start(bf16[384,512]{1,0:T(8,128)(2,1)} %get-tuple-element.56), channel_id=1, source_target_pairs={{0,192},{64,0},{128,64},{192,128},{1,193},{65,1},{129,65},{193,129... | collective-permute-start | bytes 1179656 | tf_op jit(solution)/shard_map/ppermute | solution.py:343
  138.3 2.9 %collective-permute-done.19.pb = bf16[384,512]{1,0:T(8,128)(2,1)} collective-permute-done((bf16[384,512]{1,0:T(8,128)(2,1)}, bf16[384,512]{1,0:T(8,128)(2,1)}, u32[]{:S(2)}, u32[]{:S(2)}) %collective-permute-start.19) | collective-permute-done | bytes 393248 | tf_op jit(solution)/shard_map/ppermute | solution.py:340
  141.2 7.5 %all-to-all-start.2 = ((bf16[32,24,128]{2,1,0:T(8,128)(2,1)}), bf16[32,24,128]{2,1,0:T(8,128)(2,1)}, u32[]{:S(2)}, u32[]{:S(2)}) async-start(bf16[32,24,128]{2,1,0:T(8,128)(2,1)} %bitcast.12), calls=%async_computation.2 | async-start | bytes 393216 | tf_op jit(solution)/shard_map/all_to_all | solution.py:351
  148.7 0.7 copy-done.3
  149.5 0.1 copy-done.4
  149.6 2.8 %finish.1 = bf16[768,512]{1,0:T(8,128)(2,1)} custom-call(s32[2]{0:T(128)} %pad_add_fusion.pos, bf16[768,512]{1,0:T(8,128)(2,1)} %get-tuple-element.49.d0, bf16[384,512]{1,0:T(8,128)(2,1)} %collective-permute-done.14.ma, bf16[384,512]{1,0:T(8,128)(2,1)} %copy-done.3, bf16[384,512]{1,0:T(8,128)(2,1)} %copy-done.4, bf16[384,512]{1,0:T(8,128)(2,1)} %collective-permute-done.19.pb), custom_call_target="tpu_custom_call" | custom-call | flops 199999995904 | tf_op jit(solution)/shard_map/finish/pallas_call | solution.py:52
  152.4 5.6 %all-to-all-done.2 = bf16[32,24,128]{2,1,0:T(8,128)(2,1)} async-done(((bf16[32,24,128]{2,1,0:T(8,128)(2,1)}), bf16[32,24,128]{2,1,0:T(8,128)(2,1)}, u32[]{:S(2)}, u32[]{:S(2)}) %all-to-all-start.2) | async-done | bytes 196640 | tf_op jit(solution)/shard_map/all_to_all | solution.py:351
  158.0 6.3 %all-to-all-start.3 = ((bf16[32,24,512]{2,1,0:T(8,128)(2,1)}), bf16[32,24,512]{2,1,0:T(8,128)(2,1)}, u32[]{:S(2)}, u32[]{:S(2)}) async-start(bf16[32,24,512]{2,1,0:T(8,128)(2,1)} %bitcast.21), calls=%async_computation.3 | async-start | bytes 1572864 | tf_op jit(solution)/shard_map/all_to_all | solution.py:351
  164.2 9.5 %wgrad.1 = (bf16[3,192,2048]{2,1,0:T(8,128)(2,1)}, bf16[3,192,2048]{2,1,0:T(8,128)(2,1)}) custom-call(s32[2]{0:T(128)} %pad_add_fusion.pos, bf16[768,768]{1,0:T(8,128)(2,1)} %get-tuple-element.62.both, bf16[768,384]{1,0:T(8,128)(2,1)} %get-tuple-element.63.hd, bf16[768,512]{1,0:T(8,128)(2,1)} %bitcast.5.x0.refs_0_, bf16[768,512]{1,0:T(8,128)(2,1)} %copy-done.1, ...), custom_call_target="tpu_custom_call" | custom-call | flops 1300000014336 | tf_op jit(solution)/shard_map/wgrad/pallas_call | solution.py:52
  173.7 9.7 %all-to-all-done.3 = bf16[32,24,512]{2,1,0:T(8,128)(2,1)} async-done(((bf16[32,24,512]{2,1,0:T(8,128)(2,1)}), bf16[32,24,512]{2,1,0:T(8,128)(2,1)}, u32[]{:S(2)}, u32[]{:S(2)}) %all-to-all-start.3) | async-done | bytes 786464 | tf_op jit(solution)/shard_map/all_to_all | solution.py:351
  183.5 2.8 %collect.1 = (bf16[144,512]{1,0:T(8,128)(2,1)}, bf16[144,512]{1,0:T(8,128)(2,1)}) custom-call(s32[2]{0:T(128)} %pad_add_fusion.pos, s32[8,128]{1,0:T(8,128)} %bitcast.32, bf16[272,512]{1,0:T(8,128)(2,1)} %copy-done.5, bf16[768,512]{1,0:T(8,128)(2,1)} %bitcast.15.r, bf16[768,128]{1,0:T(8,128)(2,1)} %bitcast.13.cb), custom_call_target="tpu_custom_call" | custom-call | flops 299999985664 | tf_op jit(solution)/shard_map/collect/pallas_call | solution.py:52
  186.3 0.5 collective-permute-start.20
  186.8 1.8 collective-permute-done.20.refs_1_
  188.5 1.5 collective-permute-start.25
  190.0 0.0 collective-permute-start.24
  190.1 2.0 collective-permute-start.23
  192.1 2.4 %collective-permute-done.22.refs_2_ = bf16[144,512]{1,0:T(8,128)(2,1)} collective-permute-done((bf16[144,512]{1,0:T(8,128)(2,1)}, bf16[144,512]{1,0:T(8,128)(2,1)}, u32[]{:S(2)}, u32[]{:S(2)}) %collective-permute-start.22) | collective-permute-done | bytes 147488 | tf_op jit(solution)/shard_map/ppermute | solution.py:340
  194.5 1.1 collective-permute-done.25.refs_5_
  195.6 2.8 %collective-permute-start.27 = (bf16[144,512]{1,0:T(8,128)(2,1)}, bf16[144,512]{1,0:T(8,128)(2,1)}, u32[]{:S(2)}, u32[]{:S(2)}) collective-permute-start(bf16[144,512]{1,0:T(8,128)(2,1)} %collective-permute-done.25.refs_5_), channel_id=1, source_target_pairs={{0,192},{64,0},{128,64},{192,128},{1,193},{65,1},{129,65},{193,129... | collective-permute-start | bytes 442376 | tf_op jit(solution)/shard_map/ppermute | solution.py:343
  198.3 4.8 %wgrad_join.1 = (bf16[192,4096]{1,0:T(8,128)(2,1)}, bf16[192,4096]{1,0:T(8,128)(2,1)}, bf16[192,4096]{1,0:T(8,128)(2,1)}) custom-call(s32[2]{0:T(128)} %pad_add_fusion.pos, bf16[3,192,2048]{2,1,0:T(8,128)(2,1)} %get-tuple-element.69.own, bf16[3,192,2048]{2,1,0:T(8,128)(2,1)} %collective-permute-done.21.got), custom_call_target="tpu_custom_call" | custom-call | flops 499999997952 | tf_op jit(solution)/shard_map/wgrad_join/pallas_call | solution.py:52
  203.1 2.4 %assemble.1 = (bf16[128,4096]{1,0:T(8,128)(2,1)}, f32[8,128]{1,0:T(8,128)}) custom-call(s32[2]{0:T(128)} %pad_add_fusion.pos, bf16[8,128]{1,0:T(8,128)(2,1)} %bitcast.36, bf16[144,512]{1,0:T(8,128)(2,1)} %get-tuple-element.73.refs_0_, bf16[144,512]{1,0:T(8,128)(2,1)} %collective-permute-done.20.refs_1_, bf16[144,512]{1,0:T(8,128)(2,1)} %collective-permute-done.22.refs_2_, ...), custom_call_target="tpu_custom_call" | custom-call | flops 199999995904 | tf_op jit(solution)/shard_map/assemble/pallas_call | solution.py:52
  (32 shorter events, 0.1 us)
Async XLA Ops:
  3.6 1.8 collective-permute-start
  5.4 0.7 copy-start.5
  9.1 34.5 %all-to-all-start = ((bf16[32,24,512]{2,1,0:T(8,128)(2,1)}), bf16[32,24,512]{2,1,0:T(8,128)(2,1)}, u32[]{:S(2)}, u32[]{:S(2)}) async-start(bf16[32,24,512]{2,1,0:T(8,128)(2,1)} %bitcast.22), calls=%async_computation | async-start | bytes 1572864 | tf_op jit(solution)/shard_map/all_to_all | solution.py:351
  24.7 42.7 %collective-permute-start.5 = (bf16[3,192,2048]{2,1,0:T(8,128)(2,1)}, bf16[3,192,2048]{2,1,0:T(8,128)(2,1)}, u32[]{:S(2)}, u32[]{:S(2)}) collective-permute-start(bf16[3,192,2048]{2,1,0:T(8,128)(2,1)} %weight_send.1), channel_id=1, source_target_pairs={{0,1},{1,0},{2,3},{3,2},{4,5},{5,4},{6,7},{7,6},{8,9},{9,8},{10,11... | collective-permute-start | bytes 7077896 | tf_op jit(solution)/shard_map/ppermute | solution.py:346
  43.6 18.6 %collective-permute-start.2 = (bf16[768,512]{1,0:T(8,128)(2,1)}, bf16[768,512]{1,0:T(8,128)(2,1)S(1)}, u32[]{:S(2)}, u32[]{:S(2)}) collective-permute-start(bf16[768,512]{1,0:T(8,128)(2,1)} %bitcast.5.x0.refs_0_), channel_id=1, source_target_pairs={{0,192},{64,0},{128,64},{192,128},{1,193},{65,1},{129,65},{193,129... | collective-permute-start | bytes 2359304 | tf_op jit(solution)/shard_map/ppermute | solution.py:343
  46.6 20.0 %collective-permute-start.1 = (bf16[768,512]{1,0:T(8,128)(2,1)}, bf16[768,512]{1,0:T(8,128)(2,1)S(1)}, u32[]{:S(2)}, u32[]{:S(2)}) collective-permute-start(bf16[768,512]{1,0:T(8,128)(2,1)} %bitcast.5.x0.refs_0_), channel_id=1, source_target_pairs={{0,64},{64,128},{128,192},{192,0},{1,65},{65,129},{129,193},{193,1... | collective-permute-start | bytes 2359304 | tf_op jit(solution)/shard_map/ppermute | solution.py:340
  46.6 27.0 %all-to-all-start.1 = ((bf16[32,24,512]{2,1,0:T(8,128)(2,1)}), bf16[32,24,512]{2,1,0:T(8,128)(2,1)}, u32[]{:S(2)}, u32[]{:S(2)}) async-start(bf16[32,24,512]{2,1,0:T(8,128)(2,1)} %bitcast.20), calls=%async_computation.1 | async-start | bytes 1572864 | tf_op jit(solution)/shard_map/all_to_all | solution.py:351
  62.2 10.8 %copy-start = (bf16[768,512]{1,0:T(8,128)(2,1)}, bf16[768,512]{1,0:T(8,128)(2,1)S(1)}, u32[]{:S(2)}) copy-start(bf16[768,512]{1,0:T(8,128)(2,1)S(1)} %collective-permute-done.2.x2.refs_2_) | copy-start | bytes 2359300
  63.0 18.8 %collective-permute-start.4 = (bf16[384,512]{1,0:T(8,128)(2,1)}, bf16[384,512]{1,0:T(8,128)(2,1)}, u32[]{:S(2)}, u32[]{:S(2)}) collective-permute-start(bf16[384,512]{1,0:T(8,128)(2,1)} %slice.25), channel_id=1, source_target_pairs={{0,192},{64,0},{128,64},{192,128},{1,193},{65,1},{129,65},{193,129... | collective-permute-start | bytes 1179656 | tf_op jit(solution)/shard_map/ppermute | solution.py:343
  66.6 6.4 %copy-start.1 = (bf16[768,512]{1,0:T(8,128)(2,1)}, bf16[768,512]{1,0:T(8,128)(2,1)S(1)}, u32[]{:S(2)}) copy-start(bf16[768,512]{1,0:T(8,128)(2,1)S(1)} %collective-permute-done.1.x1.refs_1_) | copy-start | bytes 2359300
  67.4 14.4 %collective-permute-start.3 = (bf16[384,512]{1,0:T(8,128)(2,1)}, bf16[384,512]{1,0:T(8,128)(2,1)}, u32[]{:S(2)}, u32[]{:S(2)}) collective-permute-start(bf16[384,512]{1,0:T(8,128)(2,1)} %slice.24), channel_id=1, source_target_pairs={{0,64},{64,128},{128,192},{192,0},{1,65},{65,129},{129,193},{193,1... | collective-permute-start | bytes 1179656 | tf_op jit(solution)/shard_map/ppermute | solution.py:340
  75.6 20.7 %collective-permute-start.9 = (bf16[384,512]{1,0:T(8,128)(2,1)}, bf16[384,512]{1,0:T(8,128)(2,1)}, u32[]{:S(2)}, u32[]{:S(2)}) collective-permute-start(bf16[384,512]{1,0:T(8,128)(2,1)} %bitcast.10.refs_0_.refs_5_), channel_id=1, source_target_pairs={{0,192},{64,0},{128,64},{192,128},{1,193},{65,1},{129,65},{193,129... | collective-permute-start | bytes 1179656 | tf_op jit(solution)/shard_map/ppermute | solution.py:343
  78.6 13.2 %collective-permute-start.7 = (bf16[384,512]{1,0:T(8,128)(2,1)}, bf16[384,512]{1,0:T(8,128)(2,1)}, u32[]{:S(2)}, u32[]{:S(2)}) collective-permute-start(bf16[384,512]{1,0:T(8,128)(2,1)} %bitcast.10.refs_0_.refs_5_), channel_id=1, source_target_pairs={{0,64},{64,128},{128,192},{192,0},{1,65},{65,129},{129,193},{193,1... | collective-permute-start | bytes 1179656 | tf_op jit(solution)/shard_map/ppermute | solution.py:340
  78.6 14.0 %collective-permute-start.10 = (bf16[384,512]{1,0:T(8,128)(2,1)}, bf16[384,512]{1,0:T(8,128)(2,1)}, u32[]{:S(2)}, u32[]{:S(2)}) collective-permute-start(bf16[384,512]{1,0:T(8,128)(2,1)} %bitcast.11.refs_1_.refs_6_), channel_id=1, source_target_pairs={{0,192},{64,0},{128,64},{192,128},{1,193},{65,1},{129,65},{193,129... | collective-permute-start | bytes 1179656 | tf_op jit(solution)/shard_map/ppermute | solution.py:343
  81.8 15.9 %collective-permute-start.8 = (bf16[384,512]{1,0:T(8,128)(2,1)}, bf16[384,512]{1,0:T(8,128)(2,1)}, u32[]{:S(2)}, u32[]{:S(2)}) collective-permute-start(bf16[384,512]{1,0:T(8,128)(2,1)} %bitcast.11.refs_1_.refs_6_), channel_id=1, source_target_pairs={{0,64},{64,128},{128,192},{192,0},{1,65},{65,129},{129,193},{193,1... | collective-permute-start | bytes 1179656 | tf_op jit(solution)/shard_map/ppermute | solution.py:340
  89.3 21.8 %collective-permute-start.6 = (f32[768,768]{1,0:T(8,128)}, f32[768,768]{1,0:T(8,128)}, u32[]{:S(2)}, u32[]{:S(2)}) collective-permute-start(f32[768,768]{1,0:T(8,128)} %gate_up.1.gu_a), channel_id=1, source_target_pairs={{0,1},{1,0},{2,3},{3,2},{4,5},{5,4},{6,7},{7,6},{8,9},{9,8},{10,11... | collective-permute-start | bytes 7077896 | tf_op jit(solution)/shard_map/ppermute | solution.py:346
  91.8 12.6 %collective-permute-start.11 = (bf16[384,512]{1,0:T(8,128)(2,1)}, bf16[384,512]{1,0:T(8,128)(2,1)}, u32[]{:S(2)}, u32[]{:S(2)}) collective-permute-start(bf16[384,512]{1,0:T(8,128)(2,1)} %collective-permute-done.7.refs_2_.refs_7_), channel_id=1, source_target_pairs={{0,64},{64,128},{128,192},{192,0},{1,65},{65,129},{129,193},{193,1... | collective-permute-start | bytes 1179656 | tf_op jit(solution)/shard_map/ppermute | solution.py:340
  92.6 11.8 %collective-permute-start.12 = (bf16[384,512]{1,0:T(8,128)(2,1)}, bf16[384,512]{1,0:T(8,128)(2,1)}, u32[]{:S(2)}, u32[]{:S(2)}) collective-permute-start(bf16[384,512]{1,0:T(8,128)(2,1)} %collective-permute-done.10.refs_5_.refs_10_), channel_id=1, source_target_pairs={{0,192},{64,0},{128,64},{192,128},{1,193},{65,1},{129,65},{193,129... | collective-permute-start | bytes 1179656 | tf_op jit(solution)/shard_map/ppermute | solution.py:343
  108.1 3.1 %collective-permute-start.13 = (f32[768,384]{1,0:T(8,128)}, f32[768,384]{1,0:T(8,128)S(1)}, u32[]{:S(2)}, u32[]{:S(2)}) collective-permute-start(f32[768,384]{1,0:T(8,128)} %back.1.bk_a), channel_id=1, source_target_pairs={{0,1},{1,0},{2,3},{3,2},{4,5},{5,4},{6,7},{7,6},{8,9},{9,8},{10,11... | collective-permute-start | bytes 3538952 | tf_op jit(solution)/shard_map/ppermute | solution.py:346
  111.1 1.0 copy-start.2
  119.2 13.2 %collective-permute-start.15 = (bf16[384,512]{1,0:T(8,128)(2,1)}, bf16[384,512]{1,0:T(8,128)(2,1)}, u32[]{:S(2)}, u32[]{:S(2)}) collective-permute-start(bf16[384,512]{1,0:T(8,128)(2,1)} %get-tuple-element.52), channel_id=1, source_target_pairs={{0,64},{64,128},{128,192},{192,0},{1,65},{65,129},{129,193},{193,1... | collective-permute-start | bytes 1179656 | tf_op jit(solution)/shard_map/ppermute | solution.py:340
  119.2 13.2 %collective-permute-start.16 = (bf16[384,512]{1,0:T(8,128)(2,1)}, bf16[384,512]{1,0:T(8,128)(2,1)}, u32[]{:S(2)}, u32[]{:S(2)}) collective-permute-start(bf16[384,512]{1,0:T(8,128)(2,1)} %get-tuple-element.54), channel_id=1, source_target_pairs={{0,192},{64,0},{128,64},{192,128},{1,193},{65,1},{129,65},{193,129... | collective-permute-start | bytes 1179656 | tf_op jit(solution)/shard_map/ppermute | solution.py:343
  127.6 21.1 %collective-permute-start.14 = (bf16[384,512]{1,0:T(8,128)(2,1)}, bf16[384,512]{1,0:T(8,128)(2,1)}, u32[]{:S(2)}, u32[]{:S(2)}) collective-permute-start(bf16[384,512]{1,0:T(8,128)(2,1)} %get-tuple-element.50), channel_id=1, source_target_pairs={{0,192},{64,0},{128,64},{192,128},{1,193},{65,1},{129,65},{193,129... | collective-permute-start | bytes 1179656 | tf_op jit(solution)/shard_map/ppermute | solution.py:343
  127.6 13.6 %collective-permute-start.19 = (bf16[384,512]{1,0:T(8,128)(2,1)}, bf16[384,512]{1,0:T(8,128)(2,1)}, u32[]{:S(2)}, u32[]{:S(2)}) collective-permute-start(bf16[384,512]{1,0:T(8,128)(2,1)} %get-tuple-element.57), channel_id=1, source_target_pairs={{0,64},{64,128},{128,192},{192,0},{1,65},{65,129},{129,193},{193,1... | collective-permute-start | bytes 1179656 | tf_op jit(solution)/shard_map/ppermute | solution.py:340
  134.7 14.0 %collective-permute-start.17 = (bf16[384,512]{1,0:T(8,128)(2,1)}, bf16[384,512]{1,0:T(8,128)(2,1)S(1)}, u32[]{:S(2)}, u32[]{:S(2)}) collective-permute-start(bf16[384,512]{1,0:T(8,128)(2,1)} %get-tuple-element.55), channel_id=1, source_target_pairs={{0,64},{64,128},{128,192},{192,0},{1,65},{65,129},{129,193},{193,1... | collective-permute-start | bytes 1179656 | tf_op jit(solution)/shard_map/ppermute | solution.py:340
  135.0 13.7 %collective-permute-start.18 = (bf16[384,512]{1,0:T(8,128)(2,1)}, bf16[384,512]{1,0:T(8,128)(2,1)S(1)}, u32[]{:S(2)}, u32[]{:S(2)}) collective-permute-start(bf16[384,512]{1,0:T(8,128)(2,1)} %get-tuple-element.56), channel_id=1, source_target_pairs={{0,192},{64,0},{128,64},{192,128},{1,193},{65,1},{129,65},{193,129... | collective-permute-start | bytes 1179656 | tf_op jit(solution)/shard_map/ppermute | solution.py:343
  141.2 16.7 %all-to-all-start.2 = ((bf16[32,24,128]{2,1,0:T(8,128)(2,1)}), bf16[32,24,128]{2,1,0:T(8,128)(2,1)}, u32[]{:S(2)}, u32[]{:S(2)}) async-start(bf16[32,24,128]{2,1,0:T(8,128)(2,1)} %bitcast.12), calls=%async_computation.2 | async-start | bytes 393216 | tf_op jit(solution)/shard_map/all_to_all | solution.py:351
  148.7 0.8 copy-start.3
  148.7 0.9 copy-start.4
  158.0 25.5 %all-to-all-start.3 = ((bf16[32,24,512]{2,1,0:T(8,128)(2,1)}), bf16[32,24,512]{2,1,0:T(8,128)(2,1)}, u32[]{:S(2)}, u32[]{:S(2)}) async-start(bf16[32,24,512]{2,1,0:T(8,128)(2,1)} %bitcast.21), calls=%async_computation.3 | async-start | bytes 1572864 | tf_op jit(solution)/shard_map/all_to_all | solution.py:351
  183.5 14.9 %collective-permute-start.21 = (bf16[3,192,2048]{2,1,0:T(8,128)(2,1)}, bf16[3,192,2048]{2,1,0:T(8,128)(2,1)}, u32[]{:S(2)}, u32[]{:S(2)}) collective-permute-start(bf16[3,192,2048]{2,1,0:T(8,128)(2,1)} %get-tuple-element.70), channel_id=1, source_target_pairs={{0,1},{1,0},{2,3},{3,2},{4,5},{5,4},{6,7},{7,6},{8,9},{9,8},{10,11... | collective-permute-start | bytes 7077896 | tf_op jit(solution)/shard_map/ppermute | solution.py:346
  186.3 2.3 %collective-permute-start.20 = (bf16[144,512]{1,0:T(8,128)(2,1)}, bf16[144,512]{1,0:T(8,128)(2,1)}, u32[]{:S(2)}, u32[]{:S(2)}) collective-permute-start(bf16[144,512]{1,0:T(8,128)(2,1)} %get-tuple-element.67), channel_id=1, source_target_pairs={{0,1},{1,0},{2,3},{3,2},{4,5},{5,4},{6,7},{7,6},{8,9},{9,8},{10,11... | collective-permute-start | bytes 442376 | tf_op jit(solution)/shard_map/ppermute | solution.py:346
  186.8 7.7 %collective-permute-start.22 = (bf16[144,512]{1,0:T(8,128)(2,1)}, bf16[144,512]{1,0:T(8,128)(2,1)}, u32[]{:S(2)}, u32[]{:S(2)}) collective-permute-start(bf16[144,512]{1,0:T(8,128)(2,1)} %get-tuple-element.73.refs_0_), channel_id=1, source_target_pairs={{0,64},{64,128},{128,192},{192,0},{1,65},{65,129},{129,193},{193,1... | collective-permute-start | bytes 442376 | tf_op jit(solution)/shard_map/ppermute | solution.py:340
  188.5 7.0 %collective-permute-start.25 = (bf16[144,512]{1,0:T(8,128)(2,1)}, bf16[144,512]{1,0:T(8,128)(2,1)}, u32[]{:S(2)}, u32[]{:S(2)}) collective-permute-start(bf16[144,512]{1,0:T(8,128)(2,1)} %collective-permute-done.20.refs_1_), channel_id=1, source_target_pairs={{0,192},{64,0},{128,64},{192,128},{1,193},{65,1},{129,65},{193,129... | collective-permute-start | bytes 442376 | tf_op jit(solution)/shard_map/ppermute | solution.py:343
  190.0 13.1 %collective-permute-start.24 = (bf16[144,512]{1,0:T(8,128)(2,1)}, bf16[144,512]{1,0:T(8,128)(2,1)}, u32[]{:S(2)}, u32[]{:S(2)}) collective-permute-start(bf16[144,512]{1,0:T(8,128)(2,1)} %get-tuple-element.73.refs_0_), channel_id=1, source_target_pairs={{0,192},{64,0},{128,64},{192,128},{1,193},{65,1},{129,65},{193,129... | collective-permute-start | bytes 442376 | tf_op jit(solution)/shard_map/ppermute | solution.py:343
  190.1 13.0 %collective-permute-start.23 = (bf16[144,512]{1,0:T(8,128)(2,1)}, bf16[144,512]{1,0:T(8,128)(2,1)}, u32[]{:S(2)}, u32[]{:S(2)}) collective-permute-start(bf16[144,512]{1,0:T(8,128)(2,1)} %collective-permute-done.20.refs_1_), channel_id=1, source_target_pairs={{0,64},{64,128},{128,192},{192,0},{1,65},{65,129},{129,193},{193,1... | collective-permute-start | bytes 442376 | tf_op jit(solution)/shard_map/ppermute | solution.py:340
  194.4 8.6 %collective-permute-start.26 = (bf16[144,512]{1,0:T(8,128)(2,1)}, bf16[144,512]{1,0:T(8,128)(2,1)}, u32[]{:S(2)}, u32[]{:S(2)}) collective-permute-start(bf16[144,512]{1,0:T(8,128)(2,1)} %collective-permute-done.22.refs_2_), channel_id=1, source_target_pairs={{0,64},{64,128},{128,192},{192,0},{1,65},{65,129},{129,193},{193,1... | collective-permute-start | bytes 442376 | tf_op jit(solution)/shard_map/ppermute | solution.py:340
  195.6 7.6 %collective-permute-start.27 = (bf16[144,512]{1,0:T(8,128)(2,1)}, bf16[144,512]{1,0:T(8,128)(2,1)}, u32[]{:S(2)}, u32[]{:S(2)}) collective-permute-start(bf16[144,512]{1,0:T(8,128)(2,1)} %collective-permute-done.25.refs_5_), channel_id=1, source_target_pairs={{0,192},{64,0},{128,64},{192,128},{1,193},{65,1},{129,65},{193,129... | collective-permute-start | bytes 442376 | tf_op jit(solution)/shard_map/ppermute | solution.py:343

commit v4 on v3

--- a/solution.py
+++ b/solution.py
@@ -42,9 +42,9 @@
 
 
 COST = {
-    "pack": 2, "send": 3, "weight_send": 4, "weight_join": 6, "gate_up": 8, "back_near": 5, "back": 3,
+    "pack": 2, "send": 3, "weight_send": 4, "weight_join": 6, "gate_up": 8, "back_near": 0.02, "back": 3,
     "mid": 8, "rest": 4, "pass_on": 2,
-    "wgrad": 13, "wgrad_join": 5, "finish": 2, "collect": 3, "assemble": 2,
+    "wgrad": 6, "wgrad_join": 5, "finish": 2, "collect": 3, "assemble": 2,
 }
 
 
@@ -57,7 +57,7 @@
         scratch_shapes=list(scratch),
         compiler_params=pltpu.CompilerParams(vmem_limit_bytes=60 * 1024 * 1024),
         cost_estimate=pl.CostEstimate(
-            flops=COST[name] * 100_000_000_000, transcendentals=0, bytes_accessed=0
+            flops=int(COST[name] * 1e11), transcendentals=0, bytes_accessed=0
         ),
         name=name,
     )(*args)
@@ -175,10 +175,10 @@
 
 
 def back_near_body(pos, *refs):
-    xs, w, out = refs[:6], refs[6], refs[7]
-    for half in range(2):
+    a, b, la, lb, rb, ra, w, out = refs
+    for half, xs in enumerate(((a, la, ra), (b, lb, rb))):
         acc = None
-        for x, off in zip(xs[half::2], OFFS[:3]):
+        for x, off in zip(xs, OFFS[:3]):
             part = mm(x[...], w[:, chunk_cols(pos[0], off)], NT)
             acc = part if acc is None else acc + part
         out[half * HR : (half + 1) * HR, :] = acc
@@ -262,18 +262,17 @@
         store(2, c, (last * factor).astype(BF))
 
 
-def wgrad_body(pos, both, hd, *refs):
-    xs, gs, (own, other, gu_t, hd_t) = refs[:5], refs[5:13], refs[13:]
+def wgrad_body(first, pos, both, hd, *refs):
+    xs, gs, (out, gu_t, hd_t) = refs[:5], refs[5:13], refs[13:]
     h = pos[1]
     for m in range(2):
         gu_t[m] = both[:, m * UNITS : (m + 1) * UNITS].T
     hd_t[...] = hd[...].T
-    for half, out in ((1 - h, other), (h, own)):
-
-        def store(m, c, part, out=out):
-            out[m, :, at(c, CH)] = part
-
-        wgrad(pos, half, gu_t, hd_t, xs, gs, store)
+
+    def store(m, c, part):
+        out[m, :, at(c, CH)] = part
+
+    wgrad(pos, 1 - h if first else h, gu_t, hd_t, xs, gs, store)
 
 
 def wgrad_join_body(pos, own, got, *outs):
@@ -390,11 +389,11 @@
         weight_join_body, [((2, UNITS, HALF), BF), ((UNITS, HALF), BF)],
         (pos, gw, uw, dw, wgot), name="weight_join",
     )
-    xs, gs = spread(xs), spread_halves(gs[:HR], gs[HR:])
+    xs, gs = spread(xs), list(spread_halves(gs[:HR], gs[HR:]))
     (gu_a,) = call(gate_up_body, [((ROWS, 2 * UNITS), F32)], (pos, *xs, wgu), name="gate_up")
     gu_b = swap(gu_a)
     (bk_a,) = call(
-        back_near_body, [((ROWS, UNITS), F32)], (pos, *gs[:6], wd), name="back_near"
+        back_near_body, [((ROWS, UNITS), F32)], (pos, *gs[:4], gs[5], gs[4], wd), name="back_near"
     )
     (bk_a,) = call(
         back_body, [((ROWS, UNITS), F32)], (pos, bk_a, *gs[6:], wd), name="back"
@@ -418,13 +417,17 @@
     (r,) = call(finish_body, [((ROWS, CH), BF)], (pos, d0, ma, pa, mb, pb), name="finish")
     both, r, cb = tie((both, r, cb))
     r = exchange(r)
-    w_own, w_other = call(
-        wgrad_body, [((3, 192, HALF), BF)] * 2, (pos, both, hd, *xs, *gs),
-        scratch=[pltpu.VMEM((2, UNITS, ROWS), BF), pltpu.VMEM((UNITS, ROWS), BF)],
-        name="wgrad",
-    )
-    r, w_other = tie((r, w_other))
-    dgot = swap(w_other)
+    def weight_grads(first):
+        return call(
+            functools.partial(wgrad_body, first), [((3, 192, HALF), BF)],
+            (pos, both, hd, *xs, *gs),
+            scratch=[pltpu.VMEM((2, UNITS, ROWS), BF), pltpu.VMEM((UNITS, ROWS), BF)],
+            name="wgrad",
+        )[0]
+
+    dgot = swap(weight_grads(True))
+    w_own = weight_grads(False)
+    r, w_own = tie((r, w_own))
     qa, sib = call(
         collect_body, [((144, CH), BF)] * 2, (pos, ids, pk, r, cb), name="collect"
     )

time: 206 us -> 215 us (1.044)
  Pallas kernels: 70.5 us -> 75.7 us
  waiting for transfers between devices: 64.2 us -> 68.5 us
    pallas_call x16 -> x17, Pallas kernels: 70.5 us -> 75.7 us  [call(): pl.pallas_call(body, out_shape=[jax.ShapeDtypeStruct(s, t) for s, t in ou...]
    ppermute x11, waiting for transfers between devices: 14.1 us -> 19.1 us  [up(): return lax.ppermute(x, 'dp', up_ring)]
    all_to_all x4, waiting for transfers between devices: 31.6 us -> 26.9 us  [exchange(): lax.all_to_all(x, 'expert', split_axis=0, concat_axis=0, axis_index_group...]
    ppermute x11, waiting for transfers between devices: 11.9 us -> 16.2 us  [down(): return lax.ppermute(x, 'dp', down_ring)]
    all_to_all x4, starting transfers between devices: 31 us -> 33.4 us  [exchange(): lax.all_to_all(x, 'expert', split_axis=0, concat_axis=0, axis_index_group...]
  transfers between devices with their start and end apart: 32 -> 32, of which waited for: 16 -> 12; matrix products, arithmetic and copies ran while one was open for 2% -> 1% of each run, Pallas kernels for 26% -> 27%
where the time goes in v4:
time: 215 us
  Pallas kernels  75.7 us (35%)
  waiting for transfers between devices  68.5 us (32%)
  starting transfers between devices  63.9 us (30%)
  local copies, waits for them, and re-layouts  5.33 us (2%)
    pallas_call x17, Pallas kernels, call(): pl.pallas_call(body, out_shape=[jax.ShapeDtypeStruct(s, t) for s, t in ou...  75.7 us
    all_to_all x4, starting transfers between devices, exchange(): lax.all_to_all(x, 'expert', split_axis=0, concat_axis=0, axis_index_group...  33.4 us
    all_to_all x4, waiting for transfers between devices, exchange(): lax.all_to_all(x, 'expert', split_axis=0, concat_axis=0, axis_index_group...  26.9 us
    ppermute x11, starting transfers between devices, down(): return lax.ppermute(x, 'dp', down_ring)  26 us
    ppermute x11, waiting for transfers between devices, up(): return lax.ppermute(x, 'dp', up_ring)  19.1 us
    ppermute x11, waiting for transfers between devices, down(): return lax.ppermute(x, 'dp', down_ring)  16.2 us
    ppermute x6, waiting for transfers between devices, swap(): return lax.ppermute(x, 'expert', cores)  6.16 us
  transfers between devices with their start and end apart: 32, of which 12 were waited for; matrix products, arithmetic and copies ran while one was open for 1% of the time, Pallas kernels for 27%

profile of v4, /device:TPU:2, one launch (start us, length us, event | category | flops | bytes accessed | tf_op | source)
XLA Modules:
  0.0 214.8 jit_solution(2458731597289886475)
XLA Ops:
  0.6 0.7 pad_add_fusion.pos
  1.3 2.3 %pack.1 = bf16[272,512]{1,0:T(8,128)(2,1)} custom-call(s32[2]{0:T(128)} %pad_add_fusion.pos, s32[8,128]{1,0:T(8,128)} %bitcast.29, bf16[8,128]{1,0:T(8,128)(2,1)} %bitcast.33, bf16[128,4096]{1,0:T(8,128)(2,1)} %rows_ref.3, bf16[128,4096]{1,0:T(8,128)(2,1)} %rows_ref.2), custom_call_target="tpu_custom_call" | custom-call | flops 199999995904 | tf_op jit(solution)/shard_map/pack/pallas_call | solution.py:52
  3.6 1.8 collective-permute-done.pk
  5.4 0.7 copy-done.5
  6.1 3.0 %send.3 = bf16[768,512]{1,0:T(8,128)(2,1)} custom-call(s32[2]{0:T(128)} %pad_add_fusion.pos, s32[8,128]{1,0:T(8,128)} %bitcast.30, bf16[8,128]{1,0:T(8,128)(2,1)} %bitcast.34, bf16[272,512]{1,0:T(8,128)(2,1)} %copy-done.5, bf16[128,4096]{1,0:T(8,128)(2,1)} %rows_ref.3), custom_call_target="tpu_custom_call" | custom-call | flops 299999985664 | tf_op jit(solution)/shard_map/send/pallas_call | solution.py:52
  9.1 11.7 %all-to-all-start = ((bf16[32,24,512]{2,1,0:T(8,128)(2,1)}), bf16[32,24,512]{2,1,0:T(8,128)(2,1)}, u32[]{:S(2)}, u32[]{:S(2)}) async-start(bf16[32,24,512]{2,1,0:T(8,128)(2,1)} %bitcast.22), calls=%async_computation | async-start | bytes 1572864 | tf_op jit(solution)/shard_map/all_to_all | solution.py:350
  20.8 3.9 %weight_send.1 = bf16[3,192,2048]{2,1,0:T(8,128)(2,1)} custom-call(s32[2]{0:T(128)} %pad_add_fusion.pos, bf16[192,4096]{1,0:T(8,128)(2,1)} %bitcast.23, bf16[192,4096]{1,0:T(8,128)(2,1)} %bitcast.25, bf16[192,4096]{1,0:T(8,128)(2,1)} %bitcast.27), custom_call_target="tpu_custom_call" | custom-call | flops 399999991808 | tf_op jit(solution)/shard_map/weight_send/pallas_call | solution.py:52
  24.7 0.0 collective-permute-start.5
  24.7 3.1 %send.2 = bf16[768,512]{1,0:T(8,128)(2,1)} custom-call(s32[2]{0:T(128)} %pad_add_fusion.pos, s32[8,128]{1,0:T(8,128)} %bitcast.31, bf16[8,128]{1,0:T(8,128)(2,1)} %bitcast.35, bf16[272,512]{1,0:T(8,128)(2,1)} %copy-done.5, bf16[128,4096]{1,0:T(8,128)(2,1)} %rows_ref.2), custom_call_target="tpu_custom_call" | custom-call | flops 299999985664 | tf_op jit(solution)/shard_map/send/pallas_call | solution.py:52
  27.8 15.7 %all-to-all-done = bf16[32,24,512]{2,1,0:T(8,128)(2,1)} async-done(((bf16[32,24,512]{2,1,0:T(8,128)(2,1)}), bf16[32,24,512]{2,1,0:T(8,128)(2,1)}, u32[]{:S(2)}, u32[]{:S(2)}) %all-to-all-start) | async-done | bytes 786464 | tf_op jit(solution)/shard_map/all_to_all | solution.py:350
  43.6 5.6 %all-to-all-start.1 = ((bf16[32,24,512]{2,1,0:T(8,128)(2,1)}), bf16[32,24,512]{2,1,0:T(8,128)(2,1)S(1)}, u32[]{:S(2)}, u32[]{:S(2)}) async-start(bf16[32,24,512]{2,1,0:T(8,128)(2,1)} %bitcast.21), calls=%async_computation.1 | async-start | bytes 1572864 | tf_op jit(solution)/shard_map/all_to_all | solution.py:350
  49.1 3.1 %collective-permute-start.2 = (bf16[768,512]{1,0:T(8,128)(2,1)}, bf16[768,512]{1,0:T(8,128)(2,1)S(1)}, u32[]{:S(2)}, u32[]{:S(2)}) collective-permute-start(bf16[768,512]{1,0:T(8,128)(2,1)} %bitcast.5.x0.refs_0_), channel_id=1, source_target_pairs={{0,192},{64,0},{128,64},{192,128},{1,193},{65,1},{129,65},{193,129... | collective-permute-start | bytes 2359304 | tf_op jit(solution)/shard_map/ppermute | solution.py:342
  52.2 15.7 %collective-permute-done.2.x2.refs_2_ = bf16[768,512]{1,0:T(8,128)(2,1)S(1)} collective-permute-done((bf16[768,512]{1,0:T(8,128)(2,1)}, bf16[768,512]{1,0:T(8,128)(2,1)S(1)}, u32[]{:S(2)}, u32[]{:S(2)}) %collective-permute-start.2) | collective-permute-done | bytes 786464 | tf_op jit(solution)/shard_map/ppermute | solution.py:342
  67.9 0.8 slice.25
  68.7 3.6 %collective-permute-start.4 = (bf16[384,512]{1,0:T(8,128)(2,1)}, bf16[384,512]{1,0:T(8,128)(2,1)}, u32[]{:S(2)}, u32[]{:S(2)}) collective-permute-start(bf16[384,512]{1,0:T(8,128)(2,1)} %slice.25), channel_id=1, source_target_pairs={{0,192},{64,0},{128,64},{192,128},{1,193},{65,1},{129,65},{193,129... | collective-permute-start | bytes 1179656 | tf_op jit(solution)/shard_map/ppermute | solution.py:342
  72.3 0.8 slice.24
  73.1 0.2 copy-done.1
  73.3 0.0 collective-permute-start.3
  73.3 0.0 all-to-all-done.1
  73.3 0.9 fusion
  74.2 0.0 collective-permute-start.7
  74.2 3.2 %collective-permute-start.9 = (bf16[384,512]{1,0:T(8,128)(2,1)}, bf16[384,512]{1,0:T(8,128)(2,1)}, u32[]{:S(2)}, u32[]{:S(2)}) collective-permute-start(bf16[384,512]{1,0:T(8,128)(2,1)} %bitcast.11.refs_1_.refs_6_), channel_id=1, source_target_pairs={{0,192},{64,0},{128,64},{192,128},{1,193},{65,1},{129,65},{193,129... | collective-permute-start | bytes 1179656 | tf_op jit(solution)/shard_map/ppermute | solution.py:342
  77.5 5.6 %weight_join.1 = (bf16[2,384,2048]{2,1,0:T(8,128)(2,1)}, bf16[384,2048]{1,0:T(8,128)(2,1)}) custom-call(s32[2]{0:T(128)} %pad_add_fusion.pos, bf16[192,4096]{1,0:T(8,128)(2,1)} %bitcast.24, bf16[192,4096]{1,0:T(8,128)(2,1)} %bitcast.26, bf16[192,4096]{1,0:T(8,128)(2,1)} %bitcast.28, bf16[3,192,2048]{2,1,0:T(8,128)(2,1)} %collective-permute-done.5.got), custom_call_target="tpu_custom_call" | custom-call | flops 599999971328 | tf_op jit(solution)/shard_map/weight_join/pallas_call | solution.py:52
  83.0 2.0 collective-permute-start.10
  85.1 0.0 collective-permute-start.8
  85.1 10.3 %collective-permute-done.7.refs_2_.refs_7_ = bf16[384,512]{1,0:T(8,128)(2,1)} collective-permute-done((bf16[384,512]{1,0:T(8,128)(2,1)}, bf16[384,512]{1,0:T(8,128)(2,1)}, u32[]{:S(2)}, u32[]{:S(2)}) %collective-permute-start.7) | collective-permute-done | bytes 393248 | tf_op jit(solution)/shard_map/ppermute | solution.py:339
  95.3 0.0 collective-permute-start.11
  95.3 0.0 collective-permute-done.9.refs_4_.refs_10_
  95.3 3.2 %collective-permute-start.12 = (bf16[384,512]{1,0:T(8,128)(2,1)}, bf16[384,512]{1,0:T(8,128)(2,1)}, u32[]{:S(2)}, u32[]{:S(2)}) collective-permute-start(bf16[384,512]{1,0:T(8,128)(2,1)} %collective-permute-done.9.refs_4_.refs_10_), channel_id=1, source_target_pairs={{0,192},{64,0},{128,64},{192,128},{1,193},{65,1},{129,65},{193,129... | collective-permute-start | bytes 1179656 | tf_op jit(solution)/shard_map/ppermute | solution.py:342
  98.6 0.0 collective-permute-done.3.xa.refs_3_
  98.6 7.5 %gate_up.1.gu_a = f32[768,768]{1,0:T(8,128)} custom-call(s32[2]{0:T(128)} %pad_add_fusion.pos, bf16[768,512]{1,0:T(8,128)(2,1)} %bitcast.5.x0.refs_0_, bf16[768,512]{1,0:T(8,128)(2,1)} %copy-done.1, bf16[768,512]{1,0:T(8,128)(2,1)} %copy-done, bf16[384,512]{1,0:T(8,128)(2,1)} %collective-permute-done.3.xa.refs_3_, ...), custom_call_target="tpu_custom_call" | custom-call | flops 799999983616 | tf_op jit(solution)/shard_map/gate_up/pallas_call | solution.py:52
  106.1 0.0 collective-permute-start.6
  106.1 4.6 %back_near.1.acc = f32[768,384]{1,0:T(8,128)} custom-call(s32[2]{0:T(128)} %pad_add_fusion.pos, bf16[384,512]{1,0:T(8,128)(2,1)} %bitcast.10.refs_0_.refs_5_, bf16[384,512]{1,0:T(8,128)(2,1)} %bitcast.11.refs_1_.refs_6_, bf16[384,512]{1,0:T(8,128)(2,1)} %collective-permute-done.7.refs_2_.refs_7_, bf16[384,512]{1,0:T(8,128)(2,1)} %collective-permute-done.8.refs_3_.refs_8_, ...), custom_call_target="tpu_custom_call" | custom-call | flops 2000000000 | tf_op jit(solution)/shard_map/back_near/pallas_call | solution.py:52
  110.7 3.6 %back.1.bk_a = f32[768,384]{1,0:T(8,128)} custom-call(s32[2]{0:T(128)} %pad_add_fusion.pos, f32[768,384]{1,0:T(8,128)} %back_near.1.acc, bf16[384,512]{1,0:T(8,128)(2,1)} %collective-permute-done.11.xa.refs_11_, bf16[384,512]{1,0:T(8,128)(2,1)} %collective-permute-done.12.xb.refs_12_, bf16[384,2048]{1,0:T(8,128)(2,1)} %get-tuple-element.45.refs_6_.w), custom_call_target="tpu_custom_call" | custom-call | flops 299999985664 | tf_op jit(solution)/shard_map/back/pallas_call | solution.py:52
  114.3 0.5 collective-permute-start.13
  114.8 2.7 %collective-permute-done.13.bk_b = f32[768,384]{1,0:T(8,128)S(1)} collective-permute-done((f32[768,384]{1,0:T(8,128)}, f32[768,384]{1,0:T(8,128)S(1)}, u32[]{:S(2)}, u32[]{:S(2)}) %collective-permute-start.13) | collective-permute-done | bytes 1179680 | tf_op jit(solution)/shard_map/ppermute | solution.py:345
  117.5 1.0 copy-done.2
  118.5 7.0 %mid.1 = (bf16[768,768]{1,0:T(8,128)(2,1)}, bf16[768,384]{1,0:T(8,128)(2,1)}, bf16[768,128]{1,0:T(8,128)(2,1)}, bf16[384,512]{1,0:T(8,128)(2,1)}, bf16[384,512]{1,0:T(8,128)(2,1)}) custom-call(s32[2]{0:T(128)} %pad_add_fusion.pos, f32[768,768]{1,0:T(8,128)} %gate_up.1.gu_a, f32[768,768]{1,0:T(8,128)} %collective-permute-done.6.gu_b, f32[768,384]{1,0:T(8,128)} %back.1.bk_a, ...), custom_call_target="tpu_custom_call" | custom-call | flops 799999983616 | tf_op jit(solution)/shard_map/mid/pallas_call | solution.py:52
  125.5 3.2 %collective-permute-start.16 = (bf16[384,512]{1,0:T(8,128)(2,1)}, bf16[384,512]{1,0:T(8,128)(2,1)}, u32[]{:S(2)}, u32[]{:S(2)}) collective-permute-start(bf16[384,512]{1,0:T(8,128)(2,1)} %get-tuple-element.52), channel_id=1, source_target_pairs={{0,192},{64,0},{128,64},{192,128},{1,193},{65,1},{129,65},{193,129... | collective-permute-start | bytes 1179656 | tf_op jit(solution)/shard_map/ppermute | solution.py:342
  128.8 5.2 %rest.1 = (bf16[384,512]{1,0:T(8,128)(2,1)}, bf16[384,512]{1,0:T(8,128)(2,1)}, bf16[384,512]{1,0:T(8,128)(2,1)}, bf16[384,512]{1,0:T(8,128)(2,1)}, bf16[768,512]{1,0:T(8,128)(2,1)}) custom-call(s32[2]{0:T(128)} %pad_add_fusion.pos, bf16[768,768]{1,0:T(8,128)(2,1)} %get-tuple-element.60.both, bf16[2,384,2048]{2,1,0:T(8,128)(2,1)} %get-tuple-element.43.w), custom_call_target="tpu_custom_call" | custom-call | flops 399999991808 | tf_op jit(solution)/shard_map/rest/pallas_call | solution.py:52
  134.0 2.0 collective-permute-start.19
  136.0 3.0 %collective-permute-done.15.r2 = bf16[384,512]{1,0:T(8,128)(2,1)} collective-permute-done((bf16[384,512]{1,0:T(8,128)(2,1)}, bf16[384,512]{1,0:T(8,128)(2,1)}, u32[]{:S(2)}, u32[]{:S(2)}) %collective-permute-start.15) | collective-permute-done | bytes 393248 | tf_op jit(solution)/shard_map/ppermute | solution.py:339
  139.0 2.3 %pass_on.1 = (bf16[384,512]{1,0:T(8,128)(2,1)}, bf16[384,512]{1,0:T(8,128)(2,1)}) custom-call(s32[2]{0:T(128)} %pad_add_fusion.pos, bf16[384,512]{1,0:T(8,128)(2,1)} %get-tuple-element.49.dpa, bf16[384,512]{1,0:T(8,128)(2,1)} %collective-permute-done.15.r2, bf16[384,512]{1,0:T(8,128)(2,1)} %get-tuple-element.51.dmb, bf16[384,512]{1,0:T(8,128)(2,1)} %collective-permute-done.16.q2), custom_call_target="tpu_custom_call" | custom-call | flops 199999995904 | tf_op jit(solution)/shard_map/pass_on/pallas_call | solution.py:52
  141.4 3.3 %collective-permute-start.18 = (bf16[384,512]{1,0:T(8,128)(2,1)}, bf16[384,512]{1,0:T(8,128)(2,1)S(1)}, u32[]{:S(2)}, u32[]{:S(2)}) collective-permute-start(bf16[384,512]{1,0:T(8,128)(2,1)} %get-tuple-element.54), channel_id=1, source_target_pairs={{0,192},{64,0},{128,64},{192,128},{1,193},{65,1},{129,65},{193,129... | collective-permute-start | bytes 1179656 | tf_op jit(solution)/shard_map/ppermute | solution.py:342
  144.6 2.9 %collective-permute-done.19.pb = bf16[384,512]{1,0:T(8,128)(2,1)} collective-permute-done((bf16[384,512]{1,0:T(8,128)(2,1)}, bf16[384,512]{1,0:T(8,128)(2,1)}, u32[]{:S(2)}, u32[]{:S(2)}) %collective-permute-start.19) | collective-permute-done | bytes 393248 | tf_op jit(solution)/shard_map/ppermute | solution.py:339
  147.5 9.8 %all-to-all-start.2 = ((bf16[32,24,128]{2,1,0:T(8,128)(2,1)}), bf16[32,24,128]{2,1,0:T(8,128)(2,1)}, u32[]{:S(2)}, u32[]{:S(2)}) async-start(bf16[32,24,128]{2,1,0:T(8,128)(2,1)} %bitcast.12), calls=%async_computation.2 | async-start | bytes 393216 | tf_op jit(solution)/shard_map/all_to_all | solution.py:350
  157.4 0.8 copy-done.3
  158.2 0.1 copy-done.4
  158.3 2.8 %finish.1 = bf16[768,512]{1,0:T(8,128)(2,1)} custom-call(s32[2]{0:T(128)} %pad_add_fusion.pos, bf16[768,512]{1,0:T(8,128)(2,1)} %get-tuple-element.47.d0, bf16[384,512]{1,0:T(8,128)(2,1)} %collective-permute-done.14.ma, bf16[384,512]{1,0:T(8,128)(2,1)} %copy-done.3, bf16[384,512]{1,0:T(8,128)(2,1)} %copy-done.4, bf16[384,512]{1,0:T(8,128)(2,1)} %collective-permute-done.19.pb), custom_call_target="tpu_custom_call" | custom-call | flops 199999995904 | tf_op jit(solution)/shard_map/finish/pallas_call | solution.py:52
  161.0 5.7 %all-to-all-done.2 = bf16[32,24,128]{2,1,0:T(8,128)(2,1)} async-done(((bf16[32,24,128]{2,1,0:T(8,128)(2,1)}), bf16[32,24,128]{2,1,0:T(8,128)(2,1)}, u32[]{:S(2)}, u32[]{:S(2)}) %all-to-all-start.2) | async-done | bytes 196640 | tf_op jit(solution)/shard_map/all_to_all | solution.py:350
  166.7 6.3 %all-to-all-start.3 = ((bf16[32,24,512]{2,1,0:T(8,128)(2,1)}), bf16[32,24,512]{2,1,0:T(8,128)(2,1)}, u32[]{:S(2)}, u32[]{:S(2)}) async-start(bf16[32,24,512]{2,1,0:T(8,128)(2,1)} %bitcast.20), calls=%async_computation.3 | async-start | bytes 1572864 | tf_op jit(solution)/shard_map/all_to_all | solution.py:350
  173.1 7.4 %wgrad.3 = bf16[3,192,2048]{2,1,0:T(8,128)(2,1)} custom-call(s32[2]{0:T(128)} %pad_add_fusion.pos, bf16[768,768]{1,0:T(8,128)(2,1)} %get-tuple-element.60.both, bf16[768,384]{1,0:T(8,128)(2,1)} %get-tuple-element.61.hd, bf16[768,512]{1,0:T(8,128)(2,1)} %bitcast.5.x0.refs_0_, bf16[768,512]{1,0:T(8,128)(2,1)} %copy-done.1, bf16[768,512]{1,0:T(8,128)(2,1)} %copy-done, ...), custom_call_target="tpu_custom_call" | custom-call | flops 599999971328 | tf_op jit(solution)/shard_map/wgrad/pallas_call | solution.py:52
  180.4 7.3 %wgrad.2.own = bf16[3,192,2048]{2,1,0:T(8,128)(2,1)} custom-call(s32[2]{0:T(128)} %pad_add_fusion.pos, bf16[768,768]{1,0:T(8,128)(2,1)} %get-tuple-element.60.both, bf16[768,384]{1,0:T(8,128)(2,1)} %get-tuple-element.61.hd, bf16[768,512]{1,0:T(8,128)(2,1)} %bitcast.5.x0.refs_0_, bf16[768,512]{1,0:T(8,128)(2,1)} %copy-done.1, bf16[768,512]{1,0:T(8,128)(2,1)} %copy-done, ...), custom_call_target="tpu_custom_call" | custom-call | flops 599999971328 | tf_op jit(solution)/shard_map/wgrad/pallas_call | solution.py:52
  187.8 5.6 %all-to-all-done.3 = bf16[32,24,512]{2,1,0:T(8,128)(2,1)} async-done(((bf16[32,24,512]{2,1,0:T(8,128)(2,1)}), bf16[32,24,512]{2,1,0:T(8,128)(2,1)}, u32[]{:S(2)}, u32[]{:S(2)}) %all-to-all-start.3) | async-done | bytes 786464 | tf_op jit(solution)/shard_map/all_to_all | solution.py:350
  193.3 2.8 %collect.1 = (bf16[144,512]{1,0:T(8,128)(2,1)}, bf16[144,512]{1,0:T(8,128)(2,1)}) custom-call(s32[2]{0:T(128)} %pad_add_fusion.pos, s32[8,128]{1,0:T(8,128)} %bitcast.32, bf16[272,512]{1,0:T(8,128)(2,1)} %copy-done.5, bf16[768,512]{1,0:T(8,128)(2,1)} %bitcast.15.r, bf16[768,128]{1,0:T(8,128)(2,1)} %bitcast.13.cb), custom_call_target="tpu_custom_call" | custom-call | flops 299999985664 | tf_op jit(solution)/shard_map/collect/pallas_call | solution.py:52
  196.1 1.7 collective-permute-done.20.refs_1_
  197.9 1.5 collective-permute-start.25
  199.4 0.0 collective-permute-start.24
  199.4 2.0 collective-permute-start.23
  201.4 2.9 %collective-permute-done.22.refs_2_ = bf16[144,512]{1,0:T(8,128)(2,1)} collective-permute-done((bf16[144,512]{1,0:T(8,128)(2,1)}, bf16[144,512]{1,0:T(8,128)(2,1)}, u32[]{:S(2)}, u32[]{:S(2)}) %collective-permute-start.22) | collective-permute-done | bytes 147488 | tf_op jit(solution)/shard_map/ppermute | solution.py:339
  204.3 0.5 collective-permute-done.25.refs_5_
  204.9 2.7 %collective-permute-start.27 = (bf16[144,512]{1,0:T(8,128)(2,1)}, bf16[144,512]{1,0:T(8,128)(2,1)}, u32[]{:S(2)}, u32[]{:S(2)}) collective-permute-start(bf16[144,512]{1,0:T(8,128)(2,1)} %collective-permute-done.25.refs_5_), channel_id=1, source_target_pairs={{0,192},{64,0},{128,64},{192,128},{1,193},{65,1},{129,65},{193,129... | collective-permute-start | bytes 442376 | tf_op jit(solution)/shard_map/ppermute | solution.py:342
  207.6 4.8 %wgrad_join.1 = (bf16[192,4096]{1,0:T(8,128)(2,1)}, bf16[192,4096]{1,0:T(8,128)(2,1)}, bf16[192,4096]{1,0:T(8,128)(2,1)}) custom-call(s32[2]{0:T(128)} %pad_add_fusion.pos, bf16[3,192,2048]{2,1,0:T(8,128)(2,1)} %wgrad.2.own, bf16[3,192,2048]{2,1,0:T(8,128)(2,1)} %collective-permute-done.21.got), custom_call_target="tpu_custom_call" | custom-call | flops 499999997952 | tf_op jit(solution)/shard_map/wgrad_join/pallas_call | solution.py:52
  212.4 2.4 %assemble.1 = (bf16[128,4096]{1,0:T(8,128)(2,1)}, f32[8,128]{1,0:T(8,128)}) custom-call(s32[2]{0:T(128)} %pad_add_fusion.pos, bf16[8,128]{1,0:T(8,128)(2,1)} %bitcast.36, bf16[144,512]{1,0:T(8,128)(2,1)} %get-tuple-element.69.refs_0_, bf16[144,512]{1,0:T(8,128)(2,1)} %collective-permute-done.20.refs_1_, bf16[144,512]{1,0:T(8,128)(2,1)} %collective-permute-done.22.refs_2_, ...), custom_call_target="tpu_custom_call" | custom-call | flops 199999995904 | tf_op jit(solution)/shard_map/assemble/pallas_call | solution.py:52
  (33 shorter events, 0.1 us)
Async XLA Ops:
  3.6 1.8 collective-permute-start
  5.4 0.7 copy-start.5
  9.1 34.5 %all-to-all-start = ((bf16[32,24,512]{2,1,0:T(8,128)(2,1)}), bf16[32,24,512]{2,1,0:T(8,128)(2,1)}, u32[]{:S(2)}, u32[]{:S(2)}) async-start(bf16[32,24,512]{2,1,0:T(8,128)(2,1)} %bitcast.22), calls=%async_computation | async-start | bytes 1572864 | tf_op jit(solution)/shard_map/all_to_all | solution.py:350
  24.7 52.8 %collective-permute-start.5 = (bf16[3,192,2048]{2,1,0:T(8,128)(2,1)}, bf16[3,192,2048]{2,1,0:T(8,128)(2,1)}, u32[]{:S(2)}, u32[]{:S(2)}) collective-permute-start(bf16[3,192,2048]{2,1,0:T(8,128)(2,1)} %weight_send.1), channel_id=1, source_target_pairs={{0,1},{1,0},{2,3},{3,2},{4,5},{5,4},{6,7},{7,6},{8,9},{9,8},{10,11... | collective-permute-start | bytes 7077896 | tf_op jit(solution)/shard_map/ppermute | solution.py:345
  43.6 29.8 %all-to-all-start.1 = ((bf16[32,24,512]{2,1,0:T(8,128)(2,1)}), bf16[32,24,512]{2,1,0:T(8,128)(2,1)S(1)}, u32[]{:S(2)}, u32[]{:S(2)}) async-start(bf16[32,24,512]{2,1,0:T(8,128)(2,1)} %bitcast.21), calls=%async_computation.1 | async-start | bytes 1572864 | tf_op jit(solution)/shard_map/all_to_all | solution.py:350
  49.1 18.8 %collective-permute-start.2 = (bf16[768,512]{1,0:T(8,128)(2,1)}, bf16[768,512]{1,0:T(8,128)(2,1)S(1)}, u32[]{:S(2)}, u32[]{:S(2)}) collective-permute-start(bf16[768,512]{1,0:T(8,128)(2,1)} %bitcast.5.x0.refs_0_), channel_id=1, source_target_pairs={{0,192},{64,0},{128,64},{192,128},{1,193},{65,1},{129,65},{193,129... | collective-permute-start | bytes 2359304 | tf_op jit(solution)/shard_map/ppermute | solution.py:342
  52.2 20.1 %collective-permute-start.1 = (bf16[768,512]{1,0:T(8,128)(2,1)}, bf16[768,512]{1,0:T(8,128)(2,1)S(1)}, u32[]{:S(2)}, u32[]{:S(2)}) collective-permute-start(bf16[768,512]{1,0:T(8,128)(2,1)} %bitcast.5.x0.refs_0_), channel_id=1, source_target_pairs={{0,64},{64,128},{128,192},{192,0},{1,65},{65,129},{129,193},{193,1... | collective-permute-start | bytes 2359304 | tf_op jit(solution)/shard_map/ppermute | solution.py:339
  67.9 5.2 %copy-start = (bf16[768,512]{1,0:T(8,128)(2,1)}, bf16[768,512]{1,0:T(8,128)(2,1)S(1)}, u32[]{:S(2)}) copy-start(bf16[768,512]{1,0:T(8,128)(2,1)S(1)} %collective-permute-done.2.x2.refs_2_) | copy-start | bytes 2359300
  68.7 16.3 %collective-permute-start.4 = (bf16[384,512]{1,0:T(8,128)(2,1)}, bf16[384,512]{1,0:T(8,128)(2,1)}, u32[]{:S(2)}, u32[]{:S(2)}) collective-permute-start(bf16[384,512]{1,0:T(8,128)(2,1)} %slice.25), channel_id=1, source_target_pairs={{0,192},{64,0},{128,64},{192,128},{1,193},{65,1},{129,65},{193,129... | collective-permute-start | bytes 1179656 | tf_op jit(solution)/shard_map/ppermute | solution.py:342
  72.3 1.0 copy-start.1
  73.3 25.2 %collective-permute-start.3 = (bf16[384,512]{1,0:T(8,128)(2,1)}, bf16[384,512]{1,0:T(8,128)(2,1)}, u32[]{:S(2)}, u32[]{:S(2)}) collective-permute-start(bf16[384,512]{1,0:T(8,128)(2,1)} %slice.24), channel_id=1, source_target_pairs={{0,64},{64,128},{128,192},{192,0},{1,65},{65,129},{129,193},{193,1... | collective-permute-start | bytes 1179656 | tf_op jit(solution)/shard_map/ppermute | solution.py:339
  74.2 21.1 %collective-permute-start.7 = (bf16[384,512]{1,0:T(8,128)(2,1)}, bf16[384,512]{1,0:T(8,128)(2,1)}, u32[]{:S(2)}, u32[]{:S(2)}) collective-permute-start(bf16[384,512]{1,0:T(8,128)(2,1)} %bitcast.10.refs_0_.refs_5_), channel_id=1, source_target_pairs={{0,64},{64,128},{128,192},{192,0},{1,65},{65,129},{129,193},{193,1... | collective-permute-start | bytes 1179656 | tf_op jit(solution)/shard_map/ppermute | solution.py:339
  74.2 21.1 %collective-permute-start.9 = (bf16[384,512]{1,0:T(8,128)(2,1)}, bf16[384,512]{1,0:T(8,128)(2,1)}, u32[]{:S(2)}, u32[]{:S(2)}) collective-permute-start(bf16[384,512]{1,0:T(8,128)(2,1)} %bitcast.11.refs_1_.refs_6_), channel_id=1, source_target_pairs={{0,192},{64,0},{128,64},{192,128},{1,193},{65,1},{129,65},{193,129... | collective-permute-start | bytes 1179656 | tf_op jit(solution)/shard_map/ppermute | solution.py:342
  83.0 23.1 %collective-permute-start.10 = (bf16[384,512]{1,0:T(8,128)(2,1)}, bf16[384,512]{1,0:T(8,128)(2,1)}, u32[]{:S(2)}, u32[]{:S(2)}) collective-permute-start(bf16[384,512]{1,0:T(8,128)(2,1)} %bitcast.10.refs_0_.refs_5_), channel_id=1, source_target_pairs={{0,192},{64,0},{128,64},{192,128},{1,193},{65,1},{129,65},{193,129... | collective-permute-start | bytes 1179656 | tf_op jit(solution)/shard_map/ppermute | solution.py:342
  85.1 21.1 %collective-permute-start.8 = (bf16[384,512]{1,0:T(8,128)(2,1)}, bf16[384,512]{1,0:T(8,128)(2,1)}, u32[]{:S(2)}, u32[]{:S(2)}) collective-permute-start(bf16[384,512]{1,0:T(8,128)(2,1)} %bitcast.11.refs_1_.refs_6_), channel_id=1, source_target_pairs={{0,64},{64,128},{128,192},{192,0},{1,65},{65,129},{129,193},{193,1... | collective-permute-start | bytes 1179656 | tf_op jit(solution)/shard_map/ppermute | solution.py:339
  95.3 15.4 %collective-permute-start.11 = (bf16[384,512]{1,0:T(8,128)(2,1)}, bf16[384,512]{1,0:T(8,128)(2,1)}, u32[]{:S(2)}, u32[]{:S(2)}) collective-permute-start(bf16[384,512]{1,0:T(8,128)(2,1)} %collective-permute-done.7.refs_2_.refs_7_), channel_id=1, source_target_pairs={{0,64},{64,128},{128,192},{192,0},{1,65},{65,129},{129,193},{193,1... | collective-permute-start | bytes 1179656 | tf_op jit(solution)/shard_map/ppermute | solution.py:339
  95.3 15.4 %collective-permute-start.12 = (bf16[384,512]{1,0:T(8,128)(2,1)}, bf16[384,512]{1,0:T(8,128)(2,1)}, u32[]{:S(2)}, u32[]{:S(2)}) collective-permute-start(bf16[384,512]{1,0:T(8,128)(2,1)} %collective-permute-done.9.refs_4_.refs_10_), channel_id=1, source_target_pairs={{0,192},{64,0},{128,64},{192,128},{1,193},{65,1},{129,65},{193,129... | collective-permute-start | bytes 1179656 | tf_op jit(solution)/shard_map/ppermute | solution.py:342
  106.1 11.4 %collective-permute-start.6 = (f32[768,768]{1,0:T(8,128)}, f32[768,768]{1,0:T(8,128)}, u32[]{:S(2)}, u32[]{:S(2)}) collective-permute-start(f32[768,768]{1,0:T(8,128)} %gate_up.1.gu_a), channel_id=1, source_target_pairs={{0,1},{1,0},{2,3},{3,2},{4,5},{5,4},{6,7},{7,6},{8,9},{9,8},{10,11... | collective-permute-start | bytes 7077896 | tf_op jit(solution)/shard_map/ppermute | solution.py:345
  114.3 3.2 %collective-permute-start.13 = (f32[768,384]{1,0:T(8,128)}, f32[768,384]{1,0:T(8,128)S(1)}, u32[]{:S(2)}, u32[]{:S(2)}) collective-permute-start(f32[768,384]{1,0:T(8,128)} %back.1.bk_a), channel_id=1, source_target_pairs={{0,1},{1,0},{2,3},{3,2},{4,5},{5,4},{6,7},{7,6},{8,9},{9,8},{10,11... | collective-permute-start | bytes 3538952 | tf_op jit(solution)/shard_map/ppermute | solution.py:345
  117.5 1.0 copy-start.2
  125.5 13.5 %collective-permute-start.15 = (bf16[384,512]{1,0:T(8,128)(2,1)}, bf16[384,512]{1,0:T(8,128)(2,1)}, u32[]{:S(2)}, u32[]{:S(2)}) collective-permute-start(bf16[384,512]{1,0:T(8,128)(2,1)} %get-tuple-element.50), channel_id=1, source_target_pairs={{0,64},{64,128},{128,192},{192,0},{1,65},{65,129},{129,193},{193,1... | collective-permute-start | bytes 1179656 | tf_op jit(solution)/shard_map/ppermute | solution.py:339
  125.5 13.5 %collective-permute-start.16 = (bf16[384,512]{1,0:T(8,128)(2,1)}, bf16[384,512]{1,0:T(8,128)(2,1)}, u32[]{:S(2)}, u32[]{:S(2)}) collective-permute-start(bf16[384,512]{1,0:T(8,128)(2,1)} %get-tuple-element.52), channel_id=1, source_target_pairs={{0,192},{64,0},{128,64},{192,128},{1,193},{65,1},{129,65},{193,129... | collective-permute-start | bytes 1179656 | tf_op jit(solution)/shard_map/ppermute | solution.py:342
  134.0 23.4 %collective-permute-start.14 = (bf16[384,512]{1,0:T(8,128)(2,1)}, bf16[384,512]{1,0:T(8,128)(2,1)}, u32[]{:S(2)}, u32[]{:S(2)}) collective-permute-start(bf16[384,512]{1,0:T(8,128)(2,1)} %get-tuple-element.48), channel_id=1, source_target_pairs={{0,192},{64,0},{128,64},{192,128},{1,193},{65,1},{129,65},{193,129... | collective-permute-start | bytes 1179656 | tf_op jit(solution)/shard_map/ppermute | solution.py:342
  134.0 13.6 %collective-permute-start.19 = (bf16[384,512]{1,0:T(8,128)(2,1)}, bf16[384,512]{1,0:T(8,128)(2,1)}, u32[]{:S(2)}, u32[]{:S(2)}) collective-permute-start(bf16[384,512]{1,0:T(8,128)(2,1)} %get-tuple-element.55), channel_id=1, source_target_pairs={{0,64},{64,128},{128,192},{192,0},{1,65},{65,129},{129,193},{193,1... | collective-permute-start | bytes 1179656 | tf_op jit(solution)/shard_map/ppermute | solution.py:339
  141.4 16.0 %collective-permute-start.17 = (bf16[384,512]{1,0:T(8,128)(2,1)}, bf16[384,512]{1,0:T(8,128)(2,1)S(1)}, u32[]{:S(2)}, u32[]{:S(2)}) collective-permute-start(bf16[384,512]{1,0:T(8,128)(2,1)} %get-tuple-element.53), channel_id=1, source_target_pairs={{0,64},{64,128},{128,192},{192,0},{1,65},{65,129},{129,193},{193,1... | collective-permute-start | bytes 1179656 | tf_op jit(solution)/shard_map/ppermute | solution.py:339
  141.4 16.0 %collective-permute-start.18 = (bf16[384,512]{1,0:T(8,128)(2,1)}, bf16[384,512]{1,0:T(8,128)(2,1)S(1)}, u32[]{:S(2)}, u32[]{:S(2)}) collective-permute-start(bf16[384,512]{1,0:T(8,128)(2,1)} %get-tuple-element.54), channel_id=1, source_target_pairs={{0,192},{64,0},{128,64},{192,128},{1,193},{65,1},{129,65},{193,129... | collective-permute-start | bytes 1179656 | tf_op jit(solution)/shard_map/ppermute | solution.py:342
  147.5 19.2 %all-to-all-start.2 = ((bf16[32,24,128]{2,1,0:T(8,128)(2,1)}), bf16[32,24,128]{2,1,0:T(8,128)(2,1)}, u32[]{:S(2)}, u32[]{:S(2)}) async-start(bf16[32,24,128]{2,1,0:T(8,128)(2,1)} %bitcast.12), calls=%async_computation.2 | async-start | bytes 393216 | tf_op jit(solution)/shard_map/all_to_all | solution.py:350
  157.4 0.8 copy-start.3
  157.4 0.9 copy-start.4
  166.7 26.6 %all-to-all-start.3 = ((bf16[32,24,512]{2,1,0:T(8,128)(2,1)}), bf16[32,24,512]{2,1,0:T(8,128)(2,1)}, u32[]{:S(2)}, u32[]{:S(2)}) async-start(bf16[32,24,512]{2,1,0:T(8,128)(2,1)} %bitcast.20), calls=%async_computation.3 | async-start | bytes 1572864 | tf_op jit(solution)/shard_map/all_to_all | solution.py:350
  180.4 27.2 %collective-permute-start.21 = (bf16[3,192,2048]{2,1,0:T(8,128)(2,1)}, bf16[3,192,2048]{2,1,0:T(8,128)(2,1)}, u32[]{:S(2)}, u32[]{:S(2)}) collective-permute-start(bf16[3,192,2048]{2,1,0:T(8,128)(2,1)} %wgrad.3), channel_id=1, source_target_pairs={{0,1},{1,0},{2,3},{3,2},{4,5},{5,4},{6,7},{7,6},{8,9},{9,8},{10,11... | collective-permute-start | bytes 7077896 | tf_op jit(solution)/shard_map/ppermute | solution.py:345
  196.1 1.7 collective-permute-start.20
  196.1 8.2 %collective-permute-start.22 = (bf16[144,512]{1,0:T(8,128)(2,1)}, bf16[144,512]{1,0:T(8,128)(2,1)}, u32[]{:S(2)}, u32[]{:S(2)}) collective-permute-start(bf16[144,512]{1,0:T(8,128)(2,1)} %get-tuple-element.69.refs_0_), channel_id=1, source_target_pairs={{0,64},{64,128},{128,192},{192,0},{1,65},{65,129},{129,193},{193,1... | collective-permute-start | bytes 442376 | tf_op jit(solution)/shard_map/ppermute | solution.py:339
  197.9 7.0 %collective-permute-start.25 = (bf16[144,512]{1,0:T(8,128)(2,1)}, bf16[144,512]{1,0:T(8,128)(2,1)}, u32[]{:S(2)}, u32[]{:S(2)}) collective-permute-start(bf16[144,512]{1,0:T(8,128)(2,1)} %collective-permute-done.20.refs_1_), channel_id=1, source_target_pairs={{0,192},{64,0},{128,64},{192,128},{1,193},{65,1},{129,65},{193,129... | collective-permute-start | bytes 442376 | tf_op jit(solution)/shard_map/ppermute | solution.py:342
  199.4 13.0 %collective-permute-start.24 = (bf16[144,512]{1,0:T(8,128)(2,1)}, bf16[144,512]{1,0:T(8,128)(2,1)}, u32[]{:S(2)}, u32[]{:S(2)}) collective-permute-start(bf16[144,512]{1,0:T(8,128)(2,1)} %get-tuple-element.69.refs_0_), channel_id=1, source_target_pairs={{0,192},{64,0},{128,64},{192,128},{1,193},{65,1},{129,65},{193,129... | collective-permute-start | bytes 442376 | tf_op jit(solution)/shard_map/ppermute | solution.py:342
  199.4 13.0 %collective-permute-start.23 = (bf16[144,512]{1,0:T(8,128)(2,1)}, bf16[144,512]{1,0:T(8,128)(2,1)}, u32[]{:S(2)}, u32[]{:S(2)}) collective-permute-start(bf16[144,512]{1,0:T(8,128)(2,1)} %collective-permute-done.20.refs_1_), channel_id=1, source_target_pairs={{0,64},{64,128},{128,192},{192,0},{1,65},{65,129},{129,193},{193,1... | collective-permute-start | bytes 442376 | tf_op jit(solution)/shard_map/ppermute | solution.py:339
  204.3 8.1 %collective-permute-start.26 = (bf16[144,512]{1,0:T(8,128)(2,1)}, bf16[144,512]{1,0:T(8,128)(2,1)}, u32[]{:S(2)}, u32[]{:S(2)}) collective-permute-start(bf16[144,512]{1,0:T(8,128)(2,1)} %collective-permute-done.22.refs_2_), channel_id=1, source_target_pairs={{0,64},{64,128},{128,192},{192,0},{1,65},{65,129},{129,193},{193,1... | collective-permute-start | bytes 442376 | tf_op jit(solution)/shard_map/ppermute | solution.py:339
  204.9 7.5 %collective-permute-start.27 = (bf16[144,512]{1,0:T(8,128)(2,1)}, bf16[144,512]{1,0:T(8,128)(2,1)}, u32[]{:S(2)}, u32[]{:S(2)}) collective-permute-start(bf16[144,512]{1,0:T(8,128)(2,1)} %collective-permute-done.25.refs_5_), channel_id=1, source_target_pairs={{0,192},{64,0},{128,64},{192,128},{1,193},{65,1},{129,65},{193,129... | collective-permute-start | bytes 442376 | tf_op jit(solution)/shard_map/ppermute | solution.py:342

commit v5 on v3

--- a/solution.py
+++ b/solution.py
@@ -55,7 +55,7 @@
         in_specs=[SMEM] + [VMEM] * (len(args) - 1),
         out_specs=[VMEM] * len(outs),
         scratch_shapes=list(scratch),
-        compiler_params=pltpu.CompilerParams(vmem_limit_bytes=60 * 1024 * 1024),
+        compiler_params=pltpu.CompilerParams(vmem_limit_bytes=40 * 1024 * 1024),
         cost_estimate=pl.CostEstimate(
             flops=COST[name] * 100_000_000_000, transcendentals=0, bytes_accessed=0
         ),
@@ -424,12 +424,15 @@
         name="wgrad",
     )
     r, w_other = tie((r, w_other))
-    dgot = swap(w_other)
     qa, sib = call(
         collect_body, [((144, CH), BF)] * 2, (pos, ids, pk, r, cb), name="collect"
     )
-    qb = swap(sib)
-    parts = spread_halves(qa, qb)
+    la, ra = up(qa), down(qa)
+    sib, la, ra = tie((sib, la, ra))
+    qb, w_other = tie((swap(sib), w_other))
+    dgot = swap(w_other)
+    lb, rb = up(qb), down(qb)
+    parts = (qa, qb, la, lb, ra, rb, up(la), down(rb))
     qb, w_own = tie((qb, w_own))
     dwg, dwu, dwd = call(
         wgrad_join_body, [((192, D), BF)] * 3, (pos, w_own, dgot), name="wgrad_join"

time: 206 us -> 209 us (1.015)
  Pallas kernels: 70.5 us -> 46.4 us
  local copies, waits for them, and re-layouts: 6.28 us -> 25.8 us
  waiting for transfers between devices: 64.2 us -> 70.9 us
    pallas_call x16, Pallas kernels: 70.5 us -> 46.4 us  [call(): pl.pallas_call(body, out_shape=[jax.ShapeDtypeStruct(s, t) for s, t in ou...]
    unnamed x12 -> x74, local copies, waits for them, and re-layouts: 2.61 us -> 22.2 us
    ppermute x11, waiting for transfers between devices: 11.9 us -> 17.9 us  [down(): return lax.ppermute(x, 'dp', down_ring)]
    ppermute x11, waiting for transfers between devices: 14.1 us -> 17.1 us  [up(): return lax.ppermute(x, 'dp', up_ring)]
  transfers between devices with their start and end apart: 32 -> 32, of which waited for: 16 -> 18; matrix products, arithmetic and copies ran while one was open for 2% -> 2% of each run, Pallas kernels for 26% -> 15%
where the time goes in v5:
time: 209 us; the launch traced here: 207 us
  waiting for transfers between devices  70.9 us (34%)
  starting transfers between devices  63.2 us (30%)
  Pallas kernels  46.4 us (22%)
  local copies, waits for them, and re-layouts  25.8 us (12%)
    pallas_call x16, Pallas kernels, call(): pl.pallas_call(body, out_shape=[jax.ShapeDtypeStruct(s, t) for s, t in ou...  46.4 us
    all_to_all x4, starting transfers between devices, exchange(): lax.all_to_all(x, 'expert', split_axis=0, concat_axis=0, axis_index_group...  31.2 us
    all_to_all x4, waiting for transfers between devices, exchange(): lax.all_to_all(x, 'expert', split_axis=0, concat_axis=0, axis_index_group...  30 us
    ppermute x11, starting transfers between devices, down(): return lax.ppermute(x, 'dp', down_ring)  26.3 us
    unnamed x74, local copies, waits for them, and re-layouts  22.2 us
    ppermute x11, waiting for transfers between devices, down(): return lax.ppermute(x, 'dp', down_ring)  17.9 us
    ppermute x11, waiting for transfers between devices, up(): return lax.ppermute(x, 'dp', up_ring)  17.1 us
    ppermute x6, waiting for transfers between devices, swap(): return lax.ppermute(x, 'expert', cores)  5.89 us
  transfers between devices with their start and end apart: 32, of which 18 were waited for; matrix products, arithmetic and copies ran while one was open for 2% of the time, Pallas kernels for 15%

profile of v5, /device:TPU:2, one launch (start us, length us, event | category | flops | bytes accessed | tf_op | source)
XLA Modules:
  0.0 207.3 jit_solution(17688292948937595766)
XLA Ops:
  0.7 1.2 copy-done.8
  1.9 1.2 copy-done.9
  5.2 1.5 collective-permute-done.pk
  6.8 2.2 %send.3 = bf16[768,512]{1,0:T(8,128)(2,1)} custom-call(s32[2]{0:T(128)S(1)} %pad_add_fusion.pos, s32[8,128]{1,0:T(8,128)S(1)} %bitcast.27, bf16[8,128]{1,0:T(8,128)(2,1)S(1)} %bitcast.31, bf16[272,512]{1,0:T(8,128)(2,1)S(1)} %collective-permute-done.pk, bf16[128,4096]{1,0:T(8,128)(2,1)S(1)} %copy-done.8), custom_call_target="tpu_custom_call" | custom-call | flops 299999985664 | tf_op jit(solution)/shard_map/send/pallas_call | solution.py:52
  8.9 11.8 %all-to-all-start = ((bf16[32,24,512]{2,1,0:T(8,128)(2,1)}), bf16[32,24,512]{2,1,0:T(8,128)(2,1)}, u32[]{:S(2)}, u32[]{:S(2)}) async-start(bf16[32,24,512]{2,1,0:T(8,128)(2,1)} %bitcast.4), calls=%async_computation | async-start | bytes 1572864 | tf_op jit(solution)/shard_map/all_to_all | solution.py:351
  20.8 1.4 copy-done.4
  22.2 1.4 copy-done.6
  23.6 2.1 %weight_send.1 = bf16[3,192,2048]{2,1,0:T(8,128)(2,1)} custom-call(s32[2]{0:T(128)S(1)} %pad_add_fusion.pos, bf16[192,4096]{1,0:T(8,128)(2,1)S(1)} %bitcast.20, bf16[192,4096]{1,0:T(8,128)(2,1)S(1)} %bitcast.22, bf16[192,4096]{1,0:T(8,128)(2,1)S(1)} %bitcast.24), custom_call_target="tpu_custom_call" | custom-call | flops 399999991808 | tf_op jit(solution)/shard_map/weight_send/pallas_call | solution.py:52
  25.7 2.3 %send.2 = bf16[768,512]{1,0:T(8,128)(2,1)} custom-call(s32[2]{0:T(128)S(1)} %pad_add_fusion.pos, s32[8,128]{1,0:T(8,128)S(1)} %bitcast.28, bf16[8,128]{1,0:T(8,128)(2,1)S(1)} %bitcast.32, bf16[272,512]{1,0:T(8,128)(2,1)S(1)} %copy-done.12, bf16[128,4096]{1,0:T(8,128)(2,1)S(1)} %copy-done.10), custom_call_target="tpu_custom_call" | custom-call | flops 299999985664 | tf_op jit(solution)/shard_map/send/pallas_call | solution.py:52
  28.0 15.5 %all-to-all-done = bf16[32,24,512]{2,1,0:T(8,128)(2,1)} async-done(((bf16[32,24,512]{2,1,0:T(8,128)(2,1)}), bf16[32,24,512]{2,1,0:T(8,128)(2,1)}, u32[]{:S(2)}, u32[]{:S(2)}) %all-to-all-start) | async-done | bytes 786464 | tf_op jit(solution)/shard_map/all_to_all | solution.py:351
  43.5 3.0 %collective-permute-start.2 = (bf16[768,512]{1,0:T(8,128)(2,1)}, bf16[768,512]{1,0:T(8,128)(2,1)S(1)}, u32[]{:S(2)}, u32[]{:S(2)}) collective-permute-start(bf16[768,512]{1,0:T(8,128)(2,1)} %bitcast.5.x0.refs_0_), channel_id=1, source_target_pairs={{0,192},{64,0},{128,64},{192,128},{1,193},{65,1},{129,65},{193,129... | collective-permute-start | bytes 2359304 | tf_op jit(solution)/shard_map/ppermute | solution.py:343
  46.6 5.7 %all-to-all-start.1 = ((bf16[32,24,512]{2,1,0:T(8,128)(2,1)}), bf16[32,24,512]{2,1,0:T(8,128)(2,1)}, u32[]{:S(2)}, u32[]{:S(2)}) async-start(bf16[32,24,512]{2,1,0:T(8,128)(2,1)} %bitcast.9), calls=%async_computation.1 | async-start | bytes 1572864 | tf_op jit(solution)/shard_map/all_to_all | solution.py:351
  52.3 9.8 %collective-permute-done.2.x2.refs_2_ = bf16[768,512]{1,0:T(8,128)(2,1)S(1)} collective-permute-done((bf16[768,512]{1,0:T(8,128)(2,1)}, bf16[768,512]{1,0:T(8,128)(2,1)S(1)}, u32[]{:S(2)}, u32[]{:S(2)}) %collective-permute-start.2) | collective-permute-done | bytes 786464 | tf_op jit(solution)/shard_map/ppermute | solution.py:343
  62.9 3.6 %collective-permute-start.4 = (bf16[384,512]{1,0:T(8,128)(2,1)}, bf16[384,512]{1,0:T(8,128)(2,1)}, u32[]{:S(2)}, u32[]{:S(2)}) collective-permute-start(bf16[384,512]{1,0:T(8,128)(2,1)} %slice.25), channel_id=1, source_target_pairs={{0,192},{64,0},{128,64},{192,128},{1,193},{65,1},{129,65},{193,129... | collective-permute-start | bytes 1179656 | tf_op jit(solution)/shard_map/ppermute | solution.py:343
  66.5 0.8 slice.24
  67.3 1.4 copy-done.5
  68.7 1.4 copy-done.7
  70.1 2.0 weight_join.1
  72.1 1.6 copy-done.26
  73.8 1.1 copy-done.29
  74.9 2.1 fusion
  77.0 3.2 %collective-permute-start.9 = (bf16[384,512]{1,0:T(8,128)(2,1)}, bf16[384,512]{1,0:T(8,128)(2,1)}, u32[]{:S(2)}, u32[]{:S(2)}) collective-permute-start(bf16[384,512]{1,0:T(8,128)(2,1)} %bitcast.10.refs_0_.refs_5_), channel_id=1, source_target_pairs={{0,192},{64,0},{128,64},{192,128},{1,193},{65,1},{129,65},{193,129... | collective-permute-start | bytes 1179656 | tf_op jit(solution)/shard_map/ppermute | solution.py:343
  80.2 3.2 %collective-permute-start.10 = (bf16[384,512]{1,0:T(8,128)(2,1)}, bf16[384,512]{1,0:T(8,128)(2,1)}, u32[]{:S(2)}, u32[]{:S(2)}) collective-permute-start(bf16[384,512]{1,0:T(8,128)(2,1)} %bitcast.11.refs_1_.refs_6_), channel_id=1, source_target_pairs={{0,192},{64,0},{128,64},{192,128},{1,193},{65,1},{129,65},{193,129... | collective-permute-start | bytes 1179656 | tf_op jit(solution)/shard_map/ppermute | solution.py:343
  83.5 1.9 copy-done.27
  85.3 6.2 %gate_up.1.gu_a = f32[768,768]{1,0:T(8,128)} custom-call(s32[2]{0:T(128)S(1)} %pad_add_fusion.pos, bf16[768,512]{1,0:T(8,128)(2,1)} %bitcast.5.x0.refs_0_, bf16[768,512]{1,0:T(8,128)(2,1)S(1)} %collective-permute-done.1.x1.refs_1_, bf16[768,512]{1,0:T(8,128)(2,1)S(1)} %collective-permute-done.2.x2.refs_2_, ...), custom_call_target="tpu_custom_call" | custom-call | flops 799999983616 | tf_op jit(solution)/shard_map/gate_up/pallas_call | solution.py:52
  91.5 2.1 %collective-permute-done.7.refs_2_.refs_7_ = bf16[384,512]{1,0:T(8,128)(2,1)} collective-permute-done((bf16[384,512]{1,0:T(8,128)(2,1)}, bf16[384,512]{1,0:T(8,128)(2,1)}, u32[]{:S(2)}, u32[]{:S(2)}) %collective-permute-start.7) | collective-permute-done | bytes 393248 | tf_op jit(solution)/shard_map/ppermute | solution.py:340
  93.6 0.8 collective-permute-done.10.refs_5_.refs_10_
  94.4 3.7 %collective-permute-start.12 = (bf16[384,512]{1,0:T(8,128)(2,1)}, bf16[384,512]{1,0:T(8,128)(2,1)}, u32[]{:S(2)}, u32[]{:S(2)}) collective-permute-start(bf16[384,512]{1,0:T(8,128)(2,1)} %collective-permute-done.10.refs_5_.refs_10_), channel_id=1, source_target_pairs={{0,192},{64,0},{128,64},{192,128},{1,193},{65,1},{129,65},{193,129... | collective-permute-start | bytes 1179656 | tf_op jit(solution)/shard_map/ppermute | solution.py:343
  98.1 1.0 collective-permute-done.8.refs_3_.refs_8_
  99.1 3.0 %back_near.1.acc = f32[768,384]{1,0:T(8,128)S(1)} custom-call(s32[2]{0:T(128)S(1)} %pad_add_fusion.pos, bf16[384,512]{1,0:T(8,128)(2,1)} %bitcast.10.refs_0_.refs_5_, bf16[384,512]{1,0:T(8,128)(2,1)} %bitcast.11.refs_1_.refs_6_, bf16[384,512]{1,0:T(8,128)(2,1)} %collective-permute-done.7.refs_2_.refs_7_, ...), custom_call_target="tpu_custom_call" | custom-call | flops 499999997952 | tf_op jit(solution)/shard_map/back_near/pallas_call | solution.py:52
  102.2 4.1 %collective-permute-done.11.xa.refs_11_ = bf16[384,512]{1,0:T(8,128)(2,1)} collective-permute-done((bf16[384,512]{1,0:T(8,128)(2,1)}, bf16[384,512]{1,0:T(8,128)(2,1)}, u32[]{:S(2)}, u32[]{:S(2)}) %collective-permute-start.11) | collective-permute-done | bytes 393248 | tf_op jit(solution)/shard_map/ppermute | solution.py:340
  106.3 1.9 back.1.bk_a
  108.2 2.8 %collective-permute-done.13.bk_b = f32[768,384]{1,0:T(8,128)S(1)} collective-permute-done((f32[768,384]{1,0:T(8,128)S(1)}, f32[768,384]{1,0:T(8,128)S(1)}, u32[]{:S(2)}, u32[]{:S(2)}) %collective-permute-start.13) | collective-permute-done | bytes 1179680 | tf_op jit(solution)/shard_map/ppermute | solution.py:346
  111.1 5.4 %mid.1 = (bf16[768,768]{1,0:T(8,128)(2,1)S(1)}, bf16[768,384]{1,0:T(8,128)(2,1)S(1)}, bf16[768,128]{1,0:T(8,128)(2,1)}, bf16[384,512]{1,0:T(8,128)(2,1)}, bf16[384,512]{1,0:T(8,128)(2,1)}) custom-call(s32[2]{0:T(128)S(1)} %pad_add_fusion.pos, f32[768,768]{1,0:T(8,128)} %gate_up.1.gu_a, f32[768,768]{1,0:T(8,128)} %collective-permute-done.6.gu_b, ...), custom_call_target="tpu_custom_call" | custom-call | flops 799999983616 | tf_op jit(solution)/shard_map/mid/pallas_call | solution.py:52
  116.5 0.8 copy-done.35
  117.3 3.2 %collective-permute-start.16 = (bf16[384,512]{1,0:T(8,128)(2,1)}, bf16[384,512]{1,0:T(8,128)(2,1)}, u32[]{:S(2)}, u32[]{:S(2)}) collective-permute-start(bf16[384,512]{1,0:T(8,128)(2,1)} %get-tuple-element.59), channel_id=1, source_target_pairs={{0,192},{64,0},{128,64},{192,128},{1,193},{65,1},{129,65},{193,129... | collective-permute-start | bytes 1179656 | tf_op jit(solution)/shard_map/ppermute | solution.py:343
  120.5 2.6 %rest.1 = (bf16[384,512]{1,0:T(8,128)(2,1)S(1)}, bf16[384,512]{1,0:T(8,128)(2,1)}, bf16[384,512]{1,0:T(8,128)(2,1)}, bf16[384,512]{1,0:T(8,128)(2,1)S(1)}, bf16[768,512]{1,0:T(8,128)(2,1)S(1)}) custom-call(s32[2]{0:T(128)S(1)} %pad_add_fusion.pos, bf16[768,768]{1,0:T(8,128)(2,1)S(1)} %get-tuple-element.67.both, bf16[2,384,2048]{2,1,0:T(8,128)(2,1)S(1)} %copy-done.28), custom_call_target="tpu_custom_call" | custom-call | flops 399999991808 | tf_op jit(solution)/shard_map/rest/pallas_call | solution.py:52
  123.2 0.9 copy-done.24
  124.5 1.6 collective-permute-start.19
  126.1 4.7 %collective-permute-done.15.r2 = bf16[384,512]{1,0:T(8,128)(2,1)} collective-permute-done((bf16[384,512]{1,0:T(8,128)(2,1)}, bf16[384,512]{1,0:T(8,128)(2,1)}, u32[]{:S(2)}, u32[]{:S(2)}) %collective-permute-start.15) | collective-permute-done | bytes 393248 | tf_op jit(solution)/shard_map/ppermute | solution.py:340
  130.8 1.3 pass_on.1
  132.5 3.0 %collective-permute-start.18 = (bf16[384,512]{1,0:T(8,128)(2,1)S(1)}, bf16[384,512]{1,0:T(8,128)(2,1)S(1)}, u32[]{:S(2)}, u32[]{:S(2)}) collective-permute-start(bf16[384,512]{1,0:T(8,128)(2,1)S(1)} %get-tuple-element.61), channel_id=1, source_target_pairs={{0,192},{64,0},{128,64},{192,128},{1,193},{65,1},{129,65},{193,129... | collective-permute-start | bytes 1179656 | tf_op jit(solution)/shard_map/ppermute | solution.py:343
  135.6 3.7 %collective-permute-done.19.pb = bf16[384,512]{1,0:T(8,128)(2,1)} collective-permute-done((bf16[384,512]{1,0:T(8,128)(2,1)}, bf16[384,512]{1,0:T(8,128)(2,1)}, u32[]{:S(2)}, u32[]{:S(2)}) %collective-permute-start.19) | collective-permute-done | bytes 393248 | tf_op jit(solution)/shard_map/ppermute | solution.py:340
  139.2 7.2 %all-to-all-start.2 = ((bf16[32,24,128]{2,1,0:T(8,128)(2,1)}), bf16[32,24,128]{2,1,0:T(8,128)(2,1)}, u32[]{:S(2)}, u32[]{:S(2)}) async-start(bf16[32,24,128]{2,1,0:T(8,128)(2,1)} %bitcast.12), calls=%async_computation.2 | async-start | bytes 393216 | tf_op jit(solution)/shard_map/all_to_all | solution.py:351
  146.7 1.1 copy-done.25
  147.9 2.3 %finish.1 = bf16[768,512]{1,0:T(8,128)(2,1)} custom-call(s32[2]{0:T(128)S(1)} %pad_add_fusion.pos, bf16[768,512]{1,0:T(8,128)(2,1)S(1)} %copy-done.25, bf16[384,512]{1,0:T(8,128)(2,1)} %collective-permute-done.14.ma, bf16[384,512]{1,0:T(8,128)(2,1)S(1)} %collective-permute-done.17.pa, bf16[384,512]{1,0:T(8,128)(2,1)S(1)} %collective-permute-done.18.mb, ...), custom_call_target="tpu_custom_call" | custom-call | flops 199999995904 | tf_op jit(solution)/shard_map/finish/pallas_call | solution.py:52
  150.2 5.5 %all-to-all-done.2 = bf16[32,24,128]{2,1,0:T(8,128)(2,1)} async-done(((bf16[32,24,128]{2,1,0:T(8,128)(2,1)}), bf16[32,24,128]{2,1,0:T(8,128)(2,1)}, u32[]{:S(2)}, u32[]{:S(2)}) %all-to-all-start.2) | async-done | bytes 196640 | tf_op jit(solution)/shard_map/all_to_all | solution.py:351
  155.6 6.5 %all-to-all-start.3 = ((bf16[32,24,512]{2,1,0:T(8,128)(2,1)}), bf16[32,24,512]{2,1,0:T(8,128)(2,1)}, u32[]{:S(2)}, u32[]{:S(2)}) async-start(bf16[32,24,512]{2,1,0:T(8,128)(2,1)} %bitcast.14), calls=%async_computation.3 | async-start | bytes 1572864 | tf_op jit(solution)/shard_map/all_to_all | solution.py:351
  162.1 1.1 copy-done.36
  163.2 7.1 %wgrad.1 = (bf16[3,192,2048]{2,1,0:T(8,128)(2,1)S(1)}, bf16[3,192,2048]{2,1,0:T(8,128)(2,1)S(1)}) custom-call(s32[2]{0:T(128)S(1)} %pad_add_fusion.pos, bf16[768,768]{1,0:T(8,128)(2,1)S(1)} %copy-done.34, bf16[768,384]{1,0:T(8,128)(2,1)S(1)} %copy-done.36, bf16[768,512]{1,0:T(8,128)(2,1)} %bitcast.5.x0.refs_0_, ...), custom_call_target="tpu_custom_call" | custom-call | flops 1300000014336 | tf_op jit(solution)/shard_map/wgrad/pallas_call | solution.py:52
  170.3 1.4 copy-done
  171.7 1.4 copy-done.31
  173.1 9.0 %all-to-all-done.3 = bf16[32,24,512]{2,1,0:T(8,128)(2,1)} async-done(((bf16[32,24,512]{2,1,0:T(8,128)(2,1)}), bf16[32,24,512]{2,1,0:T(8,128)(2,1)}, u32[]{:S(2)}, u32[]{:S(2)}) %all-to-all-start.3) | async-done | bytes 786464 | tf_op jit(solution)/shard_map/all_to_all | solution.py:351
  182.1 2.2 %collect.1 = (bf16[144,512]{1,0:T(8,128)(2,1)S(1)}, bf16[144,512]{1,0:T(8,128)(2,1)S(1)}) custom-call(s32[2]{0:T(128)S(1)} %pad_add_fusion.pos, s32[8,128]{1,0:T(8,128)S(1)} %bitcast.29, bf16[272,512]{1,0:T(8,128)(2,1)S(1)} %copy-done.13, bf16[768,512]{1,0:T(8,128)(2,1)} %bitcast.15.r, bf16[768,128]{1,0:T(8,128)(2,1)} %bitcast.13.cb), custom_call_target="tpu_custom_call" | custom-call | flops 299999985664 | tf_op jit(solution)/shard_map/collect/pallas_call | solution.py:52
  184.8 1.6 collective-permute-start.20
  187.1 2.5 %collective-permute-done.21.refs_4_ = bf16[144,512]{1,0:T(8,128)(2,1)S(1)} collective-permute-done((bf16[144,512]{1,0:T(8,128)(2,1)S(1)}, bf16[144,512]{1,0:T(8,128)(2,1)S(1)}, u32[]{:S(2)}, u32[]{:S(2)}) %collective-permute-start.21) | collective-permute-done | bytes 147488 | tf_op jit(solution)/shard_map/ppermute | solution.py:343
  190.2 1.1 collective-permute-done.20.refs_2_
  191.3 1.5 collective-permute-done.22.refs_1_
  193.5 1.5 collective-permute-start.26
  195.3 4.0 %collective-permute-done.25.refs_5_ = bf16[144,512]{1,0:T(8,128)(2,1)} collective-permute-done((bf16[144,512]{1,0:T(8,128)(2,1)}, bf16[144,512]{1,0:T(8,128)(2,1)}, u32[]{:S(2)}, u32[]{:S(2)}) %collective-permute-start.25) | collective-permute-done | bytes 147488 | tf_op jit(solution)/shard_map/ppermute | solution.py:343
  199.4 1.8 collective-permute-start.27
  201.2 3.0 %wgrad_join.1 = (bf16[192,4096]{1,0:T(8,128)(2,1)}, bf16[192,4096]{1,0:T(8,128)(2,1)}, bf16[192,4096]{1,0:T(8,128)(2,1)}) custom-call(s32[2]{0:T(128)S(1)} %pad_add_fusion.pos, bf16[3,192,2048]{2,1,0:T(8,128)(2,1)S(1)} %copy-done.32, bf16[3,192,2048]{2,1,0:T(8,128)(2,1)S(1)} %collective-permute-done.23.got), custom_call_target="tpu_custom_call" | custom-call | flops 499999997952 | tf_op jit(solution)/shard_map/wgrad_join/pallas_call | solution.py:52
  204.2 0.8 collective-permute-done.27.refs_7_
  205.0 2.3 %assemble.1 = (bf16[128,4096]{1,0:T(8,128)(2,1)}, f32[8,128]{1,0:T(8,128)}) custom-call(s32[2]{0:T(128)S(1)} %pad_add_fusion.pos, bf16[8,128]{1,0:T(8,128)(2,1)S(1)} %bitcast.33, bf16[144,512]{1,0:T(8,128)(2,1)S(1)} %copy-done.15, bf16[144,512]{1,0:T(8,128)(2,1)} %collective-permute-done.22.refs_1_, bf16[144,512]{1,0:T(8,128)(2,1)} %collective-permute-done.20.refs_2_, ...), custom_call_target="tpu_custom_call" | custom-call | flops 199999995904 | tf_op jit(solution)/shard_map/assemble/pallas_call | solution.py:52
  (94 shorter events, 7.2 us)
Async XLA Ops:
  0.7 1.2 copy-start.8
  1.9 1.2 copy-start.9
  5.1 1.6 collective-permute-start
  6.7 2.2 %copy-start.11 = (bf16[272,512]{1,0:T(8,128)(2,1)}, bf16[272,512]{1,0:T(8,128)(2,1)S(1)}, u32[]{:S(2)}) copy-start(bf16[272,512]{1,0:T(8,128)(2,1)S(1)} %collective-permute-done.pk) | copy-start | bytes 835588
  8.9 11.8 %copy-start.2 = (bf16[1,192,4096]{2,1,0:T(8,128)(2,1)S(1)}, bf16[1,192,4096]{2,1,0:T(8,128)(2,1)}, u32[]{:S(2)}) copy-start(bf16[1,192,4096]{2,1,0:T(8,128)(2,1)} %param.11) | copy-start | bytes 4718596
  8.9 34.6 %all-to-all-start = ((bf16[32,24,512]{2,1,0:T(8,128)(2,1)}), bf16[32,24,512]{2,1,0:T(8,128)(2,1)}, u32[]{:S(2)}, u32[]{:S(2)}) async-start(bf16[32,24,512]{2,1,0:T(8,128)(2,1)} %bitcast.4), calls=%async_computation | async-start | bytes 1572864 | tf_op jit(solution)/shard_map/all_to_all | solution.py:351
  20.7 1.4 copy-start.4
  22.2 1.4 copy-start.6
  23.6 2.1 %copy-start.10 = (bf16[128,4096]{1,0:T(8,128)(2,1)S(1)}, bf16[128,4096]{1,0:T(8,128)(2,1)}, u32[]{:S(2)}) copy-start(bf16[128,4096]{1,0:T(8,128)(2,1)} %rows_ref.2) | copy-start | bytes 3145732
  23.6 2.1 %copy-start.12 = (bf16[272,512]{1,0:T(8,128)(2,1)S(1)}, bf16[272,512]{1,0:T(8,128)(2,1)}, u32[]{:S(2)}) copy-start(bf16[272,512]{1,0:T(8,128)(2,1)} %copy-done.11) | copy-start | bytes 835588
  23.6 2.1 %copy-start.19 = (s32[128,8]{0,1:T(8,128)S(1)}, s32[128,8]{0,1:T(8,128)}, u32[]{:S(2)}) copy-start(s32[128,8]{0,1:T(8,128)} %param.9) | copy-start | bytes 12292
  23.6 2.1 %copy-start.22 = (bf16[128,8]{0,1:T(8,128)(2,1)S(1)}, bf16[128,8]{0,1:T(8,128)(2,1)}, u32[]{:S(2)}) copy-start(bf16[128,8]{0,1:T(8,128)(2,1)} %param.10) | copy-start | bytes 6148
  25.7 41.6 %collective-permute-start.5 = (bf16[3,192,2048]{2,1,0:T(8,128)(2,1)}, bf16[3,192,2048]{2,1,0:T(8,128)(2,1)}, u32[]{:S(2)}, u32[]{:S(2)}) collective-permute-start(bf16[3,192,2048]{2,1,0:T(8,128)(2,1)} %weight_send.1), channel_id=1, source_target_pairs={{0,1},{1,0},{2,3},{3,2},{4,5},{5,4},{6,7},{7,6},{8,9},{9,8},{10,11... | collective-permute-start | bytes 7077896 | tf_op jit(solution)/shard_map/ppermute | solution.py:346
  43.5 18.6 %collective-permute-start.2 = (bf16[768,512]{1,0:T(8,128)(2,1)}, bf16[768,512]{1,0:T(8,128)(2,1)S(1)}, u32[]{:S(2)}, u32[]{:S(2)}) collective-permute-start(bf16[768,512]{1,0:T(8,128)(2,1)} %bitcast.5.x0.refs_0_), channel_id=1, source_target_pairs={{0,192},{64,0},{128,64},{192,128},{1,193},{65,1},{129,65},{193,129... | collective-permute-start | bytes 2359304 | tf_op jit(solution)/shard_map/ppermute | solution.py:343
  46.6 20.0 %collective-permute-start.1 = (bf16[768,512]{1,0:T(8,128)(2,1)}, bf16[768,512]{1,0:T(8,128)(2,1)S(1)}, u32[]{:S(2)}, u32[]{:S(2)}) collective-permute-start(bf16[768,512]{1,0:T(8,128)(2,1)} %bitcast.5.x0.refs_0_), channel_id=1, source_target_pairs={{0,64},{64,128},{128,192},{192,0},{1,65},{65,129},{129,193},{193,1... | collective-permute-start | bytes 2359304 | tf_op jit(solution)/shard_map/ppermute | solution.py:340
  46.6 20.7 %copy-start.3 = (bf16[1,192,4096]{2,1,0:T(8,128)(2,1)S(1)}, bf16[1,192,4096]{2,1,0:T(8,128)(2,1)}, u32[]{:S(2)}) copy-start(bf16[1,192,4096]{2,1,0:T(8,128)(2,1)} %param.11) | copy-start | bytes 4718596
  46.6 28.4 %all-to-all-start.1 = ((bf16[32,24,512]{2,1,0:T(8,128)(2,1)}), bf16[32,24,512]{2,1,0:T(8,128)(2,1)}, u32[]{:S(2)}, u32[]{:S(2)}) async-start(bf16[32,24,512]{2,1,0:T(8,128)(2,1)} %bitcast.9), calls=%async_computation.1 | async-start | bytes 1572864 | tf_op jit(solution)/shard_map/all_to_all | solution.py:351
  62.9 20.5 %collective-permute-start.4 = (bf16[384,512]{1,0:T(8,128)(2,1)}, bf16[384,512]{1,0:T(8,128)(2,1)}, u32[]{:S(2)}, u32[]{:S(2)}) collective-permute-start(bf16[384,512]{1,0:T(8,128)(2,1)} %slice.25), channel_id=1, source_target_pairs={{0,192},{64,0},{128,64},{192,128},{1,193},{65,1},{129,65},{193,129... | collective-permute-start | bytes 1179656 | tf_op jit(solution)/shard_map/ppermute | solution.py:343
  67.3 16.2 %collective-permute-start.3 = (bf16[384,512]{1,0:T(8,128)(2,1)}, bf16[384,512]{1,0:T(8,128)(2,1)}, u32[]{:S(2)}, u32[]{:S(2)}) collective-permute-start(bf16[384,512]{1,0:T(8,128)(2,1)} %slice.24), channel_id=1, source_target_pairs={{0,64},{64,128},{128,192},{192,0},{1,65},{65,129},{129,193},{193,1... | collective-permute-start | bytes 1179656 | tf_op jit(solution)/shard_map/ppermute | solution.py:340
  67.3 1.4 copy-start.5
  68.7 1.4 copy-start.7
  72.1 1.7 copy-start.26
  73.8 1.1 copy-start.29
  77.0 21.2 %collective-permute-start.9 = (bf16[384,512]{1,0:T(8,128)(2,1)}, bf16[384,512]{1,0:T(8,128)(2,1)}, u32[]{:S(2)}, u32[]{:S(2)}) collective-permute-start(bf16[384,512]{1,0:T(8,128)(2,1)} %bitcast.10.refs_0_.refs_5_), channel_id=1, source_target_pairs={{0,192},{64,0},{128,64},{192,128},{1,193},{65,1},{129,65},{193,129... | collective-permute-start | bytes 1179656 | tf_op jit(solution)/shard_map/ppermute | solution.py:343
  80.2 13.4 %collective-permute-start.7 = (bf16[384,512]{1,0:T(8,128)(2,1)}, bf16[384,512]{1,0:T(8,128)(2,1)}, u32[]{:S(2)}, u32[]{:S(2)}) collective-permute-start(bf16[384,512]{1,0:T(8,128)(2,1)} %bitcast.10.refs_0_.refs_5_), channel_id=1, source_target_pairs={{0,64},{64,128},{128,192},{192,0},{1,65},{65,129},{129,193},{193,1... | collective-permute-start | bytes 1179656 | tf_op jit(solution)/shard_map/ppermute | solution.py:340
  80.2 14.2 %collective-permute-start.10 = (bf16[384,512]{1,0:T(8,128)(2,1)}, bf16[384,512]{1,0:T(8,128)(2,1)}, u32[]{:S(2)}, u32[]{:S(2)}) collective-permute-start(bf16[384,512]{1,0:T(8,128)(2,1)} %bitcast.11.refs_1_.refs_6_), channel_id=1, source_target_pairs={{0,192},{64,0},{128,64},{192,128},{1,193},{65,1},{129,65},{193,129... | collective-permute-start | bytes 1179656 | tf_op jit(solution)/shard_map/ppermute | solution.py:343
  83.4 15.7 %collective-permute-start.8 = (bf16[384,512]{1,0:T(8,128)(2,1)}, bf16[384,512]{1,0:T(8,128)(2,1)}, u32[]{:S(2)}, u32[]{:S(2)}) collective-permute-start(bf16[384,512]{1,0:T(8,128)(2,1)} %bitcast.11.refs_1_.refs_6_), channel_id=1, source_target_pairs={{0,64},{64,128},{128,192},{192,0},{1,65},{65,129},{129,193},{193,1... | collective-permute-start | bytes 1179656 | tf_op jit(solution)/shard_map/ppermute | solution.py:340
  83.5 1.9 copy-start.27
  85.3 13.8 %copy-start.30 = (bf16[384,2048]{1,0:T(8,128)(2,1)S(1)}, bf16[384,2048]{1,0:T(8,128)(2,1)}, u32[]{:S(2)}) copy-start(bf16[384,2048]{1,0:T(8,128)(2,1)} %copy-done.29) | copy-start | bytes 4718596
  91.5 19.5 %collective-permute-start.6 = (f32[768,768]{1,0:T(8,128)}, f32[768,768]{1,0:T(8,128)}, u32[]{:S(2)}, u32[]{:S(2)}) collective-permute-start(f32[768,768]{1,0:T(8,128)} %gate_up.1.gu_a), channel_id=1, source_target_pairs={{0,1},{1,0},{2,3},{3,2},{4,5},{5,4},{6,7},{7,6},{8,9},{9,8},{10,11... | collective-permute-start | bytes 7077896 | tf_op jit(solution)/shard_map/ppermute | solution.py:346
  93.6 12.6 %collective-permute-start.11 = (bf16[384,512]{1,0:T(8,128)(2,1)}, bf16[384,512]{1,0:T(8,128)(2,1)}, u32[]{:S(2)}, u32[]{:S(2)}) collective-permute-start(bf16[384,512]{1,0:T(8,128)(2,1)} %collective-permute-done.7.refs_2_.refs_7_), channel_id=1, source_target_pairs={{0,64},{64,128},{128,192},{192,0},{1,65},{65,129},{129,193},{193,1... | collective-permute-start | bytes 1179656 | tf_op jit(solution)/shard_map/ppermute | solution.py:340
  94.4 11.8 %collective-permute-start.12 = (bf16[384,512]{1,0:T(8,128)(2,1)}, bf16[384,512]{1,0:T(8,128)(2,1)}, u32[]{:S(2)}, u32[]{:S(2)}) collective-permute-start(bf16[384,512]{1,0:T(8,128)(2,1)} %collective-permute-done.10.refs_5_.refs_10_), channel_id=1, source_target_pairs={{0,192},{64,0},{128,64},{192,128},{1,193},{65,1},{129,65},{193,129... | collective-permute-start | bytes 1179656 | tf_op jit(solution)/shard_map/ppermute | solution.py:343
  106.3 4.8 %copy-start.28 = (bf16[2,384,2048]{2,1,0:T(8,128)(2,1)S(1)}, bf16[2,384,2048]{2,1,0:T(8,128)(2,1)}, u32[]{:S(2)}) copy-start(bf16[2,384,2048]{2,1,0:T(8,128)(2,1)} %copy-done.26) | copy-start | bytes 9437188
  108.1 2.9 %collective-permute-start.13 = (f32[768,384]{1,0:T(8,128)S(1)}, f32[768,384]{1,0:T(8,128)S(1)}, u32[]{:S(2)}, u32[]{:S(2)}) collective-permute-start(f32[768,384]{1,0:T(8,128)S(1)} %back.1.bk_a), channel_id=1, source_target_pairs={{0,1},{1,0},{2,3},{3,2},{4,5},{5,4},{6,7},{7,6},{8,9},{9,8},{10,11... | collective-permute-start | bytes 3538952 | tf_op jit(solution)/shard_map/ppermute | solution.py:346
  117.3 5.8 %copy-start.33 = (bf16[768,768]{1,0:T(8,128)(2,1)}, bf16[768,768]{1,0:T(8,128)(2,1)S(1)}, u32[]{:S(2)}) copy-start(bf16[768,768]{1,0:T(8,128)(2,1)S(1)} %get-tuple-element.67.both) | copy-start | bytes 3538948
  117.3 13.5 %collective-permute-start.15 = (bf16[384,512]{1,0:T(8,128)(2,1)}, bf16[384,512]{1,0:T(8,128)(2,1)}, u32[]{:S(2)}, u32[]{:S(2)}) collective-permute-start(bf16[384,512]{1,0:T(8,128)(2,1)} %get-tuple-element.57), channel_id=1, source_target_pairs={{0,64},{64,128},{128,192},{192,0},{1,65},{65,129},{129,193},{193,1... | collective-permute-start | bytes 1179656 | tf_op jit(solution)/shard_map/ppermute | solution.py:340
  117.3 13.5 %collective-permute-start.16 = (bf16[384,512]{1,0:T(8,128)(2,1)}, bf16[384,512]{1,0:T(8,128)(2,1)}, u32[]{:S(2)}, u32[]{:S(2)}) collective-permute-start(bf16[384,512]{1,0:T(8,128)(2,1)} %get-tuple-element.59), channel_id=1, source_target_pairs={{0,192},{64,0},{128,64},{192,128},{1,193},{65,1},{129,65},{193,129... | collective-permute-start | bytes 1179656 | tf_op jit(solution)/shard_map/ppermute | solution.py:343
  123.2 0.9 copy-start.24
  124.0 22.4 %collective-permute-start.14 = (bf16[384,512]{1,0:T(8,128)(2,1)}, bf16[384,512]{1,0:T(8,128)(2,1)}, u32[]{:S(2)}, u32[]{:S(2)}) collective-permute-start(bf16[384,512]{1,0:T(8,128)(2,1)} %get-tuple-element.55), channel_id=1, source_target_pairs={{0,192},{64,0},{128,64},{192,128},{1,193},{65,1},{129,65},{193,129... | collective-permute-start | bytes 1179656 | tf_op jit(solution)/shard_map/ppermute | solution.py:343
  124.5 14.8 %collective-permute-start.19 = (bf16[384,512]{1,0:T(8,128)(2,1)}, bf16[384,512]{1,0:T(8,128)(2,1)}, u32[]{:S(2)}, u32[]{:S(2)}) collective-permute-start(bf16[384,512]{1,0:T(8,128)(2,1)} %get-tuple-element.62), channel_id=1, source_target_pairs={{0,64},{64,128},{128,192},{192,0},{1,65},{65,129},{129,193},{193,1... | collective-permute-start | bytes 1179656 | tf_op jit(solution)/shard_map/ppermute | solution.py:340
  132.1 14.6 %collective-permute-start.17 = (bf16[384,512]{1,0:T(8,128)(2,1)S(1)}, bf16[384,512]{1,0:T(8,128)(2,1)S(1)}, u32[]{:S(2)}, u32[]{:S(2)}) collective-permute-start(bf16[384,512]{1,0:T(8,128)(2,1)S(1)} %get-tuple-element.60), channel_id=1, source_target_pairs={{0,64},{64,128},{128,192},{192,0},{1,65},{65,129},{129,193},{193,1... | collective-permute-start | bytes 1179656 | tf_op jit(solution)/shard_map/ppermute | solution.py:340
  132.5 14.2 %collective-permute-start.18 = (bf16[384,512]{1,0:T(8,128)(2,1)S(1)}, bf16[384,512]{1,0:T(8,128)(2,1)S(1)}, u32[]{:S(2)}, u32[]{:S(2)}) collective-permute-start(bf16[384,512]{1,0:T(8,128)(2,1)S(1)} %get-tuple-element.61), channel_id=1, source_target_pairs={{0,192},{64,0},{128,64},{192,128},{1,193},{65,1},{129,65},{193,129... | collective-permute-start | bytes 1179656 | tf_op jit(solution)/shard_map/ppermute | solution.py:343
  139.2 16.4 %all-to-all-start.2 = ((bf16[32,24,128]{2,1,0:T(8,128)(2,1)}), bf16[32,24,128]{2,1,0:T(8,128)(2,1)}, u32[]{:S(2)}, u32[]{:S(2)}) async-start(bf16[32,24,128]{2,1,0:T(8,128)(2,1)} %bitcast.12), calls=%async_computation.2 | async-start | bytes 393216 | tf_op jit(solution)/shard_map/all_to_all | solution.py:351
  146.7 1.1 copy-start.25
  150.2 11.9 %copy-start.34 = (bf16[768,768]{1,0:T(8,128)(2,1)S(1)}, bf16[768,768]{1,0:T(8,128)(2,1)}, u32[]{:S(2)}) copy-start(bf16[768,768]{1,0:T(8,128)(2,1)} %copy-done.33) | copy-start | bytes 3538948
  155.6 26.4 %all-to-all-start.3 = ((bf16[32,24,512]{2,1,0:T(8,128)(2,1)}), bf16[32,24,512]{2,1,0:T(8,128)(2,1)}, u32[]{:S(2)}, u32[]{:S(2)}) async-start(bf16[32,24,512]{2,1,0:T(8,128)(2,1)} %bitcast.14), calls=%async_computation.3 | async-start | bytes 1572864 | tf_op jit(solution)/shard_map/all_to_all | solution.py:351
  162.1 1.1 copy-start.36
  163.2 18.9 %copy-start.13 = (bf16[272,512]{1,0:T(8,128)(2,1)S(1)}, bf16[272,512]{1,0:T(8,128)(2,1)}, u32[]{:S(2)}) copy-start(bf16[272,512]{1,0:T(8,128)(2,1)} %copy-done.11) | copy-start | bytes 835588
  163.2 18.9 %copy-start.20 = (s32[128,8]{0,1:T(8,128)S(1)}, s32[128,8]{0,1:T(8,128)}, u32[]{:S(2)}) copy-start(s32[128,8]{0,1:T(8,128)} %param.9) | copy-start | bytes 12292
  170.3 1.4 copy-start
  171.7 1.4 copy-start.31
  182.1 10.7 %copy-start.1 = (bf16[3,192,2048]{2,1,0:T(8,128)(2,1)S(1)}, bf16[3,192,2048]{2,1,0:T(8,128)(2,1)}, u32[]{:S(2)}) copy-start(bf16[3,192,2048]{2,1,0:T(8,128)(2,1)} %copy-done) | copy-start | bytes 7077892
  182.1 19.1 %copy-start.32 = (bf16[3,192,2048]{2,1,0:T(8,128)(2,1)S(1)}, bf16[3,192,2048]{2,1,0:T(8,128)(2,1)}, u32[]{:S(2)}) copy-start(bf16[3,192,2048]{2,1,0:T(8,128)(2,1)} %copy-done.31) | copy-start | bytes 7077892
  184.3 5.2 %collective-permute-start.21 = (bf16[144,512]{1,0:T(8,128)(2,1)S(1)}, bf16[144,512]{1,0:T(8,128)(2,1)S(1)}, u32[]{:S(2)}, u32[]{:S(2)}) collective-permute-start(bf16[144,512]{1,0:T(8,128)(2,1)S(1)} %get-tuple-element.73.refs_0_), channel_id=1, source_target_pairs={{0,192},{64,0},{128,64},{192,128},{1,193},{65,1},{129,65},{193,129... | collective-permute-start | bytes 442376 | tf_op jit(solution)/shard_map/ppermute | solution.py:343
  184.8 6.5 %collective-permute-start.20 = (bf16[144,512]{1,0:T(8,128)(2,1)S(1)}, bf16[144,512]{1,0:T(8,128)(2,1)}, u32[]{:S(2)}, u32[]{:S(2)}) collective-permute-start(bf16[144,512]{1,0:T(8,128)(2,1)S(1)} %get-tuple-element.73.refs_0_), channel_id=1, source_target_pairs={{0,64},{64,128},{128,192},{192,0},{1,65},{65,129},{129,193},{193,1... | collective-permute-start | bytes 442376 | tf_op jit(solution)/shard_map/ppermute | solution.py:340
  191.3 1.5 collective-permute-start.22
  192.8 8.3 %collective-permute-start.23 = (bf16[3,192,2048]{2,1,0:T(8,128)(2,1)S(1)}, bf16[3,192,2048]{2,1,0:T(8,128)(2,1)S(1)}, u32[]{:S(2)}, u32[]{:S(2)}) collective-permute-start(bf16[3,192,2048]{2,1,0:T(8,128)(2,1)S(1)} %copy-done.1), channel_id=1, source_target_pairs={{0,1},{1,0},{2,3},{3,2},{4,5},{5,4},{6,7},{7,6},{8,9},{9,8},{10,11... | collective-permute-start | bytes 7077896 | tf_op jit(solution)/shard_map/ppermute | solution.py:346
  192.9 6.4 %collective-permute-start.25 = (bf16[144,512]{1,0:T(8,128)(2,1)}, bf16[144,512]{1,0:T(8,128)(2,1)}, u32[]{:S(2)}, u32[]{:S(2)}) collective-permute-start(bf16[144,512]{1,0:T(8,128)(2,1)} %collective-permute-done.22.refs_1_), channel_id=1, source_target_pairs={{0,192},{64,0},{128,64},{192,128},{1,193},{65,1},{129,65},{193,129... | collective-permute-start | bytes 442376 | tf_op jit(solution)/shard_map/ppermute | solution.py:343
  193.5 10.7 %collective-permute-start.26 = (bf16[144,512]{1,0:T(8,128)(2,1)}, bf16[144,512]{1,0:T(8,128)(2,1)}, u32[]{:S(2)}, u32[]{:S(2)}) collective-permute-start(bf16[144,512]{1,0:T(8,128)(2,1)} %collective-permute-done.20.refs_2_), channel_id=1, source_target_pairs={{0,64},{64,128},{128,192},{192,0},{1,65},{65,129},{129,193},{193,1... | collective-permute-start | bytes 442376 | tf_op jit(solution)/shard_map/ppermute | solution.py:340
  195.0 9.2 %collective-permute-start.24 = (bf16[144,512]{1,0:T(8,128)(2,1)}, bf16[144,512]{1,0:T(8,128)(2,1)}, u32[]{:S(2)}, u32[]{:S(2)}) collective-permute-start(bf16[144,512]{1,0:T(8,128)(2,1)} %collective-permute-done.22.refs_1_), channel_id=1, source_target_pairs={{0,64},{64,128},{128,192},{192,0},{1,65},{65,129},{129,193},{193,1... | collective-permute-start | bytes 442376 | tf_op jit(solution)/shard_map/ppermute | solution.py:340
  199.4 5.6 %collective-permute-start.27 = (bf16[144,512]{1,0:T(8,128)(2,1)}, bf16[144,512]{1,0:T(8,128)(2,1)}, u32[]{:S(2)}, u32[]{:S(2)}) collective-permute-start(bf16[144,512]{1,0:T(8,128)(2,1)} %collective-permute-done.25.refs_5_), channel_id=1, source_target_pairs={{0,192},{64,0},{128,64},{192,128},{1,193},{65,1},{129,65},{193,129... | collective-permute-start | bytes 442376 | tf_op jit(solution)/shard_map/ppermute | solution.py:343
  201.1 3.8 %copy-start.15 = (bf16[144,512]{1,0:T(8,128)(2,1)S(1)}, bf16[144,512]{1,0:T(8,128)(2,1)}, u32[]{:S(2)}) copy-start(bf16[144,512]{1,0:T(8,128)(2,1)} %copy-done.14) | copy-start | bytes 442372
  201.1 3.8 %copy-start.17 = (bf16[144,512]{1,0:T(8,128)(2,1)S(1)}, bf16[144,512]{1,0:T(8,128)(2,1)}, u32[]{:S(2)}) copy-start(bf16[144,512]{1,0:T(8,128)(2,1)} %copy-done.16) | copy-start | bytes 442372
  201.2 3.8 %copy-start.23 = (bf16[128,8]{0,1:T(8,128)(2,1)S(1)}, bf16[128,8]{0,1:T(8,128)(2,1)}, u32[]{:S(2)}) copy-start(bf16[128,8]{0,1:T(8,128)(2,1)} %param.10) | copy-start | bytes 6148
  (5 other events, 3.5 us)

commit v6 on v3

--- a/solution.py
+++ b/solution.py
@@ -47,6 +47,8 @@
     "wgrad": 13, "wgrad_join": 5, "finish": 2, "collect": 3, "assemble": 2,
 }
 
+CHAIN = ("back", "mid", "rest", "pass_on", "finish", "assemble", "gate_up", "back_near")
+
 
 def call(body, outs, args, scratch=(), name=None):
     return pl.pallas_call(
@@ -55,7 +57,7 @@
         in_specs=[SMEM] + [VMEM] * (len(args) - 1),
         out_specs=[VMEM] * len(outs),
         scratch_shapes=list(scratch),
-        compiler_params=pltpu.CompilerParams(vmem_limit_bytes=60 * 1024 * 1024),
+        compiler_params=pltpu.CompilerParams(vmem_limit_bytes=(40 if name in CHAIN else 60) * 1024 * 1024),
         cost_estimate=pl.CostEstimate(
             flops=COST[name] * 100_000_000_000, transcendentals=0, bytes_accessed=0
         ),

time: 206 us -> 202 us (0.981)
  Pallas kernels: 70.5 us -> 60.1 us
  waiting for transfers between devices: 64.2 us -> 70.5 us
    pallas_call x16, Pallas kernels: 70.5 us -> 60.1 us  [call(): pl.pallas_call(body, out_shape=[jax.ShapeDtypeStruct(s, t) for s, t in ou...]
    ppermute x11, waiting for transfers between devices: 14.1 us -> 19.1 us  [up(): return lax.ppermute(x, 'dp', up_ring)]
  transfers between devices with their start and end apart: 32 -> 32, of which waited for: 16 -> 17; matrix products, arithmetic and copies ran while one was open for 2% -> 2% of each run, Pallas kernels for 26% -> 22%
where the time goes in v6:
time: 202 us; the launch traced here: 201 us
  waiting for transfers between devices  70.5 us (35%)
  starting transfers between devices  63 us (31%)
  Pallas kernels  60.1 us (30%)
  local copies, waits for them, and re-layouts  6.35 us (3%)
    pallas_call x16, Pallas kernels, call(): pl.pallas_call(body, out_shape=[jax.ShapeDtypeStruct(s, t) for s, t in ou...  60.1 us
    all_to_all x4, waiting for transfers between devices, exchange(): lax.all_to_all(x, 'expert', split_axis=0, concat_axis=0, axis_index_group...  33.1 us
    all_to_all x4, starting transfers between devices, exchange(): lax.all_to_all(x, 'expert', split_axis=0, concat_axis=0, axis_index_group...  30.9 us
    ppermute x11, starting transfers between devices, down(): return lax.ppermute(x, 'dp', down_ring)  27.5 us
    ppermute x11, waiting for transfers between devices, up(): return lax.ppermute(x, 'dp', up_ring)  19.1 us
    ppermute x11, waiting for transfers between devices, down(): return lax.ppermute(x, 'dp', down_ring)  11.9 us
    ppermute x6, waiting for transfers between devices, swap(): return lax.ppermute(x, 'expert', cores)  6.36 us
  transfers between devices with their start and end apart: 32, of which 17 were waited for; matrix products, arithmetic and copies ran while one was open for 2% of the time, Pallas kernels for 22%

profile of v6, /device:TPU:2, one launch (start us, length us, event | category | flops | bytes accessed | tf_op | source)
XLA Modules:
  0.0 201.4 jit_solution(10885182781140473875)
XLA Ops:
  0.6 0.6 pad_add_fusion.pos
  1.3 2.3 %pack.1 = bf16[272,512]{1,0:T(8,128)(2,1)} custom-call(s32[2]{0:T(128)} %pad_add_fusion.pos, s32[8,128]{1,0:T(8,128)} %bitcast.32, bf16[8,128]{1,0:T(8,128)(2,1)} %bitcast.20, bf16[128,4096]{1,0:T(8,128)(2,1)} %rows_ref.3, bf16[128,4096]{1,0:T(8,128)(2,1)} %rows_ref.2), custom_call_target="tpu_custom_call" | custom-call | flops 199999995904 | tf_op jit(solution)/shard_map/pack/pallas_call | solution.py:54
  3.6 0.0 collective-permute-start
  3.6 1.8 collective-permute-done.pk
  5.4 0.7 copy-done.11
  6.1 3.0 %send.3 = bf16[768,512]{1,0:T(8,128)(2,1)} custom-call(s32[2]{0:T(128)} %pad_add_fusion.pos, s32[8,128]{1,0:T(8,128)} %bitcast.33, bf16[8,128]{1,0:T(8,128)(2,1)} %bitcast.21, bf16[272,512]{1,0:T(8,128)(2,1)} %copy-done.11, bf16[128,4096]{1,0:T(8,128)(2,1)} %rows_ref.3), custom_call_target="tpu_custom_call" | custom-call | flops 299999985664 | tf_op jit(solution)/shard_map/send/pallas_call | solution.py:54
  9.1 11.7 %all-to-all-start = ((bf16[32,24,512]{2,1,0:T(8,128)(2,1)}), bf16[32,24,512]{2,1,0:T(8,128)(2,1)}, u32[]{:S(2)}, u32[]{:S(2)}) async-start(bf16[32,24,512]{2,1,0:T(8,128)(2,1)} %bitcast.25), calls=%async_computation | async-start | bytes 1572864 | tf_op jit(solution)/shard_map/all_to_all | solution.py:353
  20.7 4.0 %weight_send.1 = bf16[3,192,2048]{2,1,0:T(8,128)(2,1)} custom-call(s32[2]{0:T(128)} %pad_add_fusion.pos, bf16[192,4096]{1,0:T(8,128)(2,1)} %bitcast.26, bf16[192,4096]{1,0:T(8,128)(2,1)} %bitcast.28, bf16[192,4096]{1,0:T(8,128)(2,1)} %bitcast.30), custom_call_target="tpu_custom_call" | custom-call | flops 399999991808 | tf_op jit(solution)/shard_map/weight_send/pallas_call | solution.py:54
  24.7 3.2 %send.2 = bf16[768,512]{1,0:T(8,128)(2,1)} custom-call(s32[2]{0:T(128)} %pad_add_fusion.pos, s32[8,128]{1,0:T(8,128)} %bitcast.34, bf16[8,128]{1,0:T(8,128)(2,1)} %bitcast.22, bf16[272,512]{1,0:T(8,128)(2,1)} %copy-done.11, bf16[128,4096]{1,0:T(8,128)(2,1)} %rows_ref.2), custom_call_target="tpu_custom_call" | custom-call | flops 299999985664 | tf_op jit(solution)/shard_map/send/pallas_call | solution.py:54
  27.9 15.6 %all-to-all-done = bf16[32,24,512]{2,1,0:T(8,128)(2,1)} async-done(((bf16[32,24,512]{2,1,0:T(8,128)(2,1)}), bf16[32,24,512]{2,1,0:T(8,128)(2,1)}, u32[]{:S(2)}, u32[]{:S(2)}) %all-to-all-start) | async-done | bytes 786464 | tf_op jit(solution)/shard_map/all_to_all | solution.py:353
  43.5 3.0 %collective-permute-start.2 = (bf16[768,512]{1,0:T(8,128)(2,1)}, bf16[768,512]{1,0:T(8,128)(2,1)S(1)}, u32[]{:S(2)}, u32[]{:S(2)}) collective-permute-start(bf16[768,512]{1,0:T(8,128)(2,1)} %bitcast.5.x0.refs_0_), channel_id=1, source_target_pairs={{0,192},{64,0},{128,64},{192,128},{1,193},{65,1},{129,65},{193,129... | collective-permute-start | bytes 2359304 | tf_op jit(solution)/shard_map/ppermute | solution.py:345
  46.6 0.0 collective-permute-start.1
  46.6 5.6 %all-to-all-start.1 = ((bf16[32,24,512]{2,1,0:T(8,128)(2,1)}), bf16[32,24,512]{2,1,0:T(8,128)(2,1)}, u32[]{:S(2)}, u32[]{:S(2)}) async-start(bf16[32,24,512]{2,1,0:T(8,128)(2,1)} %bitcast.24), calls=%async_computation.1 | async-start | bytes 1572864 | tf_op jit(solution)/shard_map/all_to_all | solution.py:353
  52.2 10.0 %collective-permute-done.2.x2.refs_2_ = bf16[768,512]{1,0:T(8,128)(2,1)S(1)} collective-permute-done((bf16[768,512]{1,0:T(8,128)(2,1)}, bf16[768,512]{1,0:T(8,128)(2,1)S(1)}, u32[]{:S(2)}, u32[]{:S(2)}) %collective-permute-start.2) | collective-permute-done | bytes 786464 | tf_op jit(solution)/shard_map/ppermute | solution.py:345
  62.2 0.9 slice.25
  63.1 3.6 %collective-permute-start.4 = (bf16[384,512]{1,0:T(8,128)(2,1)}, bf16[384,512]{1,0:T(8,128)(2,1)}, u32[]{:S(2)}, u32[]{:S(2)}) collective-permute-start(bf16[384,512]{1,0:T(8,128)(2,1)} %slice.25), channel_id=1, source_target_pairs={{0,192},{64,0},{128,64},{192,128},{1,193},{65,1},{129,65},{193,129... | collective-permute-start | bytes 1179656 | tf_op jit(solution)/shard_map/ppermute | solution.py:345
  66.7 0.0 collective-permute-done.1.x1.refs_1_
  66.7 0.8 slice.24
  67.5 0.0 collective-permute-start.3
  67.5 5.6 %weight_join.1 = (bf16[2,384,2048]{2,1,0:T(8,128)(2,1)}, bf16[384,2048]{1,0:T(8,128)(2,1)}) custom-call(s32[2]{0:T(128)} %pad_add_fusion.pos, bf16[192,4096]{1,0:T(8,128)(2,1)} %bitcast.27, bf16[192,4096]{1,0:T(8,128)(2,1)} %bitcast.29, bf16[192,4096]{1,0:T(8,128)(2,1)} %bitcast.31, bf16[3,192,2048]{2,1,0:T(8,128)(2,1)} %collective-permute-done.5.got), custom_call_target="tpu_custom_call" | custom-call | flops 599999971328 | tf_op jit(solution)/shard_map/weight_join/pallas_call | solution.py:54
  73.0 0.5 all-to-all-done.1
  73.5 2.1 %fusion = (bf16[16,24,512]{2,1,0:T(8,128)(2,1)}, bf16[16,24,512]{2,1,0:T(8,128)(2,1)}) fusion(bf16[32,24,512]{2,1,0:T(8,128)(2,1)} %all-to-all-done.1), kind=kLoop, calls=%fused_computation.1 | loop fusion | bytes 1572864 | tf_op jit(solution)/shard_map/slice | solution.py:395
  75.6 3.0 %collective-permute-start.9 = (bf16[384,512]{1,0:T(8,128)(2,1)}, bf16[384,512]{1,0:T(8,128)(2,1)}, u32[]{:S(2)}, u32[]{:S(2)}) collective-permute-start(bf16[384,512]{1,0:T(8,128)(2,1)} %bitcast.10.refs_0_.refs_5_), channel_id=1, source_target_pairs={{0,192},{64,0},{128,64},{192,128},{1,193},{65,1},{129,65},{193,129... | collective-permute-start | bytes 1179656 | tf_op jit(solution)/shard_map/ppermute | solution.py:345
  78.5 3.2 %collective-permute-start.10 = (bf16[384,512]{1,0:T(8,128)(2,1)}, bf16[384,512]{1,0:T(8,128)(2,1)}, u32[]{:S(2)}, u32[]{:S(2)}) collective-permute-start(bf16[384,512]{1,0:T(8,128)(2,1)} %bitcast.11.refs_1_.refs_6_), channel_id=1, source_target_pairs={{0,192},{64,0},{128,64},{192,128},{1,193},{65,1},{129,65},{193,129... | collective-permute-start | bytes 1179656 | tf_op jit(solution)/shard_map/ppermute | solution.py:345
  81.8 1.9 copy-done.6
  83.7 6.1 %gate_up.1.gu_a = f32[768,768]{1,0:T(8,128)} custom-call(s32[2]{0:T(128)S(1)} %copy-done.4, bf16[768,512]{1,0:T(8,128)(2,1)} %bitcast.5.x0.refs_0_, bf16[768,512]{1,0:T(8,128)(2,1)S(1)} %collective-permute-done.1.x1.refs_1_, bf16[768,512]{1,0:T(8,128)(2,1)S(1)} %collective-permute-done.2.x2.refs_2_, bf16[384,512]{1,0:T(8,128)(2,1)} %collective-permute-done.3.xa.refs_3_, ...), custom_call_target="tpu_custom_call" | custom-call | flops 799999983616 | tf_op jit(solution)/shard_map/gate_up/pallas_call | solution.py:54
  89.8 0.0 collective-permute-start.6
  89.9 1.9 collective-permute-done.7.refs_2_.refs_7_
  91.8 0.8 collective-permute-done.10.refs_5_.refs_10_
  92.6 3.7 %collective-permute-start.12 = (bf16[384,512]{1,0:T(8,128)(2,1)}, bf16[384,512]{1,0:T(8,128)(2,1)}, u32[]{:S(2)}, u32[]{:S(2)}) collective-permute-start(bf16[384,512]{1,0:T(8,128)(2,1)} %collective-permute-done.10.refs_5_.refs_10_), channel_id=1, source_target_pairs={{0,192},{64,0},{128,64},{192,128},{1,193},{65,1},{129,65},{193,129... | collective-permute-start | bytes 1179656 | tf_op jit(solution)/shard_map/ppermute | solution.py:345
  96.3 0.9 collective-permute-done.8.refs_3_.refs_8_
  97.2 3.0 %back_near.1.acc = f32[768,384]{1,0:T(8,128)S(1)} custom-call(s32[2]{0:T(128)S(1)} %copy-done.4, bf16[384,512]{1,0:T(8,128)(2,1)} %bitcast.10.refs_0_.refs_5_, bf16[384,512]{1,0:T(8,128)(2,1)} %bitcast.11.refs_1_.refs_6_, bf16[384,512]{1,0:T(8,128)(2,1)} %collective-permute-done.7.refs_2_.refs_7_, bf16[384,512]{1,0:T(8,128)(2,1)} %collective-permute-done.8.refs_3_.refs_8_, ...), custom_call_target="tpu_custom_call" | custom-call | flops 499999997952 | tf_op jit(solution)/shard_map/back_near/pallas_call | solution.py:54
  100.2 4.3 %collective-permute-done.11.xa.refs_11_ = bf16[384,512]{1,0:T(8,128)(2,1)} collective-permute-done((bf16[384,512]{1,0:T(8,128)(2,1)}, bf16[384,512]{1,0:T(8,128)(2,1)}, u32[]{:S(2)}, u32[]{:S(2)}) %collective-permute-start.11) | collective-permute-done | bytes 393248 | tf_op jit(solution)/shard_map/ppermute | solution.py:342
  104.4 1.9 back.1.bk_a
  106.3 0.1 collective-permute-start.13
  106.4 2.8 %collective-permute-done.13.bk_b = f32[768,384]{1,0:T(8,128)S(1)} collective-permute-done((f32[768,384]{1,0:T(8,128)S(1)}, f32[768,384]{1,0:T(8,128)S(1)}, u32[]{:S(2)}, u32[]{:S(2)}) %collective-permute-start.13) | collective-permute-done | bytes 1179680 | tf_op jit(solution)/shard_map/ppermute | solution.py:348
  109.2 5.4 %mid.1 = (bf16[768,768]{1,0:T(8,128)(2,1)S(1)}, bf16[768,384]{1,0:T(8,128)(2,1)S(1)}, bf16[768,128]{1,0:T(8,128)(2,1)}, bf16[384,512]{1,0:T(8,128)(2,1)}, bf16[384,512]{1,0:T(8,128)(2,1)}) custom-call(s32[2]{0:T(128)S(1)} %copy-done.4, f32[768,768]{1,0:T(8,128)} %gate_up.1.gu_a, f32[768,768]{1,0:T(8,128)} %collective-permute-done.6.gu_b, ...), custom_call_target="tpu_custom_call" | custom-call | flops 799999983616 | tf_op jit(solution)/shard_map/mid/pallas_call | solution.py:54
  114.6 3.2 %collective-permute-start.16 = (bf16[384,512]{1,0:T(8,128)(2,1)}, bf16[384,512]{1,0:T(8,128)(2,1)}, u32[]{:S(2)}, u32[]{:S(2)}) collective-permute-start(bf16[384,512]{1,0:T(8,128)(2,1)} %get-tuple-element.54), channel_id=1, source_target_pairs={{0,192},{64,0},{128,64},{192,128},{1,193},{65,1},{129,65},{193,129... | collective-permute-start | bytes 1179656 | tf_op jit(solution)/shard_map/ppermute | solution.py:345
  117.8 2.6 %rest.1 = (bf16[384,512]{1,0:T(8,128)(2,1)S(1)}, bf16[384,512]{1,0:T(8,128)(2,1)}, bf16[384,512]{1,0:T(8,128)(2,1)}, bf16[384,512]{1,0:T(8,128)(2,1)S(1)}, bf16[768,512]{1,0:T(8,128)(2,1)S(1)}) custom-call(s32[2]{0:T(128)S(1)} %copy-done.4, bf16[768,768]{1,0:T(8,128)(2,1)S(1)} %get-tuple-element.62.both, bf16[2,384,2048]{2,1,0:T(8,128)(2,1)S(1)} %copy-done.7), custom_call_target="tpu_custom_call" | custom-call | flops 399999991808 | tf_op jit(solution)/shard_map/rest/pallas_call | solution.py:54
  120.4 0.6 collective-permute-start.14
  121.1 1.4 collective-permute-start.19
  122.5 5.6 %collective-permute-done.15.r2 = bf16[384,512]{1,0:T(8,128)(2,1)} collective-permute-done((bf16[384,512]{1,0:T(8,128)(2,1)}, bf16[384,512]{1,0:T(8,128)(2,1)}, u32[]{:S(2)}, u32[]{:S(2)}) %collective-permute-start.15) | collective-permute-done | bytes 393248 | tf_op jit(solution)/shard_map/ppermute | solution.py:342
  128.1 1.3 pass_on.1
  129.4 0.6 collective-permute-start.17
  129.9 2.9 %collective-permute-start.18 = (bf16[384,512]{1,0:T(8,128)(2,1)S(1)}, bf16[384,512]{1,0:T(8,128)(2,1)S(1)}, u32[]{:S(2)}, u32[]{:S(2)}) collective-permute-start(bf16[384,512]{1,0:T(8,128)(2,1)S(1)} %get-tuple-element.56), channel_id=1, source_target_pairs={{0,192},{64,0},{128,64},{192,128},{1,193},{65,1},{129,65},{193,129... | collective-permute-start | bytes 1179656 | tf_op jit(solution)/shard_map/ppermute | solution.py:345
  132.8 3.7 %collective-permute-done.19.pb = bf16[384,512]{1,0:T(8,128)(2,1)} collective-permute-done((bf16[384,512]{1,0:T(8,128)(2,1)}, bf16[384,512]{1,0:T(8,128)(2,1)}, u32[]{:S(2)}, u32[]{:S(2)}) %collective-permute-start.19) | collective-permute-done | bytes 393248 | tf_op jit(solution)/shard_map/ppermute | solution.py:342
  136.5 7.1 %all-to-all-start.2 = ((bf16[32,24,128]{2,1,0:T(8,128)(2,1)}), bf16[32,24,128]{2,1,0:T(8,128)(2,1)}, u32[]{:S(2)}, u32[]{:S(2)}) async-start(bf16[32,24,128]{2,1,0:T(8,128)(2,1)} %bitcast.12), calls=%async_computation.2 | async-start | bytes 393216 | tf_op jit(solution)/shard_map/all_to_all | solution.py:353
  143.6 0.4 collective-permute-done.17.pa
  144.0 2.3 %finish.1 = bf16[768,512]{1,0:T(8,128)(2,1)} custom-call(s32[2]{0:T(128)S(1)} %copy-done.4, bf16[768,512]{1,0:T(8,128)(2,1)S(1)} %get-tuple-element.49.d0, bf16[384,512]{1,0:T(8,128)(2,1)} %collective-permute-done.14.ma, bf16[384,512]{1,0:T(8,128)(2,1)S(1)} %collective-permute-done.17.pa, bf16[384,512]{1,0:T(8,128)(2,1)S(1)} %collective-permute-done.18.mb, ...), custom_call_target="tpu_custom_call" | custom-call | flops 199999995904 | tf_op jit(solution)/shard_map/finish/pallas_call | solution.py:54
  146.3 6.5 %all-to-all-done.2 = bf16[32,24,128]{2,1,0:T(8,128)(2,1)} async-done(((bf16[32,24,128]{2,1,0:T(8,128)(2,1)}), bf16[32,24,128]{2,1,0:T(8,128)(2,1)}, u32[]{:S(2)}, u32[]{:S(2)}) %all-to-all-start.2) | async-done | bytes 196640 | tf_op jit(solution)/shard_map/all_to_all | solution.py:353
  152.9 6.5 %all-to-all-start.3 = ((bf16[32,24,512]{2,1,0:T(8,128)(2,1)}), bf16[32,24,512]{2,1,0:T(8,128)(2,1)}, u32[]{:S(2)}, u32[]{:S(2)}) async-start(bf16[32,24,512]{2,1,0:T(8,128)(2,1)} %bitcast.14), calls=%async_computation.3 | async-start | bytes 1572864 | tf_op jit(solution)/shard_map/all_to_all | solution.py:353
  159.3 9.6 %wgrad.1 = (bf16[3,192,2048]{2,1,0:T(8,128)(2,1)}, bf16[3,192,2048]{2,1,0:T(8,128)(2,1)}) custom-call(s32[2]{0:T(128)} %pad_add_fusion.pos, bf16[768,768]{1,0:T(8,128)(2,1)} %copy-done.9, bf16[768,384]{1,0:T(8,128)(2,1)} %copy-done.10, bf16[768,512]{1,0:T(8,128)(2,1)} %bitcast.5.x0.refs_0_, bf16[768,512]{1,0:T(8,128)(2,1)} %copy-done.1, ...), custom_call_target="tpu_custom_call" | custom-call | flops 1300000014336 | tf_op jit(solution)/shard_map/wgrad/pallas_call | solution.py:54
  168.9 10.4 %all-to-all-done.3 = bf16[32,24,512]{2,1,0:T(8,128)(2,1)} async-done(((bf16[32,24,512]{2,1,0:T(8,128)(2,1)}), bf16[32,24,512]{2,1,0:T(8,128)(2,1)}, u32[]{:S(2)}, u32[]{:S(2)}) %all-to-all-start.3) | async-done | bytes 786464 | tf_op jit(solution)/shard_map/all_to_all | solution.py:353
  179.3 2.8 %collect.1 = (bf16[144,512]{1,0:T(8,128)(2,1)}, bf16[144,512]{1,0:T(8,128)(2,1)}) custom-call(s32[2]{0:T(128)} %pad_add_fusion.pos, s32[8,128]{1,0:T(8,128)} %bitcast.35, bf16[272,512]{1,0:T(8,128)(2,1)} %copy-done.11, bf16[768,512]{1,0:T(8,128)(2,1)} %bitcast.15.r, bf16[768,128]{1,0:T(8,128)(2,1)} %bitcast.13.cb), custom_call_target="tpu_custom_call" | custom-call | flops 299999985664 | tf_op jit(solution)/shard_map/collect/pallas_call | solution.py:54
  182.1 0.5 collective-permute-start.20
  182.7 1.8 collective-permute-done.20.refs_1_
  184.4 1.5 collective-permute-start.25
  185.9 0.0 collective-permute-start.24
  185.9 2.0 collective-permute-start.23
  187.9 2.4 %collective-permute-done.22.refs_2_ = bf16[144,512]{1,0:T(8,128)(2,1)} collective-permute-done((bf16[144,512]{1,0:T(8,128)(2,1)}, bf16[144,512]{1,0:T(8,128)(2,1)}, u32[]{:S(2)}, u32[]{:S(2)}) %collective-permute-start.22) | collective-permute-done | bytes 147488 | tf_op jit(solution)/shard_map/ppermute | solution.py:342
  190.3 1.1 collective-permute-done.25.refs_5_
  191.4 2.8 %collective-permute-start.27 = (bf16[144,512]{1,0:T(8,128)(2,1)}, bf16[144,512]{1,0:T(8,128)(2,1)}, u32[]{:S(2)}, u32[]{:S(2)}) collective-permute-start(bf16[144,512]{1,0:T(8,128)(2,1)} %collective-permute-done.25.refs_5_), channel_id=1, source_target_pairs={{0,192},{64,0},{128,64},{192,128},{1,193},{65,1},{129,65},{193,129... | collective-permute-start | bytes 442376 | tf_op jit(solution)/shard_map/ppermute | solution.py:345
  194.2 4.8 %wgrad_join.1 = (bf16[192,4096]{1,0:T(8,128)(2,1)}, bf16[192,4096]{1,0:T(8,128)(2,1)}, bf16[192,4096]{1,0:T(8,128)(2,1)}) custom-call(s32[2]{0:T(128)} %pad_add_fusion.pos, bf16[3,192,2048]{2,1,0:T(8,128)(2,1)} %get-tuple-element.69.own, bf16[3,192,2048]{2,1,0:T(8,128)(2,1)} %collective-permute-done.21.got), custom_call_target="tpu_custom_call" | custom-call | flops 499999997952 | tf_op jit(solution)/shard_map/wgrad_join/pallas_call | solution.py:54
  199.1 2.4 %assemble.1 = (bf16[128,4096]{1,0:T(8,128)(2,1)}, f32[8,128]{1,0:T(8,128)}) custom-call(s32[2]{0:T(128)S(1)} %copy-done.5, bf16[8,128]{1,0:T(8,128)(2,1)S(1)} %bitcast.23, bf16[144,512]{1,0:T(8,128)(2,1)S(1)} %copy-done.2, bf16[144,512]{1,0:T(8,128)(2,1)} %collective-permute-done.20.refs_1_, bf16[144,512]{1,0:T(8,128)(2,1)} %collective-permute-done.22.refs_2_, ...), custom_call_target="tpu_custom_call" | custom-call | flops 199999995904 | tf_op jit(solution)/shard_map/assemble/pallas_call | solution.py:54
  (44 shorter events, 0.1 us)
Async XLA Ops:
  3.6 1.8 collective-permute-start
  5.4 0.7 copy-start.11
  9.1 34.5 %all-to-all-start = ((bf16[32,24,512]{2,1,0:T(8,128)(2,1)}), bf16[32,24,512]{2,1,0:T(8,128)(2,1)}, u32[]{:S(2)}, u32[]{:S(2)}) async-start(bf16[32,24,512]{2,1,0:T(8,128)(2,1)} %bitcast.25), calls=%async_computation | async-start | bytes 1572864 | tf_op jit(solution)/shard_map/all_to_all | solution.py:353
  24.7 42.7 %collective-permute-start.5 = (bf16[3,192,2048]{2,1,0:T(8,128)(2,1)}, bf16[3,192,2048]{2,1,0:T(8,128)(2,1)}, u32[]{:S(2)}, u32[]{:S(2)}) collective-permute-start(bf16[3,192,2048]{2,1,0:T(8,128)(2,1)} %weight_send.1), channel_id=1, source_target_pairs={{0,1},{1,0},{2,3},{3,2},{4,5},{5,4},{6,7},{7,6},{8,9},{9,8},{10,11... | collective-permute-start | bytes 7077896 | tf_op jit(solution)/shard_map/ppermute | solution.py:348
  43.5 18.7 %collective-permute-start.2 = (bf16[768,512]{1,0:T(8,128)(2,1)}, bf16[768,512]{1,0:T(8,128)(2,1)S(1)}, u32[]{:S(2)}, u32[]{:S(2)}) collective-permute-start(bf16[768,512]{1,0:T(8,128)(2,1)} %bitcast.5.x0.refs_0_), channel_id=1, source_target_pairs={{0,192},{64,0},{128,64},{192,128},{1,193},{65,1},{129,65},{193,129... | collective-permute-start | bytes 2359304 | tf_op jit(solution)/shard_map/ppermute | solution.py:345
  46.6 20.1 %collective-permute-start.1 = (bf16[768,512]{1,0:T(8,128)(2,1)}, bf16[768,512]{1,0:T(8,128)(2,1)S(1)}, u32[]{:S(2)}, u32[]{:S(2)}) collective-permute-start(bf16[768,512]{1,0:T(8,128)(2,1)} %bitcast.5.x0.refs_0_), channel_id=1, source_target_pairs={{0,64},{64,128},{128,192},{192,0},{1,65},{65,129},{129,193},{193,1... | collective-permute-start | bytes 2359304 | tf_op jit(solution)/shard_map/ppermute | solution.py:342
  46.6 27.0 %all-to-all-start.1 = ((bf16[32,24,512]{2,1,0:T(8,128)(2,1)}), bf16[32,24,512]{2,1,0:T(8,128)(2,1)}, u32[]{:S(2)}, u32[]{:S(2)}) async-start(bf16[32,24,512]{2,1,0:T(8,128)(2,1)} %bitcast.24), calls=%async_computation.1 | async-start | bytes 1572864 | tf_op jit(solution)/shard_map/all_to_all | solution.py:353
  62.2 19.6 %copy-start = (bf16[768,512]{1,0:T(8,128)(2,1)}, bf16[768,512]{1,0:T(8,128)(2,1)S(1)}, u32[]{:S(2)}) copy-start(bf16[768,512]{1,0:T(8,128)(2,1)S(1)} %collective-permute-done.2.x2.refs_2_) | copy-start | bytes 2359300
  63.1 18.7 %collective-permute-start.4 = (bf16[384,512]{1,0:T(8,128)(2,1)}, bf16[384,512]{1,0:T(8,128)(2,1)}, u32[]{:S(2)}, u32[]{:S(2)}) collective-permute-start(bf16[384,512]{1,0:T(8,128)(2,1)} %slice.25), channel_id=1, source_target_pairs={{0,192},{64,0},{128,64},{192,128},{1,193},{65,1},{129,65},{193,129... | collective-permute-start | bytes 1179656 | tf_op jit(solution)/shard_map/ppermute | solution.py:345
  66.7 15.1 %copy-start.1 = (bf16[768,512]{1,0:T(8,128)(2,1)}, bf16[768,512]{1,0:T(8,128)(2,1)S(1)}, u32[]{:S(2)}) copy-start(bf16[768,512]{1,0:T(8,128)(2,1)S(1)} %collective-permute-done.1.x1.refs_1_) | copy-start | bytes 2359300
  67.5 14.3 %collective-permute-start.3 = (bf16[384,512]{1,0:T(8,128)(2,1)}, bf16[384,512]{1,0:T(8,128)(2,1)}, u32[]{:S(2)}, u32[]{:S(2)}) collective-permute-start(bf16[384,512]{1,0:T(8,128)(2,1)} %slice.24), channel_id=1, source_target_pairs={{0,64},{64,128},{128,192},{192,0},{1,65},{65,129},{129,193},{193,1... | collective-permute-start | bytes 1179656 | tf_op jit(solution)/shard_map/ppermute | solution.py:342
  73.0 8.8 %copy-start.4 = (s32[2]{0:T(128)S(1)}, s32[2]{0:T(128)}, u32[]{:S(2)}) copy-start(s32[2]{0:T(128)} %pad_add_fusion.pos) | copy-start | bytes 28
  75.6 20.7 %collective-permute-start.9 = (bf16[384,512]{1,0:T(8,128)(2,1)}, bf16[384,512]{1,0:T(8,128)(2,1)}, u32[]{:S(2)}, u32[]{:S(2)}) collective-permute-start(bf16[384,512]{1,0:T(8,128)(2,1)} %bitcast.10.refs_0_.refs_5_), channel_id=1, source_target_pairs={{0,192},{64,0},{128,64},{192,128},{1,193},{65,1},{129,65},{193,129... | collective-permute-start | bytes 1179656 | tf_op jit(solution)/shard_map/ppermute | solution.py:345
  78.5 13.2 %collective-permute-start.7 = (bf16[384,512]{1,0:T(8,128)(2,1)}, bf16[384,512]{1,0:T(8,128)(2,1)}, u32[]{:S(2)}, u32[]{:S(2)}) collective-permute-start(bf16[384,512]{1,0:T(8,128)(2,1)} %bitcast.10.refs_0_.refs_5_), channel_id=1, source_target_pairs={{0,64},{64,128},{128,192},{192,0},{1,65},{65,129},{129,193},{193,1... | collective-permute-start | bytes 1179656 | tf_op jit(solution)/shard_map/ppermute | solution.py:342
  78.5 14.0 %collective-permute-start.10 = (bf16[384,512]{1,0:T(8,128)(2,1)}, bf16[384,512]{1,0:T(8,128)(2,1)}, u32[]{:S(2)}, u32[]{:S(2)}) collective-permute-start(bf16[384,512]{1,0:T(8,128)(2,1)} %bitcast.11.refs_1_.refs_6_), channel_id=1, source_target_pairs={{0,192},{64,0},{128,64},{192,128},{1,193},{65,1},{129,65},{193,129... | collective-permute-start | bytes 1179656 | tf_op jit(solution)/shard_map/ppermute | solution.py:345
  81.8 15.4 %collective-permute-start.8 = (bf16[384,512]{1,0:T(8,128)(2,1)}, bf16[384,512]{1,0:T(8,128)(2,1)}, u32[]{:S(2)}, u32[]{:S(2)}) collective-permute-start(bf16[384,512]{1,0:T(8,128)(2,1)} %bitcast.11.refs_1_.refs_6_), channel_id=1, source_target_pairs={{0,64},{64,128},{128,192},{192,0},{1,65},{65,129},{129,193},{193,1... | collective-permute-start | bytes 1179656 | tf_op jit(solution)/shard_map/ppermute | solution.py:342
  81.8 1.9 copy-start.6
  83.7 13.5 %copy-start.8 = (bf16[384,2048]{1,0:T(8,128)(2,1)S(1)}, bf16[384,2048]{1,0:T(8,128)(2,1)}, u32[]{:S(2)}) copy-start(bf16[384,2048]{1,0:T(8,128)(2,1)} %get-tuple-element.47.refs_6_.w) | copy-start | bytes 4718596
  89.8 19.4 %collective-permute-start.6 = (f32[768,768]{1,0:T(8,128)}, f32[768,768]{1,0:T(8,128)}, u32[]{:S(2)}, u32[]{:S(2)}) collective-permute-start(f32[768,768]{1,0:T(8,128)} %gate_up.1.gu_a), channel_id=1, source_target_pairs={{0,1},{1,0},{2,3},{3,2},{4,5},{5,4},{6,7},{7,6},{8,9},{9,8},{10,11... | collective-permute-start | bytes 7077896 | tf_op jit(solution)/shard_map/ppermute | solution.py:348
  91.8 12.6 %collective-permute-start.11 = (bf16[384,512]{1,0:T(8,128)(2,1)}, bf16[384,512]{1,0:T(8,128)(2,1)}, u32[]{:S(2)}, u32[]{:S(2)}) collective-permute-start(bf16[384,512]{1,0:T(8,128)(2,1)} %collective-permute-done.7.refs_2_.refs_7_), channel_id=1, source_target_pairs={{0,64},{64,128},{128,192},{192,0},{1,65},{65,129},{129,193},{193,1... | collective-permute-start | bytes 1179656 | tf_op jit(solution)/shard_map/ppermute | solution.py:342
  92.6 11.8 %collective-permute-start.12 = (bf16[384,512]{1,0:T(8,128)(2,1)}, bf16[384,512]{1,0:T(8,128)(2,1)}, u32[]{:S(2)}, u32[]{:S(2)}) collective-permute-start(bf16[384,512]{1,0:T(8,128)(2,1)} %collective-permute-done.10.refs_5_.refs_10_), channel_id=1, source_target_pairs={{0,192},{64,0},{128,64},{192,128},{1,193},{65,1},{129,65},{193,129... | collective-permute-start | bytes 1179656 | tf_op jit(solution)/shard_map/ppermute | solution.py:345
  104.4 4.8 %copy-start.7 = (bf16[2,384,2048]{2,1,0:T(8,128)(2,1)S(1)}, bf16[2,384,2048]{2,1,0:T(8,128)(2,1)}, u32[]{:S(2)}) copy-start(bf16[2,384,2048]{2,1,0:T(8,128)(2,1)} %get-tuple-element.45.w) | copy-start | bytes 9437188
  106.3 2.9 %collective-permute-start.13 = (f32[768,384]{1,0:T(8,128)S(1)}, f32[768,384]{1,0:T(8,128)S(1)}, u32[]{:S(2)}, u32[]{:S(2)}) collective-permute-start(f32[768,384]{1,0:T(8,128)S(1)} %back.1.bk_a), channel_id=1, source_target_pairs={{0,1},{1,0},{2,3},{3,2},{4,5},{5,4},{6,7},{7,6},{8,9},{9,8},{10,11... | collective-permute-start | bytes 3538952 | tf_op jit(solution)/shard_map/ppermute | solution.py:348
  114.6 5.9 %copy-start.9 = (bf16[768,768]{1,0:T(8,128)(2,1)}, bf16[768,768]{1,0:T(8,128)(2,1)S(1)}, u32[]{:S(2)}) copy-start(bf16[768,768]{1,0:T(8,128)(2,1)S(1)} %get-tuple-element.62.both) | copy-start | bytes 3538948
  114.6 5.9 %copy-start.10 = (bf16[768,384]{1,0:T(8,128)(2,1)}, bf16[768,384]{1,0:T(8,128)(2,1)S(1)}, u32[]{:S(2)}) copy-start(bf16[768,384]{1,0:T(8,128)(2,1)S(1)} %get-tuple-element.63.hd) | copy-start | bytes 1769476
  114.6 13.5 %collective-permute-start.15 = (bf16[384,512]{1,0:T(8,128)(2,1)}, bf16[384,512]{1,0:T(8,128)(2,1)}, u32[]{:S(2)}, u32[]{:S(2)}) collective-permute-start(bf16[384,512]{1,0:T(8,128)(2,1)} %get-tuple-element.52), channel_id=1, source_target_pairs={{0,64},{64,128},{128,192},{192,0},{1,65},{65,129},{129,193},{193,1... | collective-permute-start | bytes 1179656 | tf_op jit(solution)/shard_map/ppermute | solution.py:342
  114.6 13.5 %collective-permute-start.16 = (bf16[384,512]{1,0:T(8,128)(2,1)}, bf16[384,512]{1,0:T(8,128)(2,1)}, u32[]{:S(2)}, u32[]{:S(2)}) collective-permute-start(bf16[384,512]{1,0:T(8,128)(2,1)} %get-tuple-element.54), channel_id=1, source_target_pairs={{0,192},{64,0},{128,64},{192,128},{1,193},{65,1},{129,65},{193,129... | collective-permute-start | bytes 1179656 | tf_op jit(solution)/shard_map/ppermute | solution.py:345
  120.4 23.2 %collective-permute-start.14 = (bf16[384,512]{1,0:T(8,128)(2,1)}, bf16[384,512]{1,0:T(8,128)(2,1)}, u32[]{:S(2)}, u32[]{:S(2)}) collective-permute-start(bf16[384,512]{1,0:T(8,128)(2,1)} %get-tuple-element.50), channel_id=1, source_target_pairs={{0,192},{64,0},{128,64},{192,128},{1,193},{65,1},{129,65},{193,129... | collective-permute-start | bytes 1179656 | tf_op jit(solution)/shard_map/ppermute | solution.py:345
  121.1 15.4 %collective-permute-start.19 = (bf16[384,512]{1,0:T(8,128)(2,1)}, bf16[384,512]{1,0:T(8,128)(2,1)}, u32[]{:S(2)}, u32[]{:S(2)}) collective-permute-start(bf16[384,512]{1,0:T(8,128)(2,1)} %get-tuple-element.57), channel_id=1, source_target_pairs={{0,64},{64,128},{128,192},{192,0},{1,65},{65,129},{129,193},{193,1... | collective-permute-start | bytes 1179656 | tf_op jit(solution)/shard_map/ppermute | solution.py:342
  129.4 14.6 %collective-permute-start.17 = (bf16[384,512]{1,0:T(8,128)(2,1)S(1)}, bf16[384,512]{1,0:T(8,128)(2,1)S(1)}, u32[]{:S(2)}, u32[]{:S(2)}) collective-permute-start(bf16[384,512]{1,0:T(8,128)(2,1)S(1)} %get-tuple-element.55), channel_id=1, source_target_pairs={{0,64},{64,128},{128,192},{192,0},{1,65},{65,129},{129,193},{193,1... | collective-permute-start | bytes 1179656 | tf_op jit(solution)/shard_map/ppermute | solution.py:342
  129.9 14.1 %collective-permute-start.18 = (bf16[384,512]{1,0:T(8,128)(2,1)S(1)}, bf16[384,512]{1,0:T(8,128)(2,1)S(1)}, u32[]{:S(2)}, u32[]{:S(2)}) collective-permute-start(bf16[384,512]{1,0:T(8,128)(2,1)S(1)} %get-tuple-element.56), channel_id=1, source_target_pairs={{0,192},{64,0},{128,64},{192,128},{1,193},{65,1},{129,65},{193,129... | collective-permute-start | bytes 1179656 | tf_op jit(solution)/shard_map/ppermute | solution.py:345
  136.5 16.4 %all-to-all-start.2 = ((bf16[32,24,128]{2,1,0:T(8,128)(2,1)}), bf16[32,24,128]{2,1,0:T(8,128)(2,1)}, u32[]{:S(2)}, u32[]{:S(2)}) async-start(bf16[32,24,128]{2,1,0:T(8,128)(2,1)} %bitcast.12), calls=%async_computation.2 | async-start | bytes 393216 | tf_op jit(solution)/shard_map/all_to_all | solution.py:353
  152.9 26.5 %all-to-all-start.3 = ((bf16[32,24,512]{2,1,0:T(8,128)(2,1)}), bf16[32,24,512]{2,1,0:T(8,128)(2,1)}, u32[]{:S(2)}, u32[]{:S(2)}) async-start(bf16[32,24,512]{2,1,0:T(8,128)(2,1)} %bitcast.14), calls=%async_computation.3 | async-start | bytes 1572864 | tf_op jit(solution)/shard_map/all_to_all | solution.py:353
  179.3 14.9 %collective-permute-start.21 = (bf16[3,192,2048]{2,1,0:T(8,128)(2,1)}, bf16[3,192,2048]{2,1,0:T(8,128)(2,1)}, u32[]{:S(2)}, u32[]{:S(2)}) collective-permute-start(bf16[3,192,2048]{2,1,0:T(8,128)(2,1)} %get-tuple-element.70), channel_id=1, source_target_pairs={{0,1},{1,0},{2,3},{3,2},{4,5},{5,4},{6,7},{7,6},{8,9},{9,8},{10,11... | collective-permute-start | bytes 7077896 | tf_op jit(solution)/shard_map/ppermute | solution.py:348
  182.1 2.3 %collective-permute-start.20 = (bf16[144,512]{1,0:T(8,128)(2,1)}, bf16[144,512]{1,0:T(8,128)(2,1)}, u32[]{:S(2)}, u32[]{:S(2)}) collective-permute-start(bf16[144,512]{1,0:T(8,128)(2,1)} %get-tuple-element.67), channel_id=1, source_target_pairs={{0,1},{1,0},{2,3},{3,2},{4,5},{5,4},{6,7},{7,6},{8,9},{9,8},{10,11... | collective-permute-start | bytes 442376 | tf_op jit(solution)/shard_map/ppermute | solution.py:348
  182.7 7.7 %collective-permute-start.22 = (bf16[144,512]{1,0:T(8,128)(2,1)}, bf16[144,512]{1,0:T(8,128)(2,1)}, u32[]{:S(2)}, u32[]{:S(2)}) collective-permute-start(bf16[144,512]{1,0:T(8,128)(2,1)} %get-tuple-element.73.refs_0_), channel_id=1, source_target_pairs={{0,64},{64,128},{128,192},{192,0},{1,65},{65,129},{129,193},{193,1... | collective-permute-start | bytes 442376 | tf_op jit(solution)/shard_map/ppermute | solution.py:342
  184.4 7.0 %collective-permute-start.25 = (bf16[144,512]{1,0:T(8,128)(2,1)}, bf16[144,512]{1,0:T(8,128)(2,1)}, u32[]{:S(2)}, u32[]{:S(2)}) collective-permute-start(bf16[144,512]{1,0:T(8,128)(2,1)} %collective-permute-done.20.refs_1_), channel_id=1, source_target_pairs={{0,192},{64,0},{128,64},{192,128},{1,193},{65,1},{129,65},{193,129... | collective-permute-start | bytes 442376 | tf_op jit(solution)/shard_map/ppermute | solution.py:345
  185.9 13.1 %collective-permute-start.24 = (bf16[144,512]{1,0:T(8,128)(2,1)}, bf16[144,512]{1,0:T(8,128)(2,1)}, u32[]{:S(2)}, u32[]{:S(2)}) collective-permute-start(bf16[144,512]{1,0:T(8,128)(2,1)} %get-tuple-element.73.refs_0_), channel_id=1, source_target_pairs={{0,192},{64,0},{128,64},{192,128},{1,193},{65,1},{129,65},{193,129... | collective-permute-start | bytes 442376 | tf_op jit(solution)/shard_map/ppermute | solution.py:345
  185.9 13.1 %collective-permute-start.23 = (bf16[144,512]{1,0:T(8,128)(2,1)}, bf16[144,512]{1,0:T(8,128)(2,1)}, u32[]{:S(2)}, u32[]{:S(2)}) collective-permute-start(bf16[144,512]{1,0:T(8,128)(2,1)} %collective-permute-done.20.refs_1_), channel_id=1, source_target_pairs={{0,64},{64,128},{128,192},{192,0},{1,65},{65,129},{129,193},{193,1... | collective-permute-start | bytes 442376 | tf_op jit(solution)/shard_map/ppermute | solution.py:342
  190.3 8.7 %collective-permute-start.26 = (bf16[144,512]{1,0:T(8,128)(2,1)}, bf16[144,512]{1,0:T(8,128)(2,1)}, u32[]{:S(2)}, u32[]{:S(2)}) collective-permute-start(bf16[144,512]{1,0:T(8,128)(2,1)} %collective-permute-done.22.refs_2_), channel_id=1, source_target_pairs={{0,64},{64,128},{128,192},{192,0},{1,65},{65,129},{129,193},{193,1... | collective-permute-start | bytes 442376 | tf_op jit(solution)/shard_map/ppermute | solution.py:342
  191.4 7.6 %collective-permute-start.27 = (bf16[144,512]{1,0:T(8,128)(2,1)}, bf16[144,512]{1,0:T(8,128)(2,1)}, u32[]{:S(2)}, u32[]{:S(2)}) collective-permute-start(bf16[144,512]{1,0:T(8,128)(2,1)} %collective-permute-done.25.refs_5_), channel_id=1, source_target_pairs={{0,192},{64,0},{128,64},{192,128},{1,193},{65,1},{129,65},{193,129... | collective-permute-start | bytes 442376 | tf_op jit(solution)/shard_map/ppermute | solution.py:345
  194.2 4.9 %copy-start.2 = (bf16[144,512]{1,0:T(8,128)(2,1)S(1)}, bf16[144,512]{1,0:T(8,128)(2,1)}, u32[]{:S(2)}) copy-start(bf16[144,512]{1,0:T(8,128)(2,1)} %get-tuple-element.73.refs_0_) | copy-start | bytes 442372
  194.2 4.9 %copy-start.3 = (bf16[128,8]{0,1:T(8,128)(2,1)S(1)}, bf16[128,8]{0,1:T(8,128)(2,1)}, u32[]{:S(2)}) copy-start(bf16[128,8]{0,1:T(8,128)(2,1)} %param.10) | copy-start | bytes 6148
  194.2 4.9 %copy-start.5 = (s32[2]{0:T(128)S(1)}, s32[2]{0:T(128)}, u32[]{:S(2)}) copy-start(s32[2]{0:T(128)} %pad_add_fusion.pos) | copy-start | bytes 28

commit v7 on v6

--- a/solution.py
+++ b/solution.py
@@ -426,11 +426,11 @@
         name="wgrad",
     )
     r, w_other = tie((r, w_other))
-    dgot = swap(w_other)
     qa, sib = call(
         collect_body, [((144, CH), BF)] * 2, (pos, ids, pk, r, cb), name="collect"
     )
-    qb = swap(sib)
+    qb, w_other = tie((swap(sib), w_other))
+    dgot = swap(w_other)
     parts = spread_halves(qa, qb)
     qb, w_own = tie((qb, w_own))
     dwg, dwu, dwd = call(

time: 202 us -> 203 us (level)
  starting transfers between devices: 63 us -> 65.1 us
    ppermute x11, starting transfers between devices: 27.5 us -> 29.9 us  [down(): return lax.ppermute(x, 'dp', down_ring)]
  transfers between devices with their start and end apart: 32 -> 32, of which waited for: 17 -> 16; matrix products, arithmetic and copies ran while one was open for 2% -> 2% of each run, Pallas kernels for 22% -> 20%
where the time goes in v7:
time: 203 us
  waiting for transfers between devices  69.8 us (34%)
  starting transfers between devices  65.1 us (32%)
  Pallas kernels  60.1 us (30%)
  local copies, waits for them, and re-layouts  6.3 us (3%)
    pallas_call x16, Pallas kernels, call(): pl.pallas_call(body, out_shape=[jax.ShapeDtypeStruct(s, t) for s, t in ou...  60.1 us
    all_to_all x4, waiting for transfers between devices, exchange(): lax.all_to_all(x, 'expert', split_axis=0, concat_axis=0, axis_index_group...  33.4 us
    all_to_all x4, starting transfers between devices, exchange(): lax.all_to_all(x, 'expert', split_axis=0, concat_axis=0, axis_index_group...  30.9 us
    ppermute x11, starting transfers between devices, down(): return lax.ppermute(x, 'dp', down_ring)  29.9 us
    ppermute x11, waiting for transfers between devices, up(): return lax.ppermute(x, 'dp', up_ring)  19.3 us
    ppermute x11, waiting for transfers between devices, down(): return lax.ppermute(x, 'dp', down_ring)  10.8 us
    ppermute x6, waiting for transfers between devices, swap(): return lax.ppermute(x, 'expert', cores)  6.32 us
  transfers between devices with their start and end apart: 32, of which 16 were waited for; matrix products, arithmetic and copies ran while one was open for 2% of the time, Pallas kernels for 20%

profile of v7, /device:TPU:2, one launch (start us, length us, event | category | flops | bytes accessed | tf_op | source)
XLA Modules:
  0.0 202.7 jit_solution(8640910278207737118)
XLA Ops:
  0.6 0.6 pad_add_fusion.pos
  1.2 2.3 %pack.1 = bf16[272,512]{1,0:T(8,128)(2,1)} custom-call(s32[2]{0:T(128)} %pad_add_fusion.pos, s32[8,128]{1,0:T(8,128)} %bitcast.32, bf16[8,128]{1,0:T(8,128)(2,1)} %bitcast.20, bf16[128,4096]{1,0:T(8,128)(2,1)} %rows_ref.3, bf16[128,4096]{1,0:T(8,128)(2,1)} %rows_ref.2), custom_call_target="tpu_custom_call" | custom-call | flops 199999995904 | tf_op jit(solution)/shard_map/pack/pallas_call | solution.py:54
  3.5 0.0 collective-permute-start
  3.5 1.8 collective-permute-done.pk
  5.3 0.7 copy-done.12
  6.0 3.0 %send.3 = bf16[768,512]{1,0:T(8,128)(2,1)} custom-call(s32[2]{0:T(128)} %pad_add_fusion.pos, s32[8,128]{1,0:T(8,128)} %bitcast.33, bf16[8,128]{1,0:T(8,128)(2,1)} %bitcast.21, bf16[272,512]{1,0:T(8,128)(2,1)} %copy-done.12, bf16[128,4096]{1,0:T(8,128)(2,1)} %rows_ref.3), custom_call_target="tpu_custom_call" | custom-call | flops 299999985664 | tf_op jit(solution)/shard_map/send/pallas_call | solution.py:54
  9.0 11.7 %all-to-all-start = ((bf16[32,24,512]{2,1,0:T(8,128)(2,1)}), bf16[32,24,512]{2,1,0:T(8,128)(2,1)}, u32[]{:S(2)}, u32[]{:S(2)}) async-start(bf16[32,24,512]{2,1,0:T(8,128)(2,1)} %bitcast.25), calls=%async_computation | async-start | bytes 1572864 | tf_op jit(solution)/shard_map/all_to_all | solution.py:353
  20.7 3.9 %weight_send.1 = bf16[3,192,2048]{2,1,0:T(8,128)(2,1)} custom-call(s32[2]{0:T(128)} %pad_add_fusion.pos, bf16[192,4096]{1,0:T(8,128)(2,1)} %bitcast.26, bf16[192,4096]{1,0:T(8,128)(2,1)} %bitcast.28, bf16[192,4096]{1,0:T(8,128)(2,1)} %bitcast.30), custom_call_target="tpu_custom_call" | custom-call | flops 399999991808 | tf_op jit(solution)/shard_map/weight_send/pallas_call | solution.py:54
  24.6 0.0 collective-permute-start.5
  24.6 3.1 %send.2 = bf16[768,512]{1,0:T(8,128)(2,1)} custom-call(s32[2]{0:T(128)} %pad_add_fusion.pos, s32[8,128]{1,0:T(8,128)} %bitcast.34, bf16[8,128]{1,0:T(8,128)(2,1)} %bitcast.22, bf16[272,512]{1,0:T(8,128)(2,1)} %copy-done.12, bf16[128,4096]{1,0:T(8,128)(2,1)} %rows_ref.2), custom_call_target="tpu_custom_call" | custom-call | flops 299999985664 | tf_op jit(solution)/shard_map/send/pallas_call | solution.py:54
  27.8 15.7 %all-to-all-done = bf16[32,24,512]{2,1,0:T(8,128)(2,1)} async-done(((bf16[32,24,512]{2,1,0:T(8,128)(2,1)}), bf16[32,24,512]{2,1,0:T(8,128)(2,1)}, u32[]{:S(2)}, u32[]{:S(2)}) %all-to-all-start) | async-done | bytes 786464 | tf_op jit(solution)/shard_map/all_to_all | solution.py:353
  43.5 3.0 %collective-permute-start.2 = (bf16[768,512]{1,0:T(8,128)(2,1)}, bf16[768,512]{1,0:T(8,128)(2,1)S(1)}, u32[]{:S(2)}, u32[]{:S(2)}) collective-permute-start(bf16[768,512]{1,0:T(8,128)(2,1)} %bitcast.5.x0.refs_0_), channel_id=1, source_target_pairs={{0,192},{64,0},{128,64},{192,128},{1,193},{65,1},{129,65},{193,129... | collective-permute-start | bytes 2359304 | tf_op jit(solution)/shard_map/ppermute | solution.py:345
  46.5 0.0 collective-permute-start.1
  46.5 5.6 %all-to-all-start.1 = ((bf16[32,24,512]{2,1,0:T(8,128)(2,1)}), bf16[32,24,512]{2,1,0:T(8,128)(2,1)}, u32[]{:S(2)}, u32[]{:S(2)}) async-start(bf16[32,24,512]{2,1,0:T(8,128)(2,1)} %bitcast.24), calls=%async_computation.1 | async-start | bytes 1572864 | tf_op jit(solution)/shard_map/all_to_all | solution.py:353
  52.1 10.0 %collective-permute-done.2.x2.refs_2_ = bf16[768,512]{1,0:T(8,128)(2,1)S(1)} collective-permute-done((bf16[768,512]{1,0:T(8,128)(2,1)}, bf16[768,512]{1,0:T(8,128)(2,1)S(1)}, u32[]{:S(2)}, u32[]{:S(2)}) %collective-permute-start.2) | collective-permute-done | bytes 786464 | tf_op jit(solution)/shard_map/ppermute | solution.py:345
  62.1 0.8 slice.25
  62.9 3.6 %collective-permute-start.4 = (bf16[384,512]{1,0:T(8,128)(2,1)}, bf16[384,512]{1,0:T(8,128)(2,1)}, u32[]{:S(2)}, u32[]{:S(2)}) collective-permute-start(bf16[384,512]{1,0:T(8,128)(2,1)} %slice.25), channel_id=1, source_target_pairs={{0,192},{64,0},{128,64},{192,128},{1,193},{65,1},{129,65},{193,129... | collective-permute-start | bytes 1179656 | tf_op jit(solution)/shard_map/ppermute | solution.py:345
  66.5 0.8 slice.24
  67.3 5.6 %weight_join.1 = (bf16[2,384,2048]{2,1,0:T(8,128)(2,1)}, bf16[384,2048]{1,0:T(8,128)(2,1)}) custom-call(s32[2]{0:T(128)} %pad_add_fusion.pos, bf16[192,4096]{1,0:T(8,128)(2,1)} %bitcast.27, bf16[192,4096]{1,0:T(8,128)(2,1)} %bitcast.29, bf16[192,4096]{1,0:T(8,128)(2,1)} %bitcast.31, bf16[3,192,2048]{2,1,0:T(8,128)(2,1)} %collective-permute-done.5.got), custom_call_target="tpu_custom_call" | custom-call | flops 599999971328 | tf_op jit(solution)/shard_map/weight_join/pallas_call | solution.py:54
  72.9 0.6 all-to-all-done.1
  73.5 2.1 %fusion = (bf16[16,24,512]{2,1,0:T(8,128)(2,1)}, bf16[16,24,512]{2,1,0:T(8,128)(2,1)}) fusion(bf16[32,24,512]{2,1,0:T(8,128)(2,1)} %all-to-all-done.1), kind=kLoop, calls=%fused_computation.1 | loop fusion | bytes 1572864 | tf_op jit(solution)/shard_map/slice | solution.py:395
  75.5 3.0 %collective-permute-start.9 = (bf16[384,512]{1,0:T(8,128)(2,1)}, bf16[384,512]{1,0:T(8,128)(2,1)}, u32[]{:S(2)}, u32[]{:S(2)}) collective-permute-start(bf16[384,512]{1,0:T(8,128)(2,1)} %bitcast.10.refs_0_.refs_5_), channel_id=1, source_target_pairs={{0,192},{64,0},{128,64},{192,128},{1,193},{65,1},{129,65},{193,129... | collective-permute-start | bytes 1179656 | tf_op jit(solution)/shard_map/ppermute | solution.py:345
  78.5 0.0 collective-permute-start.7
  78.5 3.2 %collective-permute-start.10 = (bf16[384,512]{1,0:T(8,128)(2,1)}, bf16[384,512]{1,0:T(8,128)(2,1)}, u32[]{:S(2)}, u32[]{:S(2)}) collective-permute-start(bf16[384,512]{1,0:T(8,128)(2,1)} %bitcast.11.refs_1_.refs_6_), channel_id=1, source_target_pairs={{0,192},{64,0},{128,64},{192,128},{1,193},{65,1},{129,65},{193,129... | collective-permute-start | bytes 1179656 | tf_op jit(solution)/shard_map/ppermute | solution.py:345
  81.8 1.9 copy-done.6
  83.7 6.2 %gate_up.1.gu_a = f32[768,768]{1,0:T(8,128)} custom-call(s32[2]{0:T(128)S(1)} %copy-done.4, bf16[768,512]{1,0:T(8,128)(2,1)} %bitcast.5.x0.refs_0_, bf16[768,512]{1,0:T(8,128)(2,1)S(1)} %collective-permute-done.1.x1.refs_1_, bf16[768,512]{1,0:T(8,128)(2,1)S(1)} %collective-permute-done.2.x2.refs_2_, bf16[384,512]{1,0:T(8,128)(2,1)} %collective-permute-done.3.xa.refs_3_, ...), custom_call_target="tpu_custom_call" | custom-call | flops 799999983616 | tf_op jit(solution)/shard_map/gate_up/pallas_call | solution.py:54
  89.8 0.0 collective-permute-start.6
  89.8 1.8 collective-permute-done.7.refs_2_.refs_7_
  91.6 0.8 collective-permute-done.10.refs_5_.refs_10_
  92.4 3.7 %collective-permute-start.12 = (bf16[384,512]{1,0:T(8,128)(2,1)}, bf16[384,512]{1,0:T(8,128)(2,1)}, u32[]{:S(2)}, u32[]{:S(2)}) collective-permute-start(bf16[384,512]{1,0:T(8,128)(2,1)} %collective-permute-done.10.refs_5_.refs_10_), channel_id=1, source_target_pairs={{0,192},{64,0},{128,64},{192,128},{1,193},{65,1},{129,65},{193,129... | collective-permute-start | bytes 1179656 | tf_op jit(solution)/shard_map/ppermute | solution.py:345
  96.1 0.8 collective-permute-done.8.refs_3_.refs_8_
  96.9 3.0 %back_near.1.acc = f32[768,384]{1,0:T(8,128)S(1)} custom-call(s32[2]{0:T(128)S(1)} %copy-done.4, bf16[384,512]{1,0:T(8,128)(2,1)} %bitcast.10.refs_0_.refs_5_, bf16[384,512]{1,0:T(8,128)(2,1)} %bitcast.11.refs_1_.refs_6_, bf16[384,512]{1,0:T(8,128)(2,1)} %collective-permute-done.7.refs_2_.refs_7_, bf16[384,512]{1,0:T(8,128)(2,1)} %collective-permute-done.8.refs_3_.refs_8_, ...), custom_call_target="tpu_custom_call" | custom-call | flops 499999997952 | tf_op jit(solution)/shard_map/back_near/pallas_call | solution.py:54
  99.9 4.4 %collective-permute-done.11.xa.refs_11_ = bf16[384,512]{1,0:T(8,128)(2,1)} collective-permute-done((bf16[384,512]{1,0:T(8,128)(2,1)}, bf16[384,512]{1,0:T(8,128)(2,1)}, u32[]{:S(2)}, u32[]{:S(2)}) %collective-permute-start.11) | collective-permute-done | bytes 393248 | tf_op jit(solution)/shard_map/ppermute | solution.py:342
  104.3 1.9 back.1.bk_a
  106.1 0.1 collective-permute-start.13
  106.2 2.8 %collective-permute-done.13.bk_b = f32[768,384]{1,0:T(8,128)S(1)} collective-permute-done((f32[768,384]{1,0:T(8,128)S(1)}, f32[768,384]{1,0:T(8,128)S(1)}, u32[]{:S(2)}, u32[]{:S(2)}) %collective-permute-start.13) | collective-permute-done | bytes 1179680 | tf_op jit(solution)/shard_map/ppermute | solution.py:348
  109.1 5.4 %mid.1 = (bf16[768,768]{1,0:T(8,128)(2,1)S(1)}, bf16[768,384]{1,0:T(8,128)(2,1)S(1)}, bf16[768,128]{1,0:T(8,128)(2,1)}, bf16[384,512]{1,0:T(8,128)(2,1)}, bf16[384,512]{1,0:T(8,128)(2,1)}) custom-call(s32[2]{0:T(128)S(1)} %copy-done.4, f32[768,768]{1,0:T(8,128)} %gate_up.1.gu_a, f32[768,768]{1,0:T(8,128)} %collective-permute-done.6.gu_b, ...), custom_call_target="tpu_custom_call" | custom-call | flops 799999983616 | tf_op jit(solution)/shard_map/mid/pallas_call | solution.py:54
  114.4 0.0 collective-permute-start.15
  114.5 3.2 %collective-permute-start.16 = (bf16[384,512]{1,0:T(8,128)(2,1)}, bf16[384,512]{1,0:T(8,128)(2,1)}, u32[]{:S(2)}, u32[]{:S(2)}) collective-permute-start(bf16[384,512]{1,0:T(8,128)(2,1)} %get-tuple-element.56), channel_id=1, source_target_pairs={{0,192},{64,0},{128,64},{192,128},{1,193},{65,1},{129,65},{193,129... | collective-permute-start | bytes 1179656 | tf_op jit(solution)/shard_map/ppermute | solution.py:345
  117.7 2.6 %rest.1 = (bf16[384,512]{1,0:T(8,128)(2,1)S(1)}, bf16[384,512]{1,0:T(8,128)(2,1)}, bf16[384,512]{1,0:T(8,128)(2,1)}, bf16[384,512]{1,0:T(8,128)(2,1)S(1)}, bf16[768,512]{1,0:T(8,128)(2,1)S(1)}) custom-call(s32[2]{0:T(128)S(1)} %copy-done.4, bf16[768,768]{1,0:T(8,128)(2,1)S(1)} %get-tuple-element.64.both, bf16[2,384,2048]{2,1,0:T(8,128)(2,1)S(1)} %copy-done.7), custom_call_target="tpu_custom_call" | custom-call | flops 399999991808 | tf_op jit(solution)/shard_map/rest/pallas_call | solution.py:54
  120.3 0.8 collective-permute-start.14
  121.1 1.3 collective-permute-start.19
  122.4 5.6 %collective-permute-done.15.r2 = bf16[384,512]{1,0:T(8,128)(2,1)} collective-permute-done((bf16[384,512]{1,0:T(8,128)(2,1)}, bf16[384,512]{1,0:T(8,128)(2,1)}, u32[]{:S(2)}, u32[]{:S(2)}) %collective-permute-start.15) | collective-permute-done | bytes 393248 | tf_op jit(solution)/shard_map/ppermute | solution.py:342
  127.9 1.3 pass_on.1
  129.2 0.7 collective-permute-start.17
  129.9 2.8 %collective-permute-start.18 = (bf16[384,512]{1,0:T(8,128)(2,1)S(1)}, bf16[384,512]{1,0:T(8,128)(2,1)S(1)}, u32[]{:S(2)}, u32[]{:S(2)}) collective-permute-start(bf16[384,512]{1,0:T(8,128)(2,1)S(1)} %get-tuple-element.58), channel_id=1, source_target_pairs={{0,192},{64,0},{128,64},{192,128},{1,193},{65,1},{129,65},{193,129... | collective-permute-start | bytes 1179656 | tf_op jit(solution)/shard_map/ppermute | solution.py:345
  132.7 3.7 %collective-permute-done.19.pb = bf16[384,512]{1,0:T(8,128)(2,1)} collective-permute-done((bf16[384,512]{1,0:T(8,128)(2,1)}, bf16[384,512]{1,0:T(8,128)(2,1)}, u32[]{:S(2)}, u32[]{:S(2)}) %collective-permute-start.19) | collective-permute-done | bytes 393248 | tf_op jit(solution)/shard_map/ppermute | solution.py:342
  136.4 7.2 %all-to-all-start.2 = ((bf16[32,24,128]{2,1,0:T(8,128)(2,1)}), bf16[32,24,128]{2,1,0:T(8,128)(2,1)}, u32[]{:S(2)}, u32[]{:S(2)}) async-start(bf16[32,24,128]{2,1,0:T(8,128)(2,1)} %bitcast.12), calls=%async_computation.2 | async-start | bytes 393216 | tf_op jit(solution)/shard_map/all_to_all | solution.py:353
  143.5 0.3 collective-permute-done.17.pa
  143.9 2.3 %finish.1 = bf16[768,512]{1,0:T(8,128)(2,1)} custom-call(s32[2]{0:T(128)S(1)} %copy-done.4, bf16[768,512]{1,0:T(8,128)(2,1)S(1)} %get-tuple-element.51.d0, bf16[384,512]{1,0:T(8,128)(2,1)} %collective-permute-done.14.ma, bf16[384,512]{1,0:T(8,128)(2,1)S(1)} %collective-permute-done.17.pa, bf16[384,512]{1,0:T(8,128)(2,1)S(1)} %collective-permute-done.18.mb, ...), custom_call_target="tpu_custom_call" | custom-call | flops 199999995904 | tf_op jit(solution)/shard_map/finish/pallas_call | solution.py:54
  146.2 6.6 %all-to-all-done.2 = bf16[32,24,128]{2,1,0:T(8,128)(2,1)} async-done(((bf16[32,24,128]{2,1,0:T(8,128)(2,1)}), bf16[32,24,128]{2,1,0:T(8,128)(2,1)}, u32[]{:S(2)}, u32[]{:S(2)}) %all-to-all-start.2) | async-done | bytes 196640 | tf_op jit(solution)/shard_map/all_to_all | solution.py:353
  152.7 6.5 %all-to-all-start.3 = ((bf16[32,24,512]{2,1,0:T(8,128)(2,1)}), bf16[32,24,512]{2,1,0:T(8,128)(2,1)}, u32[]{:S(2)}, u32[]{:S(2)}) async-start(bf16[32,24,512]{2,1,0:T(8,128)(2,1)} %bitcast.14), calls=%async_computation.3 | async-start | bytes 1572864 | tf_op jit(solution)/shard_map/all_to_all | solution.py:353
  159.2 9.5 %wgrad.1 = (bf16[3,192,2048]{2,1,0:T(8,128)(2,1)}, bf16[3,192,2048]{2,1,0:T(8,128)(2,1)}) custom-call(s32[2]{0:T(128)} %pad_add_fusion.pos, bf16[768,768]{1,0:T(8,128)(2,1)} %copy-done.9, bf16[768,384]{1,0:T(8,128)(2,1)} %copy-done.10, bf16[768,512]{1,0:T(8,128)(2,1)} %bitcast.5.x0.refs_0_, bf16[768,512]{1,0:T(8,128)(2,1)} %copy-done.1, ...), custom_call_target="tpu_custom_call" | custom-call | flops 1300000014336 | tf_op jit(solution)/shard_map/wgrad/pallas_call | solution.py:54
  168.7 10.5 %all-to-all-done.3 = bf16[32,24,512]{2,1,0:T(8,128)(2,1)} async-done(((bf16[32,24,512]{2,1,0:T(8,128)(2,1)}), bf16[32,24,512]{2,1,0:T(8,128)(2,1)}, u32[]{:S(2)}, u32[]{:S(2)}) %all-to-all-start.3) | async-done | bytes 786464 | tf_op jit(solution)/shard_map/all_to_all | solution.py:353
  179.2 3.0 %collect.1 = (bf16[144,512]{1,0:T(8,128)(2,1)}, bf16[144,512]{1,0:T(8,128)(2,1)}) custom-call(s32[2]{0:T(128)} %pad_add_fusion.pos, s32[8,128]{1,0:T(8,128)} %bitcast.35, bf16[272,512]{1,0:T(8,128)(2,1)} %copy-done.12, bf16[768,512]{1,0:T(8,128)(2,1)} %bitcast.15.r, bf16[768,128]{1,0:T(8,128)(2,1)} %bitcast.13.cb), custom_call_target="tpu_custom_call" | custom-call | flops 299999985664 | tf_op jit(solution)/shard_map/collect/pallas_call | solution.py:54
  182.2 1.7 collective-permute-done.20.refs_1_
  183.9 0.1 collective-permute-start.21
  184.0 3.2 %collective-permute-start.25 = (bf16[144,512]{1,0:T(8,128)(2,1)}, bf16[144,512]{1,0:T(8,128)(2,1)}, u32[]{:S(2)}, u32[]{:S(2)}) collective-permute-start(bf16[144,512]{1,0:T(8,128)(2,1)} %collective-permute-done.20.refs_1_), channel_id=1, source_target_pairs={{0,192},{64,0},{128,64},{192,128},{1,193},{65,1},{129,65},{193,129... | collective-permute-start | bytes 442376 | tf_op jit(solution)/shard_map/ppermute | solution.py:345
  187.3 0.0 collective-permute-start.24
  187.3 2.0 collective-permute-start.23
  189.3 2.7 %collective-permute-done.22.refs_2_ = bf16[144,512]{1,0:T(8,128)(2,1)} collective-permute-done((bf16[144,512]{1,0:T(8,128)(2,1)}, bf16[144,512]{1,0:T(8,128)(2,1)}, u32[]{:S(2)}, u32[]{:S(2)}) %collective-permute-start.22) | collective-permute-done | bytes 147488 | tf_op jit(solution)/shard_map/ppermute | solution.py:342
  192.0 3.5 %collective-permute-start.27 = (bf16[144,512]{1,0:T(8,128)(2,1)}, bf16[144,512]{1,0:T(8,128)(2,1)}, u32[]{:S(2)}, u32[]{:S(2)}) collective-permute-start(bf16[144,512]{1,0:T(8,128)(2,1)} %collective-permute-done.25.refs_5_), channel_id=1, source_target_pairs={{0,192},{64,0},{128,64},{192,128},{1,193},{65,1},{129,65},{193,129... | collective-permute-start | bytes 442376 | tf_op jit(solution)/shard_map/ppermute | solution.py:345
  195.5 4.8 %wgrad_join.1 = (bf16[192,4096]{1,0:T(8,128)(2,1)}, bf16[192,4096]{1,0:T(8,128)(2,1)}, bf16[192,4096]{1,0:T(8,128)(2,1)}) custom-call(s32[2]{0:T(128)} %pad_add_fusion.pos, bf16[3,192,2048]{2,1,0:T(8,128)(2,1)} %get-tuple-element.73.own, bf16[3,192,2048]{2,1,0:T(8,128)(2,1)} %collective-permute-done.21.got), custom_call_target="tpu_custom_call" | custom-call | flops 499999997952 | tf_op jit(solution)/shard_map/wgrad_join/pallas_call | solution.py:54
  200.4 2.4 %assemble.1 = (bf16[128,4096]{1,0:T(8,128)(2,1)}, f32[8,128]{1,0:T(8,128)}) custom-call(s32[2]{0:T(128)S(1)} %copy-done.5, bf16[8,128]{1,0:T(8,128)(2,1)S(1)} %bitcast.23, bf16[144,512]{1,0:T(8,128)(2,1)S(1)} %copy-done.2, bf16[144,512]{1,0:T(8,128)(2,1)} %collective-permute-done.20.refs_1_, bf16[144,512]{1,0:T(8,128)(2,1)} %collective-permute-done.22.refs_2_, ...), custom_call_target="tpu_custom_call" | custom-call | flops 199999995904 | tf_op jit(solution)/shard_map/assemble/pallas_call | solution.py:54
  (46 shorter events, 0.1 us)
Async XLA Ops:
  3.5 1.8 collective-permute-start
  5.3 0.7 copy-start.12
  9.0 34.5 %all-to-all-start = ((bf16[32,24,512]{2,1,0:T(8,128)(2,1)}), bf16[32,24,512]{2,1,0:T(8,128)(2,1)}, u32[]{:S(2)}, u32[]{:S(2)}) async-start(bf16[32,24,512]{2,1,0:T(8,128)(2,1)} %bitcast.25), calls=%async_computation | async-start | bytes 1572864 | tf_op jit(solution)/shard_map/all_to_all | solution.py:353
  24.6 42.7 %collective-permute-start.5 = (bf16[3,192,2048]{2,1,0:T(8,128)(2,1)}, bf16[3,192,2048]{2,1,0:T(8,128)(2,1)}, u32[]{:S(2)}, u32[]{:S(2)}) collective-permute-start(bf16[3,192,2048]{2,1,0:T(8,128)(2,1)} %weight_send.1), channel_id=1, source_target_pairs={{0,1},{1,0},{2,3},{3,2},{4,5},{5,4},{6,7},{7,6},{8,9},{9,8},{10,11... | collective-permute-start | bytes 7077896 | tf_op jit(solution)/shard_map/ppermute | solution.py:348
  43.5 18.6 %collective-permute-start.2 = (bf16[768,512]{1,0:T(8,128)(2,1)}, bf16[768,512]{1,0:T(8,128)(2,1)S(1)}, u32[]{:S(2)}, u32[]{:S(2)}) collective-permute-start(bf16[768,512]{1,0:T(8,128)(2,1)} %bitcast.5.x0.refs_0_), channel_id=1, source_target_pairs={{0,192},{64,0},{128,64},{192,128},{1,193},{65,1},{129,65},{193,129... | collective-permute-start | bytes 2359304 | tf_op jit(solution)/shard_map/ppermute | solution.py:345
  46.5 20.0 %collective-permute-start.1 = (bf16[768,512]{1,0:T(8,128)(2,1)}, bf16[768,512]{1,0:T(8,128)(2,1)S(1)}, u32[]{:S(2)}, u32[]{:S(2)}) collective-permute-start(bf16[768,512]{1,0:T(8,128)(2,1)} %bitcast.5.x0.refs_0_), channel_id=1, source_target_pairs={{0,64},{64,128},{128,192},{192,0},{1,65},{65,129},{129,193},{193,1... | collective-permute-start | bytes 2359304 | tf_op jit(solution)/shard_map/ppermute | solution.py:342
  46.5 27.0 %all-to-all-start.1 = ((bf16[32,24,512]{2,1,0:T(8,128)(2,1)}), bf16[32,24,512]{2,1,0:T(8,128)(2,1)}, u32[]{:S(2)}, u32[]{:S(2)}) async-start(bf16[32,24,512]{2,1,0:T(8,128)(2,1)} %bitcast.24), calls=%async_computation.1 | async-start | bytes 1572864 | tf_op jit(solution)/shard_map/all_to_all | solution.py:353
  62.1 19.6 %copy-start = (bf16[768,512]{1,0:T(8,128)(2,1)}, bf16[768,512]{1,0:T(8,128)(2,1)S(1)}, u32[]{:S(2)}) copy-start(bf16[768,512]{1,0:T(8,128)(2,1)S(1)} %collective-permute-done.2.x2.refs_2_) | copy-start | bytes 2359300
  62.9 18.8 %collective-permute-start.4 = (bf16[384,512]{1,0:T(8,128)(2,1)}, bf16[384,512]{1,0:T(8,128)(2,1)}, u32[]{:S(2)}, u32[]{:S(2)}) collective-permute-start(bf16[384,512]{1,0:T(8,128)(2,1)} %slice.25), channel_id=1, source_target_pairs={{0,192},{64,0},{128,64},{192,128},{1,193},{65,1},{129,65},{193,129... | collective-permute-start | bytes 1179656 | tf_op jit(solution)/shard_map/ppermute | solution.py:345
  66.5 15.2 %copy-start.1 = (bf16[768,512]{1,0:T(8,128)(2,1)}, bf16[768,512]{1,0:T(8,128)(2,1)S(1)}, u32[]{:S(2)}) copy-start(bf16[768,512]{1,0:T(8,128)(2,1)S(1)} %collective-permute-done.1.x1.refs_1_) | copy-start | bytes 2359300
  67.3 14.4 %collective-permute-start.3 = (bf16[384,512]{1,0:T(8,128)(2,1)}, bf16[384,512]{1,0:T(8,128)(2,1)}, u32[]{:S(2)}, u32[]{:S(2)}) collective-permute-start(bf16[384,512]{1,0:T(8,128)(2,1)} %slice.24), channel_id=1, source_target_pairs={{0,64},{64,128},{128,192},{192,0},{1,65},{65,129},{129,193},{193,1... | collective-permute-start | bytes 1179656 | tf_op jit(solution)/shard_map/ppermute | solution.py:342
  72.9 8.9 %copy-start.4 = (s32[2]{0:T(128)S(1)}, s32[2]{0:T(128)}, u32[]{:S(2)}) copy-start(s32[2]{0:T(128)} %pad_add_fusion.pos) | copy-start | bytes 28
  75.5 20.6 %collective-permute-start.9 = (bf16[384,512]{1,0:T(8,128)(2,1)}, bf16[384,512]{1,0:T(8,128)(2,1)}, u32[]{:S(2)}, u32[]{:S(2)}) collective-permute-start(bf16[384,512]{1,0:T(8,128)(2,1)} %bitcast.10.refs_0_.refs_5_), channel_id=1, source_target_pairs={{0,192},{64,0},{128,64},{192,128},{1,193},{65,1},{129,65},{193,129... | collective-permute-start | bytes 1179656 | tf_op jit(solution)/shard_map/ppermute | solution.py:345
  78.5 13.1 %collective-permute-start.7 = (bf16[384,512]{1,0:T(8,128)(2,1)}, bf16[384,512]{1,0:T(8,128)(2,1)}, u32[]{:S(2)}, u32[]{:S(2)}) collective-permute-start(bf16[384,512]{1,0:T(8,128)(2,1)} %bitcast.10.refs_0_.refs_5_), channel_id=1, source_target_pairs={{0,64},{64,128},{128,192},{192,0},{1,65},{65,129},{129,193},{193,1... | collective-permute-start | bytes 1179656 | tf_op jit(solution)/shard_map/ppermute | solution.py:342
  78.5 13.9 %collective-permute-start.10 = (bf16[384,512]{1,0:T(8,128)(2,1)}, bf16[384,512]{1,0:T(8,128)(2,1)}, u32[]{:S(2)}, u32[]{:S(2)}) collective-permute-start(bf16[384,512]{1,0:T(8,128)(2,1)} %bitcast.11.refs_1_.refs_6_), channel_id=1, source_target_pairs={{0,192},{64,0},{128,64},{192,128},{1,193},{65,1},{129,65},{193,129... | collective-permute-start | bytes 1179656 | tf_op jit(solution)/shard_map/ppermute | solution.py:345
  81.7 15.2 %collective-permute-start.8 = (bf16[384,512]{1,0:T(8,128)(2,1)}, bf16[384,512]{1,0:T(8,128)(2,1)}, u32[]{:S(2)}, u32[]{:S(2)}) collective-permute-start(bf16[384,512]{1,0:T(8,128)(2,1)} %bitcast.11.refs_1_.refs_6_), channel_id=1, source_target_pairs={{0,64},{64,128},{128,192},{192,0},{1,65},{65,129},{129,193},{193,1... | collective-permute-start | bytes 1179656 | tf_op jit(solution)/shard_map/ppermute | solution.py:342
  81.8 1.9 copy-start.6
  83.7 13.2 %copy-start.8 = (bf16[384,2048]{1,0:T(8,128)(2,1)S(1)}, bf16[384,2048]{1,0:T(8,128)(2,1)}, u32[]{:S(2)}) copy-start(bf16[384,2048]{1,0:T(8,128)(2,1)} %get-tuple-element.49.refs_6_.w) | copy-start | bytes 4718596
  89.8 19.3 %collective-permute-start.6 = (f32[768,768]{1,0:T(8,128)}, f32[768,768]{1,0:T(8,128)}, u32[]{:S(2)}, u32[]{:S(2)}) collective-permute-start(f32[768,768]{1,0:T(8,128)} %gate_up.1.gu_a), channel_id=1, source_target_pairs={{0,1},{1,0},{2,3},{3,2},{4,5},{5,4},{6,7},{7,6},{8,9},{9,8},{10,11... | collective-permute-start | bytes 7077896 | tf_op jit(solution)/shard_map/ppermute | solution.py:348
  91.6 12.6 %collective-permute-start.11 = (bf16[384,512]{1,0:T(8,128)(2,1)}, bf16[384,512]{1,0:T(8,128)(2,1)}, u32[]{:S(2)}, u32[]{:S(2)}) collective-permute-start(bf16[384,512]{1,0:T(8,128)(2,1)} %collective-permute-done.7.refs_2_.refs_7_), channel_id=1, source_target_pairs={{0,64},{64,128},{128,192},{192,0},{1,65},{65,129},{129,193},{193,1... | collective-permute-start | bytes 1179656 | tf_op jit(solution)/shard_map/ppermute | solution.py:342
  92.4 11.8 %collective-permute-start.12 = (bf16[384,512]{1,0:T(8,128)(2,1)}, bf16[384,512]{1,0:T(8,128)(2,1)}, u32[]{:S(2)}, u32[]{:S(2)}) collective-permute-start(bf16[384,512]{1,0:T(8,128)(2,1)} %collective-permute-done.10.refs_5_.refs_10_), channel_id=1, source_target_pairs={{0,192},{64,0},{128,64},{192,128},{1,193},{65,1},{129,65},{193,129... | collective-permute-start | bytes 1179656 | tf_op jit(solution)/shard_map/ppermute | solution.py:345
  104.3 4.8 %copy-start.7 = (bf16[2,384,2048]{2,1,0:T(8,128)(2,1)S(1)}, bf16[2,384,2048]{2,1,0:T(8,128)(2,1)}, u32[]{:S(2)}) copy-start(bf16[2,384,2048]{2,1,0:T(8,128)(2,1)} %get-tuple-element.47.w) | copy-start | bytes 9437188
  106.1 2.9 %collective-permute-start.13 = (f32[768,384]{1,0:T(8,128)S(1)}, f32[768,384]{1,0:T(8,128)S(1)}, u32[]{:S(2)}, u32[]{:S(2)}) collective-permute-start(f32[768,384]{1,0:T(8,128)S(1)} %back.1.bk_a), channel_id=1, source_target_pairs={{0,1},{1,0},{2,3},{3,2},{4,5},{5,4},{6,7},{7,6},{8,9},{9,8},{10,11... | collective-permute-start | bytes 3538952 | tf_op jit(solution)/shard_map/ppermute | solution.py:348
  114.4 5.9 %copy-start.9 = (bf16[768,768]{1,0:T(8,128)(2,1)}, bf16[768,768]{1,0:T(8,128)(2,1)S(1)}, u32[]{:S(2)}) copy-start(bf16[768,768]{1,0:T(8,128)(2,1)S(1)} %get-tuple-element.64.both) | copy-start | bytes 3538948
  114.4 5.9 %copy-start.10 = (bf16[768,384]{1,0:T(8,128)(2,1)}, bf16[768,384]{1,0:T(8,128)(2,1)S(1)}, u32[]{:S(2)}) copy-start(bf16[768,384]{1,0:T(8,128)(2,1)S(1)} %get-tuple-element.65.hd) | copy-start | bytes 1769476
  114.4 13.5 %collective-permute-start.15 = (bf16[384,512]{1,0:T(8,128)(2,1)}, bf16[384,512]{1,0:T(8,128)(2,1)}, u32[]{:S(2)}, u32[]{:S(2)}) collective-permute-start(bf16[384,512]{1,0:T(8,128)(2,1)} %get-tuple-element.54), channel_id=1, source_target_pairs={{0,64},{64,128},{128,192},{192,0},{1,65},{65,129},{129,193},{193,1... | collective-permute-start | bytes 1179656 | tf_op jit(solution)/shard_map/ppermute | solution.py:342
  114.5 13.4 %collective-permute-start.16 = (bf16[384,512]{1,0:T(8,128)(2,1)}, bf16[384,512]{1,0:T(8,128)(2,1)}, u32[]{:S(2)}, u32[]{:S(2)}) collective-permute-start(bf16[384,512]{1,0:T(8,128)(2,1)} %get-tuple-element.56), channel_id=1, source_target_pairs={{0,192},{64,0},{128,64},{192,128},{1,193},{65,1},{129,65},{193,129... | collective-permute-start | bytes 1179656 | tf_op jit(solution)/shard_map/ppermute | solution.py:345
  120.3 23.2 %collective-permute-start.14 = (bf16[384,512]{1,0:T(8,128)(2,1)}, bf16[384,512]{1,0:T(8,128)(2,1)}, u32[]{:S(2)}, u32[]{:S(2)}) collective-permute-start(bf16[384,512]{1,0:T(8,128)(2,1)} %get-tuple-element.52), channel_id=1, source_target_pairs={{0,192},{64,0},{128,64},{192,128},{1,193},{65,1},{129,65},{193,129... | collective-permute-start | bytes 1179656 | tf_op jit(solution)/shard_map/ppermute | solution.py:345
  121.1 15.3 %collective-permute-start.19 = (bf16[384,512]{1,0:T(8,128)(2,1)}, bf16[384,512]{1,0:T(8,128)(2,1)}, u32[]{:S(2)}, u32[]{:S(2)}) collective-permute-start(bf16[384,512]{1,0:T(8,128)(2,1)} %get-tuple-element.59), channel_id=1, source_target_pairs={{0,64},{64,128},{128,192},{192,0},{1,65},{65,129},{129,193},{193,1... | collective-permute-start | bytes 1179656 | tf_op jit(solution)/shard_map/ppermute | solution.py:342
  129.2 14.6 %collective-permute-start.17 = (bf16[384,512]{1,0:T(8,128)(2,1)S(1)}, bf16[384,512]{1,0:T(8,128)(2,1)S(1)}, u32[]{:S(2)}, u32[]{:S(2)}) collective-permute-start(bf16[384,512]{1,0:T(8,128)(2,1)S(1)} %get-tuple-element.57), channel_id=1, source_target_pairs={{0,64},{64,128},{128,192},{192,0},{1,65},{65,129},{129,193},{193,1... | collective-permute-start | bytes 1179656 | tf_op jit(solution)/shard_map/ppermute | solution.py:342
  129.9 14.0 %collective-permute-start.18 = (bf16[384,512]{1,0:T(8,128)(2,1)S(1)}, bf16[384,512]{1,0:T(8,128)(2,1)S(1)}, u32[]{:S(2)}, u32[]{:S(2)}) collective-permute-start(bf16[384,512]{1,0:T(8,128)(2,1)S(1)} %get-tuple-element.58), channel_id=1, source_target_pairs={{0,192},{64,0},{128,64},{192,128},{1,193},{65,1},{129,65},{193,129... | collective-permute-start | bytes 1179656 | tf_op jit(solution)/shard_map/ppermute | solution.py:345
  136.4 16.4 %all-to-all-start.2 = ((bf16[32,24,128]{2,1,0:T(8,128)(2,1)}), bf16[32,24,128]{2,1,0:T(8,128)(2,1)}, u32[]{:S(2)}, u32[]{:S(2)}) async-start(bf16[32,24,128]{2,1,0:T(8,128)(2,1)} %bitcast.12), calls=%async_computation.2 | async-start | bytes 393216 | tf_op jit(solution)/shard_map/all_to_all | solution.py:353
  152.7 26.4 %all-to-all-start.3 = ((bf16[32,24,512]{2,1,0:T(8,128)(2,1)}), bf16[32,24,512]{2,1,0:T(8,128)(2,1)}, u32[]{:S(2)}, u32[]{:S(2)}) async-start(bf16[32,24,512]{2,1,0:T(8,128)(2,1)} %bitcast.14), calls=%async_computation.3 | async-start | bytes 1572864 | tf_op jit(solution)/shard_map/all_to_all | solution.py:353
  179.2 4.7 %copy-start.11 = (bf16[3,192,2048]{2,1,0:T(8,128)(2,1)S(1)}, bf16[3,192,2048]{2,1,0:T(8,128)(2,1)}, u32[]{:S(2)}) copy-start(bf16[3,192,2048]{2,1,0:T(8,128)(2,1)} %get-tuple-element.74) | copy-start | bytes 7077892
  182.2 1.7 collective-permute-start.20
  183.9 11.6 %collective-permute-start.21 = (bf16[3,192,2048]{2,1,0:T(8,128)(2,1)S(1)}, bf16[3,192,2048]{2,1,0:T(8,128)(2,1)}, u32[]{:S(2)}, u32[]{:S(2)}) collective-permute-start(bf16[3,192,2048]{2,1,0:T(8,128)(2,1)S(1)} %copy-done.11), channel_id=1, source_target_pairs={{0,1},{1,0},{2,3},{3,2},{4,5},{5,4},{6,7},{7,6},{8,9},{9,8},{10,11... | collective-permute-start | bytes 7077896 | tf_op jit(solution)/shard_map/ppermute | solution.py:348
  184.0 8.0 %collective-permute-start.22 = (bf16[144,512]{1,0:T(8,128)(2,1)}, bf16[144,512]{1,0:T(8,128)(2,1)}, u32[]{:S(2)}, u32[]{:S(2)}) collective-permute-start(bf16[144,512]{1,0:T(8,128)(2,1)} %get-tuple-element.77.refs_0_), channel_id=1, source_target_pairs={{0,64},{64,128},{128,192},{192,0},{1,65},{65,129},{129,193},{193,1... | collective-permute-start | bytes 442376 | tf_op jit(solution)/shard_map/ppermute | solution.py:342
  184.0 8.0 %collective-permute-start.25 = (bf16[144,512]{1,0:T(8,128)(2,1)}, bf16[144,512]{1,0:T(8,128)(2,1)}, u32[]{:S(2)}, u32[]{:S(2)}) collective-permute-start(bf16[144,512]{1,0:T(8,128)(2,1)} %collective-permute-done.20.refs_1_), channel_id=1, source_target_pairs={{0,192},{64,0},{128,64},{192,128},{1,193},{65,1},{129,65},{193,129... | collective-permute-start | bytes 442376 | tf_op jit(solution)/shard_map/ppermute | solution.py:345
  187.3 13.1 %collective-permute-start.24 = (bf16[144,512]{1,0:T(8,128)(2,1)}, bf16[144,512]{1,0:T(8,128)(2,1)}, u32[]{:S(2)}, u32[]{:S(2)}) collective-permute-start(bf16[144,512]{1,0:T(8,128)(2,1)} %get-tuple-element.77.refs_0_), channel_id=1, source_target_pairs={{0,192},{64,0},{128,64},{192,128},{1,193},{65,1},{129,65},{193,129... | collective-permute-start | bytes 442376 | tf_op jit(solution)/shard_map/ppermute | solution.py:345
  187.3 13.0 %collective-permute-start.23 = (bf16[144,512]{1,0:T(8,128)(2,1)}, bf16[144,512]{1,0:T(8,128)(2,1)}, u32[]{:S(2)}, u32[]{:S(2)}) collective-permute-start(bf16[144,512]{1,0:T(8,128)(2,1)} %collective-permute-done.20.refs_1_), channel_id=1, source_target_pairs={{0,64},{64,128},{128,192},{192,0},{1,65},{65,129},{129,193},{193,1... | collective-permute-start | bytes 442376 | tf_op jit(solution)/shard_map/ppermute | solution.py:342
  192.0 8.3 %collective-permute-start.26 = (bf16[144,512]{1,0:T(8,128)(2,1)}, bf16[144,512]{1,0:T(8,128)(2,1)}, u32[]{:S(2)}, u32[]{:S(2)}) collective-permute-start(bf16[144,512]{1,0:T(8,128)(2,1)} %collective-permute-done.22.refs_2_), channel_id=1, source_target_pairs={{0,64},{64,128},{128,192},{192,0},{1,65},{65,129},{129,193},{193,1... | collective-permute-start | bytes 442376 | tf_op jit(solution)/shard_map/ppermute | solution.py:342
  192.0 8.3 %collective-permute-start.27 = (bf16[144,512]{1,0:T(8,128)(2,1)}, bf16[144,512]{1,0:T(8,128)(2,1)}, u32[]{:S(2)}, u32[]{:S(2)}) collective-permute-start(bf16[144,512]{1,0:T(8,128)(2,1)} %collective-permute-done.25.refs_5_), channel_id=1, source_target_pairs={{0,192},{64,0},{128,64},{192,128},{1,193},{65,1},{129,65},{193,129... | collective-permute-start | bytes 442376 | tf_op jit(solution)/shard_map/ppermute | solution.py:345
  195.5 4.9 %copy-start.2 = (bf16[144,512]{1,0:T(8,128)(2,1)S(1)}, bf16[144,512]{1,0:T(8,128)(2,1)}, u32[]{:S(2)}) copy-start(bf16[144,512]{1,0:T(8,128)(2,1)} %get-tuple-element.77.refs_0_) | copy-start | bytes 442372
  195.5 4.9 %copy-start.3 = (bf16[128,8]{0,1:T(8,128)(2,1)S(1)}, bf16[128,8]{0,1:T(8,128)(2,1)}, u32[]{:S(2)}) copy-start(bf16[128,8]{0,1:T(8,128)(2,1)} %param.10) | copy-start | bytes 6148
  195.5 4.9 %copy-start.5 = (s32[2]{0:T(128)S(1)}, s32[2]{0:T(128)}, u32[]{:S(2)}) copy-start(s32[2]{0:T(128)} %pad_add_fusion.pos) | copy-start | bytes 28
